TPU v7x, 32 devices: a whole 2x2x4 slice. The times are simulated.
32 devices in a mesh: grp: 2 (over x), seq: 16 (over z, y, core).
Axes of the slice: x: 2, y: 2, z: 4, core: 2. Of those that a mesh axis runs over, the one named last changes fastest.
Arguments:
- projected: bfloat16 [3, 4096, 4096], P(None, ('grp', 'seq')), parts along dimension 1, may hold values from -6 to 6
- short_taps: float32 [3, 3, 4096], replicated, may hold values from -3 to 3
- skip_gain: float32 [4096], replicated, may hold values from -3 to 3
- residues: float32 [2, 2, 4096], replicated, may hold values from -0.125 to 0.125
- pole_angles: float32 [2, 4096], replicated, may hold values from -3.140625 to 3.140625
- decay_rates: float32 [2, 4096], replicated, may hold values from 3.0517578e-05 to 0.03125
Outputs:
- gated: bfloat16 [4096, 4096], P(('grp', 'seq')), parts along dimension 0
There are 2 independent parts, one for each index of `grp`. A program takes and returns all parts, laid end to end along the dimension named above; an argument that names none is the same for every part. Nothing has to cross between parts.
All inputs are finite; a program needn't handle non-finite values.
Results may differ from a plain program's by a relative error of at most 0.008.
Values may be sent and summed in bfloat16 or wider, within the bound.
No kernel may reach another device: no remote copies, remote signals or barrier semaphores. Data moves between devices by JAX's collectives and lax.ppermute only.
A program may use at most 128 MiB of HBM per device.

v0:
```python
import jax
import jax.numpy as jnp
from jax import lax
from jax.experimental import pallas as pl
from jax.experimental.pallas import tpu as pltpu
from jax.sharding import PartitionSpec as P

SEGMENTS = 8
WIDTH = 256
CHUNK = 1024
POLES = 2
WIRE = jnp.float32
f32 = jnp.float32
bf16 = jnp.bfloat16

LAM, BACK, SEGMENT, SPAN = 0, 1, 2, 5


def order_matrix(row_count, inverse):
    length = row_count // SEGMENTS
    ordered = lax.broadcasted_iota(jnp.int32, (row_count, row_count), 1 if inverse else 0)
    natural = lax.broadcasted_iota(jnp.int32, (row_count, row_count), 0 if inverse else 1)
    wanted = length * (ordered % SEGMENTS) + ordered // SEGMENTS
    return (wanted == natural).astype(f32).astype(bf16)


def wide(value):
    return jnp.broadcast_to(value, (SEGMENTS, value.shape[1]))


def times(a, b):
    return (a[0] * b[0] - a[1] * b[1], a[0] * b[1] + a[1] * b[0])


def plus(a, b):
    return (a[0] + b[0], a[1] + b[1])


def pair_at(ref, index, cols):
    return (ref[4 * index : 4 * index + 2, cols], ref[4 * index + 2 : 4 * index + 4, cols])


def put_pair(ref, index, cols, value):
    ref[4 * index : 4 * index + 2, cols] = value[0]
    ref[4 * index + 2 : 4 * index + 4, cols] = value[1]


def pole_at(ref, index, pole, cols):
    return (wide(ref[pl.ds(4 * index + pole, 1), cols]), wide(ref[pl.ds(4 * index + 2 + pole, 1), cols]))


def half_angle(angle):
    x = 0.5 * angle
    u = x * x
    sine = 1.0 / 6227020800.0
    for term in (-1.0 / 39916800.0, 1.0 / 362880.0, -1.0 / 5040.0, 1.0 / 120.0, -1.0 / 6.0, 1.0):
        sine = sine * u + term
    cosine = -1.0 / 87178291200.0
    for term in (1.0 / 479001600.0, -1.0 / 3628800.0, 1.0 / 40320.0, -1.0 / 720.0, 1.0 / 24.0, -0.5, 1.0):
        cosine = cosine * u + term
    return cosine, sine * x


def fill_powers(power_ref, angle_ref, decay_ref, length, levels):
    cols = slice(None)
    cosine, sine = half_angle(angle_ref[...])
    turn = (1.0 - 2.0 * sine * sine, 2.0 * sine * cosine)
    decay = decay_ref[...]
    damping = jnp.exp(-decay)
    growth = jnp.exp(decay)
    value = (damping * turn[0], damping * turn[1])
    put_pair(power_ref, LAM, cols, value)
    put_pair(power_ref, BACK, cols, (growth * turn[0], -growth * turn[1]))
    for _ in range(length.bit_length() - 1):
        value = times(value, value)
    for level in range(3 + levels):
        put_pair(power_ref, SEGMENT + level, cols, value)
        value = times(value, value)


def steps_of(ref, cols):
    return [ref[SEGMENTS * j : SEGMENTS * (j + 1), cols] for j in range(ref.shape[0] // SEGMENTS)]


def first_mask():
    return lax.broadcasted_iota(jnp.int32, (SEGMENTS, WIDTH), 0) == 0


def delayed(value):
    return jnp.where(first_mask(), 0.0, pltpu.roll(value, 1, 0))


def short_filter(steps, taps_ref, which, cols):
    taps = [wide(taps_ref[tap, which : which + 1, cols]) for tap in range(3)]
    padded = [delayed(steps[-2]), delayed(steps[-1])] + steps
    return [
        taps[0] * padded[j] + taps[1] * padded[j + 1] + taps[2] * padded[j + 2]
        for j in range(len(steps))
    ]


def feedback(lam):
    return 2.0 * lam[0], lam[0] * lam[0] + lam[1] * lam[1]


def span(start, size):
    return pl.ds(pl.multiple_of(start, 128), size)


def loop_columns(chunk_index, chunk, body):
    for part in range(chunk // WIDTH):
        body(part * WIDTH, chunk_index * chunk + part * WIDTH)


def states_kernel(order_ref, angle_ref, decay_ref, taps_ref, proj_ref,
                  prod_ref, scan_ref, total_ref, edge_ref, power_ref,
                  k_ref, v_ref, out_ref, ks_ref, vs_ref, in_sem, out_sem, *, levels):
    rows, channels = k_ref.shape
    chunk = ks_ref.shape[1]
    count = channels // chunk

    def fetch(i, which, ref):
        cols = span(i * chunk, chunk)
        return pltpu.make_async_copy(proj_ref.at[which, :, cols], ref.at[:, cols], in_sem.at[which - 1, i])

    def send(i):
        cols = span(i * chunk, chunk)
        return pltpu.make_async_copy(out_ref.at[:, cols], prod_ref.at[:, cols], out_sem.at[i])

    for i in range(count):
        fetch(i, 1, k_ref).start()
        fetch(i, 2, v_ref).start()
    fill_powers(power_ref, angle_ref, decay_ref, rows // SEGMENTS, levels)

    def body(i, _):
        fetch(i, 1, k_ref).wait()
        fetch(i, 2, v_ref).wait()
        at = span(i * chunk, chunk)
        ks_ref[...] = jnp.dot(order_ref[...], k_ref[:, at], preferred_element_type=f32)
        vs_ref[...] = jnp.dot(order_ref[...], v_ref[:, at], preferred_element_type=f32)
        for step in range(2):
            edge_ref[step : step + 1, at] = ks_ref[SEGMENTS * step : SEGMENTS * step + 1, :]
            edge_ref[2 + step : 3 + step, at] = vs_ref[SEGMENTS * step : SEGMENTS * step + 1, :]

        def column(inner, outer):
            cols = slice(inner, inner + WIDTH)
            here = span(outer, WIDTH)
            keys = short_filter(steps_of(ks_ref, cols), taps_ref, 1, here)
            values = short_filter(steps_of(vs_ref, cols), taps_ref, 2, here)
            products = [a * b for a, b in zip(keys, values)]
            for j in range(2):
                products[j] = jnp.where(first_mask(), 0.0, products[j])
            for j in range(0, len(products), 2):
                both = jnp.concatenate(products[j : j + 2], axis=0)
                out_ref[SEGMENTS * j : SEGMENTS * (j + 2), here] = both.astype(bf16)
            sublane = lax.broadcasted_iota(jnp.int32, (SEGMENTS, WIDTH), 0)
            for pole in range(POLES):
                lam = pole_at(power_ref, LAM, pole, here)
                a1, a2 = feedback(lam)
                late = products[0]
                now = a1 * late + products[1]
                for value in products[2:]:
                    late, now = now, a1 * now - a2 * late + value
                state = (now - lam[0] * late, lam[1] * late)
                for level in range(3):
                    by = 1 << level
                    factor = pole_at(power_ref, SEGMENT + level, pole, here)
                    moved = tuple(jnp.where(sublane >= by, pltpu.roll(part, by, 0), 0.0) for part in state)
                    state = plus(state, times(factor, moved))
                for part in range(2):
                    scan_ref[2 * part + pole, :, here] = state[part]
                    total_ref[2 * part + pole : 2 * part + pole + 1, here] = state[part][SEGMENTS - 1 :]

        loop_columns(i, chunk, column)
        send(i).start()
        return 0

    lax.fori_loop(0, count, body, 0)
    for i in range(count):
        send(i).wait()


def first_products(rim_ref, edge_ref, taps_ref, cols):
    before = rim_ref[:, :, cols].astype(f32)

    def filtered(which, edge, at):
        sequence = [before[which, 0:1], before[which, 1:2], edge_ref[edge : edge + 1, cols], edge_ref[edge + 1 : edge + 2, cols]]
        return sum(taps_ref[tap, which : which + 1, cols] * sequence[at + tap] for tap in range(3))

    return [filtered(1, 0, at) * filtered(2, 2, at) for at in range(2)]


def rims_kernel(rim_ref, edge_ref, taps_ref, power_ref, total_ref, ending_ref, extra_ref):
    cols = slice(None)
    first, second = first_products(rim_ref, edge_ref, taps_ref, cols)
    back = pair_at(power_ref, BACK, cols)
    inner = times(back, (second * back[0] + first, second * back[1]))
    put_pair(extra_ref, 0, cols, inner)
    grown = times(pair_at(power_ref, SPAN, cols), inner)
    put_pair(ending_ref, 0, cols, plus(grown, pair_at(total_ref, 0, cols)))


def join_kernel(ending_ref, got_ref, power_ref, joined_ref, *, level):
    upper = (lax.axis_index("seq") >> level) % 2 == 1
    cols = slice(None)
    mine = pair_at(ending_ref, 0, cols)
    other = tuple(part.astype(f32) for part in pair_at(got_ref, 0, cols))
    factor = pair_at(power_ref, SPAN + level, cols)
    early = tuple(jnp.where(upper, o, m) for o, m in zip(other, mine))
    late = tuple(jnp.where(upper, m, o) for o, m in zip(other, mine))
    put_pair(joined_ref, 0, cols, plus(times(factor, early), late))


def local_kernel(order_ref, taps_ref, gain_ref, skip_ref, power_ref, scan_ref, proj_ref, prod_ref,
                 query_ref, local_ref, enter_ref, lead_ref,
                 q_ref, p_ref, query_out, local_out, qs_ref, in_sem, out_sem, *, levels):
    rows, channels = q_ref.shape
    chunk = qs_ref.shape[1]
    count = channels // chunk

    def copies(i):
        cols = span(i * chunk, chunk)
        return (
            pltpu.make_async_copy(proj_ref.at[0, :, cols], q_ref.at[:, cols], in_sem.at[0, i]),
            pltpu.make_async_copy(prod_ref.at[:, cols], p_ref.at[:, cols], in_sem.at[1, i]),
        )

    def sends(i):
        cols = span(i * chunk, chunk)
        return (
            pltpu.make_async_copy(query_out.at[:, cols], query_ref.at[:, cols], out_sem.at[0, i]),
            pltpu.make_async_copy(local_out.at[:, cols], local_ref.at[:, cols], out_sem.at[1, i]),
        )

    for i in range(count):
        for copy in copies(i):
            copy.start()
    device = lax.axis_index("seq")
    lead = (jnp.ones((POLES, channels), f32), jnp.zeros((POLES, channels), f32))
    for level in range(levels):
        upper = (device >> level) % 2 == 1
        put_pair(lead_ref, level, slice(None), tuple(jnp.where(upper, part, 0.0) for part in lead))
        grown = times(lead, pair_at(power_ref, SPAN + level, slice(None)))
        lead = tuple(jnp.where(upper, g, part) for g, part in zip(grown, lead))

    def body(i, _):
        for copy in copies(i):
            copy.wait()
        at = span(i * chunk, chunk)
        qs_ref[...] = jnp.dot(order_ref[...], q_ref[:, at], preferred_element_type=f32)

        def column(inner, outer):
            cols = slice(inner, inner + WIDTH)
            here = span(outer, WIDTH)
            queries = short_filter(steps_of(qs_ref, cols), taps_ref, 0, here)
            for j, value in enumerate(queries):
                query_out[SEGMENTS * j : SEGMENTS * (j + 1), here] = value
            products = []
            for j in range(0, len(queries), 2):
                both = p_ref[SEGMENTS * j : SEGMENTS * (j + 2), here].astype(f32)
                products += [both[:SEGMENTS], both[SEGMENTS:]]
            before = delayed(products[-1])
            skip = wide(skip_ref[0:1, here])
            sublane = lax.broadcasted_iota(jnp.int32, (SEGMENTS, WIDTH), 0)
            coefs = []
            for pole in range(POLES):
                lam = pole_at(power_ref, LAM, pole, here)
                back = pole_at(power_ref, BACK, pole, here)
                gain = tuple(wide(gain_ref[part, pole : pole + 1, here]) for part in range(2))
                a1, a2 = feedback(lam)
                b1 = gain[0] * lam[0] + gain[1] * lam[1]
                carry = tuple(delayed(scan_ref[2 * part + pole, :, here]) for part in range(2))
                gain_back = times(gain, back)
                y1 = gain[0] * carry[0] - gain[1] * carry[1]
                y2 = gain_back[0] * (carry[0] - before) - gain_back[1] * carry[1]
                coefs.append([a1, a2, gain[0], b1, y1, y2])
                reach = gain
                for level in range(3):
                    factor = pole_at(power_ref, SEGMENT + level, pole, here)
                    bit = (sublane // (1 << level)) % 2 == 1
                    reach = times(reach, (jnp.where(bit, factor[0], 1.0), jnp.where(bit, factor[1], 0.0)))
                for part in range(2):
                    enter_ref[2 * part + pole, :, here] = reach[part]
            previous = before
            for j, value in enumerate(products):
                total = skip * value
                for pole in range(POLES):
                    a1, a2, b0, b1, y1, y2 = coefs[pole]
                    y = a1 * y1 - a2 * y2 + (b0 * value - b1 * previous)
                    coefs[pole][4:] = [y, y1]
                    total = total + y
                previous = value
                local_out[SEGMENTS * j : SEGMENTS * (j + 1), here] = total

        loop_columns(i, chunk, column)
        for copy in sends(i):
            copy.start()
        return 0

    lax.fori_loop(0, count, body, 0)
    for i in range(count):
        for copy in sends(i):
            copy.wait()


def gate_kernel(order_ref, taps_ref, gain_ref, skip_ref, power_ref, enter_ref, lead_ref, extra_ref,
                rim_ref, edge_ref, *rest, levels):
    got_refs = rest[:levels]
    query_hbm, local_hbm, out_hbm = rest[levels : levels + 3]
    q_ref, l_ref, out_ref, gated_ref, state_ref, fix_ref, in_sem, out_sem = rest[levels + 3 :]
    rows, channels = q_ref.shape
    chunk = gated_ref.shape[1]
    count = channels // chunk

    def copies(i):
        cols = span(i * chunk, chunk)
        return (
            pltpu.make_async_copy(query_hbm.at[:, cols], q_ref.at[:, cols], in_sem.at[0, i]),
            pltpu.make_async_copy(local_hbm.at[:, cols], l_ref.at[:, cols], in_sem.at[1, i]),
        )

    def send(i):
        cols = span(i * chunk, chunk)
        return pltpu.make_async_copy(out_ref.at[:, cols], out_hbm.at[:, cols], out_sem.at[i])

    for i in range(count):
        for copy in copies(i):
            copy.start()
    cols = slice(None)
    state = pair_at(extra_ref, 0, cols)
    for level in range(levels):
        got = tuple(part.astype(f32) for part in pair_at(got_refs[level], 0, cols))
        state = plus(state, times(pair_at(lead_ref, level, cols), got))
    put_pair(state_ref, 0, cols, state)
    first, second = first_products(rim_ref, edge_ref, taps_ref, cols)
    skip = skip_ref[...]
    back = pair_at(power_ref, BACK, cols)
    jump = sum(gain_ref[0, pole : pole + 1] * back[0][pole : pole + 1] - gain_ref[1, pole : pole + 1] * back[1][pole : pole + 1]
               for pole in range(POLES))
    fix_ref[0:1] = skip * first - jump * second
    fix_ref[1:2] = skip * second
    before = rim_ref[0].astype(f32)
    fix_ref[2:3] = taps_ref[0, 0:1] * before[0:1] + taps_ref[1, 0:1] * before[1:2]
    fix_ref[3:4] = taps_ref[0, 0:1] * before[1:2]

    def body(i, _):
        for copy in copies(i):
            copy.wait()

        def column(inner, outer):
            cols = slice(inner, inner + WIDTH)
            here = span(outer, WIDTH)
            queries = steps_of(q_ref, here)
            local = steps_of(l_ref, here)
            for j in range(2):
                local[j] = local[j] + jnp.where(first_mask(), fix_ref[j : j + 1, here], 0.0)
                queries[j] = queries[j] + jnp.where(first_mask(), fix_ref[2 + j : 3 + j, here], 0.0)
            coefs = []
            for pole in range(POLES):
                lam = pole_at(power_ref, LAM, pole, here)
                back = pole_at(power_ref, BACK, pole, here)
                state = times(pole_at(state_ref, 0, pole, here), (enter_ref[pole, :, here], enter_ref[2 + pole, :, here]))
                y2 = state[0] * back[0] - state[1] * back[1]
                coefs.append([*feedback(lam), state[0], y2])
            gated = []
            for j in range(len(queries)):
                total = local[j]
                for pole in range(POLES):
                    a1, a2, y1, y2 = coefs[pole]
                    y = a1 * y1 - a2 * y2
                    coefs[pole][2:] = [y, y1]
                    total = total + y
                gated.append(queries[j] * total)
                if j % 2:
                    both = jnp.concatenate(gated[-2:], axis=0)
                    gated_ref[SEGMENTS * (j - 1) : SEGMENTS * (j + 1), cols] = both.astype(bf16)

        loop_columns(i, chunk, column)
        out_ref[:, span(i * chunk, chunk)] = jnp.dot(
            order_ref[...], gated_ref[...], preferred_element_type=f32).astype(bf16)
        send(i).start()
        return 0

    lax.fori_loop(0, count, body, 0)
    for i in range(count):
        send(i).wait()


def kernel_call(body, name, outs, scratch, operands, in_hbm, out_hbm, **options):
    def spec(far):
        return pl.BlockSpec(memory_space=pltpu.HBM if far else pltpu.VMEM)

    def bound(*refs):
        return body(*refs, **options)

    return pl.pallas_call(
        bound,
        in_specs=[spec(far) for far in in_hbm],
        out_specs=[spec(far) for far in out_hbm],
        out_shape=[jax.ShapeDtypeStruct(shape, dtype) for shape, dtype in outs],
        scratch_shapes=scratch,
        compiler_params=pltpu.CompilerParams(vmem_limit_bytes=32 << 20),
        name=name,
    )(*operands)


def on_device(projected, short_taps, skip_gain, residues, pole_angles, decay_rates):
    _, rows, channels = projected.shape
    chunk = min(CHUNK, channels)
    count = channels // chunk
    devices = lax.axis_size("seq")
    levels = devices.bit_length() - 1
    skip_row = skip_gain[None]
    state_shape = ((4, channels), f32)
    plane = (rows, channels)

    rims = lax.ppermute(projected[:, rows - 2 :, :], "seq", [(i, i + 1) for i in range(devices - 1)])

    order = jnp.asarray(order_matrix(rows, False))
    restore = jnp.asarray(order_matrix(rows, True))
    dma = pltpu.SemaphoreType.DMA

    products, scan, total, edges, powers = kernel_call(
        states_kernel, "states",
        [(plane, bf16), ((4, SEGMENTS, channels), f32), state_shape, ((4, channels), f32),
         ((4 * (SPAN + levels), channels), f32)],
        [pltpu.VMEM(plane, bf16)] * 3 + [pltpu.VMEM((rows, chunk), f32)] * 2 + [dma((2, count)), dma((count,))],
        [order, pole_angles, decay_rates, short_taps, projected],
        [False] * 4 + [True], [True] + [False] * 4, levels=levels)

    ending, extra = kernel_call(
        rims_kernel, "rims", [state_shape, state_shape], [],
        [rims, edges, short_taps, powers, total], [False] * 5, [False] * 2)

    query, local, enter, leads = kernel_call(
        local_kernel, "local",
        [(plane, f32), (plane, f32), ((4, SEGMENTS, channels), f32), ((4 * levels, channels), f32)],
        [pltpu.VMEM(plane, bf16)] * 2 + [pltpu.VMEM(plane, f32)] * 2 + [pltpu.VMEM((rows, chunk), f32)]
        + [dma((2, count)), dma((2, count))],
        [order, short_taps, residues, skip_row, powers, scan, projected, products],
        [False] * 6 + [True] * 2, [True] * 2 + [False] * 2, levels=levels)

    received = []
    for level in range(levels):
        sent = ending.astype(WIRE)
        received.append(lax.ppermute(sent, "seq", [(i, i ^ (1 << level)) for i in range(devices)]))
        if level + 1 < levels:
            (ending,) = kernel_call(
                join_kernel, "join", [state_shape], [], [ending, received[-1], powers], [False] * 3, [False],
                level=level)

    (out,) = kernel_call(
        gate_kernel, "gate", [(plane, bf16)],
        [pltpu.VMEM(plane, f32)] * 2 + [pltpu.VMEM(plane, bf16), pltpu.VMEM((rows, chunk), bf16),
         pltpu.VMEM((4, channels), f32), pltpu.VMEM((4, channels), f32), dma((2, count)), dma((count,))],
        [restore, short_taps, residues, skip_row, powers, enter, leads, extra, rims, edges, *received, query, local],
        [False] * (10 + levels) + [True] * 2, [True], levels=levels)
    return out


def solution(mesh):
    return jax.shard_map(
        on_device,
        mesh=mesh,
        in_specs=(P(None, ("grp", "seq"), None), P(), P(), P(), P(), P()),
        out_specs=P(("grp", "seq"), None),
        check_vma=False,
    )
```

profile of v0, /device:TPU:0, one launch (start us, length us, event | category | flops | bytes accessed | tf_op | source)
XLA Modules:
  0.0 33.2 jit_solution(14522728832577899833)
XLA Ops:
  0.0 1.0 %slice.3 = bf16[3,2,4096]{2,1,0:T(2,128)(2,1)S(1)} slice(bf16[3,128,4096]{2,1,0:T(8,128)(2,1)} %refs_6_.1), slice={[0:3], [126:128], [0:4096]} | slice | bytes 98304 | tf_op jit(solution)/shard_map/slice | solution.py:417
  1.0 2.4 %collective-permute-start = (bf16[3,2,4096]{2,1,0:T(2,128)(2,1)S(1)}, bf16[3,2,4096]{2,1,0:T(2,128)(2,1)S(1)}, u32[]{:S(2)}, u32[]{:S(2)}) collective-permute-start(bf16[3,2,4096]{2,1,0:T(2,128)(2,1)S(1)} %slice.3), channel_id=1, source_target_pairs={{0,1},{1,2},{2,3},{3,4},{4,5},{5,6},{6,7},{7,8},{8,9},{9,10},{10,1... | collective-permute-start | bytes 147464 | tf_op jit(solution)/shard_map/ppermute | solution.py:417
  3.4 0.2 convert_convert_fusion
  3.6 0.0 copy-start
  3.6 1.9 %copy-done = bf16[3,128,4096]{2,1,0:T(8,128)(2,1)S(1)} copy-done((bf16[3,128,4096]{2,1,0:T(8,128)(2,1)S(1)}, bf16[3,128,4096]{2,1,0:T(8,128)(2,1)}, u32[]{:S(2)}) %copy-start) | copy-done | bytes 3145752
  5.5 0.9 %copy-done.2 = f32[3,3,4096]{2,1,0:T(4,128)S(1)} copy-done((f32[3,3,4096]{2,1,0:T(4,128)S(1)}, f32[3,3,4096]{2,1,0:T(4,128)}, u32[]{:S(2)}) %copy-start.2) | copy-done | bytes 147480
  6.4 0.8 %copy-done.6 = f32[2,4096]{1,0:T(2,128)S(1)} copy-done((f32[2,4096]{1,0:T(2,128)S(1)}, f32[2,4096]{1,0:T(2,128)}, u32[]{:S(2)}) %copy-start.6) | copy-done | bytes 32792
  7.2 0.8 %copy-done.7 = f32[2,4096]{1,0:T(2,128)S(1)} copy-done((f32[2,4096]{1,0:T(2,128)S(1)}, f32[2,4096]{1,0:T(2,128)}, u32[]{:S(2)}) %copy-start.7) | copy-done | bytes 32792
  7.9 3.2 %states.1 = (bf16[128,4096]{1,0:T(8,128)(2,1)S(1)}, f32[4,8,4096]{2,1,0:T(8,128)S(1)}, f32[4,4096]{1,0:T(4,128)S(1)}, f32[4,4096]{1,0:T(4,128)S(1)}, f32[36,4096]{1,0:T(8,128)S(1)}) custom-call(bf16[128,128]{1,0:T(8,128)(2,1)S(1)} %get-tuple-element.27.refs_0_, f32[2,4096]{1,0:T(2,128)S(1)} %copy-done.6, f32[2,4096]{1,0:T(2,128)S(1)} %copy-done.7, ...), custom_call_target="tpu_custom_call" | custom-call | tf_op jit(solution)/shard_map/states/pallas_call | solution.py:396
  11.1 0.0 copy-start.1
  11.2 0.0 copy-start.5
  11.2 0.2 rims.1
  11.4 2.7 %collective-permute-start.1 = (f32[4,4096]{1,0:T(4,128)S(1)}, f32[4,4096]{1,0:T(4,128)S(1)}, u32[]{:S(2)}, u32[]{:S(2)}) collective-permute-start(f32[4,4096]{1,0:T(4,128)S(1)} %get-tuple-element.24.refs_0_), channel_id=1, source_target_pairs={{0,1},{1,0},{2,3},{3,2},{4,5},{5,4},{6,7},{7,6},{8,9},{9,8},{10,11... | collective-permute-start | bytes 196616 | tf_op jit(solution)/shard_map/ppermute | solution.py:446
  14.0 0.9 %collective-permute-done.1.refs_1_.refs_10_ = f32[4,4096]{1,0:T(4,128)S(1)} collective-permute-done((f32[4,4096]{1,0:T(4,128)S(1)}, f32[4,4096]{1,0:T(4,128)S(1)}, u32[]{:S(2)}, u32[]{:S(2)}) %collective-permute-start.1) | collective-permute-done | bytes 65568 | tf_op jit(solution)/shard_map/ppermute | solution.py:446
  15.0 0.1 join.3.refs_0_
  15.1 1.6 %collective-permute-start.2 = (f32[4,4096]{1,0:T(4,128)S(1)}, f32[4,4096]{1,0:T(4,128)S(1)}, u32[]{:S(2)}, u32[]{:S(2)}) collective-permute-start(f32[4,4096]{1,0:T(4,128)S(1)} %join.3.refs_0_), channel_id=1, source_target_pairs={{0,2},{1,3},{2,0},{3,1},{4,6},{5,7},{6,4},{7,5},{8,10},{9,11},{10,... | collective-permute-start | bytes 196616 | tf_op jit(solution)/shard_map/ppermute | solution.py:446
  16.6 2.8 %collective-permute-done.2.refs_1_.refs_11_ = f32[4,4096]{1,0:T(4,128)S(1)} collective-permute-done((f32[4,4096]{1,0:T(4,128)S(1)}, f32[4,4096]{1,0:T(4,128)S(1)}, u32[]{:S(2)}, u32[]{:S(2)}) %collective-permute-start.2) | collective-permute-done | bytes 65568 | tf_op jit(solution)/shard_map/ppermute | solution.py:446
  19.5 0.1 join.4.refs_0_
  19.6 1.7 %collective-permute-start.3 = (f32[4,4096]{1,0:T(4,128)S(1)}, f32[4,4096]{1,0:T(4,128)S(1)}, u32[]{:S(2)}, u32[]{:S(2)}) collective-permute-start(f32[4,4096]{1,0:T(4,128)S(1)} %join.4.refs_0_), channel_id=1, source_target_pairs={{0,4},{1,5},{2,6},{3,7},{4,0},{5,1},{6,2},{7,3},{8,12},{9,13},{10,... | collective-permute-start | bytes 196616 | tf_op jit(solution)/shard_map/ppermute | solution.py:446
  21.2 2.7 %collective-permute-done.3.refs_1_.refs_12_ = f32[4,4096]{1,0:T(4,128)S(1)} collective-permute-done((f32[4,4096]{1,0:T(4,128)S(1)}, f32[4,4096]{1,0:T(4,128)S(1)}, u32[]{:S(2)}, u32[]{:S(2)}) %collective-permute-start.3) | collective-permute-done | bytes 65568 | tf_op jit(solution)/shard_map/ppermute | solution.py:446
  23.9 0.1 join.5
  24.0 2.7 %collective-permute-start.4 = (f32[4,4096]{1,0:T(4,128)S(1)}, f32[4,4096]{1,0:T(4,128)S(1)}, u32[]{:S(2)}, u32[]{:S(2)}) collective-permute-start(f32[4,4096]{1,0:T(4,128)S(1)} %join.5), channel_id=1, source_target_pairs={{0,8},{1,9},{2,10},{3,11},{4,12},{5,13},{6,14},{7,15},{8,0},{9,1},... | collective-permute-start | bytes 196616 | tf_op jit(solution)/shard_map/ppermute | solution.py:446
  26.7 3.5 %local.1 = (f32[128,4096]{1,0:T(8,128)S(1)}, f32[128,4096]{1,0:T(8,128)S(1)}, f32[4,8,4096]{2,1,0:T(8,128)S(1)}, f32[16,4096]{1,0:T(8,128)S(1)}) custom-call(bf16[128,128]{1,0:T(8,128)(2,1)S(1)} %get-tuple-element.27.refs_0_, f32[3,3,4096]{2,1,0:T(4,128)S(1)} %copy-done.3, f32[2,2,4096]{2,1,0:T(2,128)S(1)} %copy-done.4, f32[1,4096]{1,0:T(1,128)S(1)} %bitcast.1, ...), custom_call_target="tpu_custom_call" | custom-call | tf_op jit(solution)/shard_map/local/pallas_call | solution.py:396
  30.2 3.1 %gate.1 = bf16[128,4096]{1,0:T(8,128)(2,1)} custom-call(bf16[128,128]{1,0:T(8,128)(2,1)S(1)} %get-tuple-element.28.refs_0_, f32[3,3,4096]{2,1,0:T(4,128)S(1)} %copy-done.3, f32[2,2,4096]{2,1,0:T(2,128)S(1)} %copy-done.4, f32[1,4096]{1,0:T(1,128)S(1)} %bitcast.2, f32[36,4096]{1,0:T(8,128)S(1)} %get-tuple-element.16.refs_4_.refs_3_.refs_2_, ...), custom_call_target="tpu_custom_call" | custom-call | tf_op jit(solution)/shard_map/gate/pallas_call | solution.py:396
  (14 shorter events, 0.0 us)
Async XLA Ops:
  1.0 10.2 %collective-permute-start = (bf16[3,2,4096]{2,1,0:T(2,128)(2,1)S(1)}, bf16[3,2,4096]{2,1,0:T(2,128)(2,1)S(1)}, u32[]{:S(2)}, u32[]{:S(2)}) collective-permute-start(bf16[3,2,4096]{2,1,0:T(2,128)(2,1)S(1)} %slice.3), channel_id=1, source_target_pairs={{0,1},{1,2},{2,3},{3,4},{4,5},{5,6},{6,7},{7,8},{8,9},{9,10},{10,1... | collective-permute-start | bytes 147464 | tf_op jit(solution)/shard_map/ppermute | solution.py:417
  3.6 1.9 %copy-start = (bf16[3,128,4096]{2,1,0:T(8,128)(2,1)S(1)}, bf16[3,128,4096]{2,1,0:T(8,128)(2,1)}, u32[]{:S(2)}) copy-start(bf16[3,128,4096]{2,1,0:T(8,128)(2,1)} %refs_6_.1) | copy-start | bytes 9437188
  5.5 0.9 %copy-start.2 = (f32[3,3,4096]{2,1,0:T(4,128)S(1)}, f32[3,3,4096]{2,1,0:T(4,128)}, u32[]{:S(2)}) copy-start(f32[3,3,4096]{2,1,0:T(4,128)} %refs_1_.5) | copy-start | bytes 442372
  6.4 0.8 %copy-start.6 = (f32[2,4096]{1,0:T(2,128)S(1)}, f32[2,4096]{1,0:T(2,128)}, u32[]{:S(2)}) copy-start(f32[2,4096]{1,0:T(2,128)} %refs_1_.3) | copy-start | bytes 98308
  7.2 0.8 %copy-start.7 = (f32[2,4096]{1,0:T(2,128)S(1)}, f32[2,4096]{1,0:T(2,128)}, u32[]{:S(2)}) copy-start(f32[2,4096]{1,0:T(2,128)} %refs_2_.4) | copy-start | bytes 98308
  7.9 3.3 %copy-start.3 = (f32[3,3,4096]{2,1,0:T(4,128)S(1)}, f32[3,3,4096]{2,1,0:T(4,128)}, u32[]{:S(2)}) copy-start(f32[3,3,4096]{2,1,0:T(4,128)} %refs_1_.5) | copy-start | bytes 442372
  11.1 15.5 %copy-start.1 = (bf16[3,128,4096]{2,1,0:T(8,128)(2,1)S(1)}, bf16[3,128,4096]{2,1,0:T(8,128)(2,1)}, u32[]{:S(2)}) copy-start(bf16[3,128,4096]{2,1,0:T(8,128)(2,1)} %refs_6_.1) | copy-start | bytes 9437188
  11.2 15.5 %copy-start.4 = (f32[2,2,4096]{2,1,0:T(2,128)S(1)}, f32[2,2,4096]{2,1,0:T(2,128)}, u32[]{:S(2)}) copy-start(f32[2,2,4096]{2,1,0:T(2,128)} %refs_2_.7) | copy-start | bytes 196612
  11.2 15.5 %copy-start.5 = (f32[4096]{0:T(1024)S(1)}, f32[4096]{0:T(1024)}, u32[]{:S(2)}) copy-start(f32[4096]{0:T(1024)} %param.8) | copy-start | bytes 49156
  11.4 3.6 %collective-permute-start.1 = (f32[4,4096]{1,0:T(4,128)S(1)}, f32[4,4096]{1,0:T(4,128)S(1)}, u32[]{:S(2)}, u32[]{:S(2)}) collective-permute-start(f32[4,4096]{1,0:T(4,128)S(1)} %get-tuple-element.24.refs_0_), channel_id=1, source_target_pairs={{0,1},{1,0},{2,3},{3,2},{4,5},{5,4},{6,7},{7,6},{8,9},{9,8},{10,11... | collective-permute-start | bytes 196616 | tf_op jit(solution)/shard_map/ppermute | solution.py:446
  15.1 4.4 %collective-permute-start.2 = (f32[4,4096]{1,0:T(4,128)S(1)}, f32[4,4096]{1,0:T(4,128)S(1)}, u32[]{:S(2)}, u32[]{:S(2)}) collective-permute-start(f32[4,4096]{1,0:T(4,128)S(1)} %join.3.refs_0_), channel_id=1, source_target_pairs={{0,2},{1,3},{2,0},{3,1},{4,6},{5,7},{6,4},{7,5},{8,10},{9,11},{10,... | collective-permute-start | bytes 196616 | tf_op jit(solution)/shard_map/ppermute | solution.py:446
  19.6 4.3 %collective-permute-start.3 = (f32[4,4096]{1,0:T(4,128)S(1)}, f32[4,4096]{1,0:T(4,128)S(1)}, u32[]{:S(2)}, u32[]{:S(2)}) collective-permute-start(f32[4,4096]{1,0:T(4,128)S(1)} %join.4.refs_0_), channel_id=1, source_target_pairs={{0,4},{1,5},{2,6},{3,7},{4,0},{5,1},{6,2},{7,3},{8,12},{9,13},{10,... | collective-permute-start | bytes 196616 | tf_op jit(solution)/shard_map/ppermute | solution.py:446
  24.0 6.2 %collective-permute-start.4 = (f32[4,4096]{1,0:T(4,128)S(1)}, f32[4,4096]{1,0:T(4,128)S(1)}, u32[]{:S(2)}, u32[]{:S(2)}) collective-permute-start(f32[4,4096]{1,0:T(4,128)S(1)} %join.5), channel_id=1, source_target_pairs={{0,8},{1,9},{2,10},{3,11},{4,12},{5,13},{6,14},{7,15},{8,0},{9,1},... | collective-permute-start | bytes 196616 | tf_op jit(solution)/shard_map/ppermute | solution.py:446
where the time goes:
time: 33.6 us; the launch traced here: 33.2 us
  starting transfers between devices  11 us (33%)
  Pallas kernels  10.2 us (30%)
  waiting for transfers between devices  6.42 us (19%)
  local copies, waits for them, and re-layouts  5.33 us (16%)
    pallas_call x7, Pallas kernels, kernel_call(): pl.pallas_call(bound, in_specs=[spec(far) for far in in_hbm], out_specs=[...  10.2 us
    ppermute x4, starting transfers between devices, on_device(): lax.ppermute(sent, 'seq', [(i, i ^ 1 << level) for i in range(devices)])  8.56 us
    ppermute x4, waiting for transfers between devices, on_device(): lax.ppermute(sent, 'seq', [(i, i ^ 1 << level) for i in range(devices)])  6.41 us
    unnamed x16, local copies, waits for them, and re-layouts  4.35 us
    ppermute x1, starting transfers between devices, on_device(): lax.ppermute(projected[:, rows - 2:, :], 'seq', [(i, i + 1) for i in rang...  2.4 us
    slice x1, local copies, waits for them, and re-layouts, on_device(): projected[:, rows - 2:, :]  0.98 us
  transfers between devices with their start and end apart: 5, of which 3 were waited for; matrix products, arithmetic and copies ran while one was open for 1% of the time, Pallas kernels for 20%

commit v1 on v0

v1 whole, which is shorter than its diff:
```python
import jax
import jax.numpy as jnp
from jax import lax
from jax.experimental import pallas as pl
from jax.experimental.pallas import tpu as pltpu
from jax.sharding import PartitionSpec as P

SEGMENTS = 8
WIDTH = 256
CHUNK = 512
POLES = 2
SUBROWS = 16
PARTS = (1, 1, 2)
f32 = jnp.float32
bf16 = jnp.bfloat16

LAM, BACK, SEGMENT, SPAN = 0, 1, 2, 5


def order_matrix(row_count, inverse):
    length = row_count // SEGMENTS
    ordered = lax.broadcasted_iota(jnp.int32, (row_count, row_count), 1 if inverse else 0)
    natural = lax.broadcasted_iota(jnp.int32, (row_count, row_count), 0 if inverse else 1)
    wanted = length * (ordered % SEGMENTS) + ordered // SEGMENTS
    return (wanted == natural).astype(f32).astype(bf16)


def wide(value):
    return jnp.broadcast_to(value, (SEGMENTS, value.shape[1]))


def times(a, b):
    return (a[0] * b[0] - a[1] * b[1], a[0] * b[1] + a[1] * b[0])


def plus(a, b):
    return (a[0] + b[0], a[1] + b[1])


def pair_at(ref, index, cols):
    return (ref[4 * index : 4 * index + 2, cols], ref[4 * index + 2 : 4 * index + 4, cols])


def put_pair(ref, index, cols, value):
    ref[4 * index : 4 * index + 2, cols] = value[0]
    ref[4 * index + 2 : 4 * index + 4, cols] = value[1]


def pole_at(ref, index, pole, cols):
    return (wide(ref[pl.ds(4 * index + pole, 1), cols]), wide(ref[pl.ds(4 * index + 2 + pole, 1), cols]))


def half_angle(angle):
    x = 0.5 * angle
    u = x * x
    sine = 1.0 / 6227020800.0
    for term in (-1.0 / 39916800.0, 1.0 / 362880.0, -1.0 / 5040.0, 1.0 / 120.0, -1.0 / 6.0, 1.0):
        sine = sine * u + term
    cosine = -1.0 / 87178291200.0
    for term in (1.0 / 479001600.0, -1.0 / 3628800.0, 1.0 / 40320.0, -1.0 / 720.0, 1.0 / 24.0, -0.5, 1.0):
        cosine = cosine * u + term
    return cosine, sine * x


def fill_powers(power_ref, angle_ref, decay_ref, length, levels):
    cols = slice(None)
    cosine, sine = half_angle(angle_ref[...])
    turn = (1.0 - 2.0 * sine * sine, 2.0 * sine * cosine)
    decay = decay_ref[...]
    damping = jnp.exp(-decay)
    growth = jnp.exp(decay)
    value = (damping * turn[0], damping * turn[1])
    put_pair(power_ref, LAM, cols, value)
    put_pair(power_ref, BACK, cols, (growth * turn[0], -growth * turn[1]))
    for _ in range(length.bit_length() - 1):
        value = times(value, value)
    for level in range(3 + levels):
        put_pair(power_ref, SEGMENT + level, cols, value)
        value = times(value, value)


def steps_of(ref, cols):
    return [ref[SEGMENTS * j : SEGMENTS * (j + 1), cols] for j in range(ref.shape[0] // SEGMENTS)]


def first_mask():
    return lax.broadcasted_iota(jnp.int32, (SEGMENTS, WIDTH), 0) == 0


def delayed(value):
    return jnp.where(first_mask(), 0.0, pltpu.roll(value, 1, 0))


def short_filter(steps, taps_ref, which, cols):
    taps = [wide(taps_ref[tap, which : which + 1, cols]) for tap in range(3)]
    padded = [delayed(steps[-2]), delayed(steps[-1])] + steps
    return [
        taps[0] * padded[j] + taps[1] * padded[j + 1] + taps[2] * padded[j + 2]
        for j in range(len(steps))
    ]


def feedback(lam):
    return 2.0 * lam[0], lam[0] * lam[0] + lam[1] * lam[1]


def span(start, size):
    return pl.ds(pl.multiple_of(start, 128), size)


def loop_columns(chunk_index, chunk, body):
    for part in range(chunk // WIDTH):
        body(part * WIDTH, chunk_index * chunk + part * WIDTH)


def states_kernel(angle_hbm, decay_hbm, taps_hbm, gain_hbm, skip_hbm, proj_ref,
                  prod_ref, scan_ref, total_ref, edge_ref, tail_ref, power_ref, taps_ref, gain_ref, skip_ref,
                  order_ref, angle_ref, decay_ref, k_ref, v_ref, top_ref, end_ref, ks_ref, vs_ref,
                  small_sem, in_sem, *, levels):
    rows, channels = k_ref.shape
    chunk = ks_ref.shape[1]
    count = channels // chunk
    last = rows - SUBROWS
    smalls = [
        pltpu.make_async_copy(source, target, small_sem.at[i])
        for i, (source, target) in enumerate([
            (angle_hbm, angle_ref), (decay_hbm, decay_ref), (taps_hbm, taps_ref), (gain_hbm, gain_ref),
            (skip_hbm, skip_ref), (proj_ref.at[pl.ds(1, 2), pl.ds(0, SUBROWS)], top_ref),
            (proj_ref.at[:, pl.ds(last, SUBROWS)], end_ref)])
    ]

    def fetch(i, which, ref):
        cols = span(i * chunk, chunk)
        return pltpu.make_async_copy(proj_ref.at[which, :, cols], ref.at[:, cols], in_sem.at[which - 1, i])

    for copy in smalls[:3]:
        copy.start()
    for i in range(count):
        fetch(i, 1, k_ref).start()
        fetch(i, 2, v_ref).start()
    for copy in smalls[3:]:
        copy.start()
    order_ref[...] = order_matrix(rows, False)
    for copy in smalls[:3]:
        copy.wait()
    fill_powers(power_ref, angle_ref, decay_ref, rows // SEGMENTS, levels)

    def body(i, _):
        fetch(i, 1, k_ref).wait()
        fetch(i, 2, v_ref).wait()
        at = span(i * chunk, chunk)
        ks_ref[...] = jnp.dot(order_ref[...], k_ref[:, at], preferred_element_type=f32)
        vs_ref[...] = jnp.dot(order_ref[...], v_ref[:, at], preferred_element_type=f32)

        def column(inner, outer):
            cols = slice(inner, inner + WIDTH)
            here = span(outer, WIDTH)
            keys = short_filter(steps_of(ks_ref, cols), taps_ref, 1, here)
            values = short_filter(steps_of(vs_ref, cols), taps_ref, 2, here)
            products = [a * b for a, b in zip(keys, values)]
            for j in range(2):
                products[j] = jnp.where(first_mask(), 0.0, products[j])
            for j in range(0, len(products), 2):
                both = jnp.concatenate(products[j : j + 2], axis=0)
                prod_ref[SEGMENTS * j : SEGMENTS * (j + 2), here] = both.astype(bf16)
            sublane = lax.broadcasted_iota(jnp.int32, (SEGMENTS, WIDTH), 0)
            for pole in range(POLES):
                lam = pole_at(power_ref, LAM, pole, here)
                a1, a2 = feedback(lam)
                late = products[0]
                now = a1 * late + products[1]
                for value in products[2:]:
                    late, now = now, a1 * now - a2 * late + value
                state = (now - lam[0] * late, lam[1] * late)
                for level in range(3):
                    by = 1 << level
                    factor = pole_at(power_ref, SEGMENT + level, pole, here)
                    moved = tuple(jnp.where(sublane >= by, pltpu.roll(part, by, 0), 0.0) for part in state)
                    state = plus(state, times(factor, moved))
                for part in range(2):
                    scan_ref[2 * part + pole, :, here] = state[part]
                    total_ref[2 * part + pole : 2 * part + pole + 1, here] = state[part][SEGMENTS - 1 :]

        loop_columns(i, chunk, column)
        return 0

    lax.fori_loop(0, count, body, 0)
    for copy in smalls[3:]:
        copy.wait()
    edge_ref[0:2] = top_ref[0, 0:2]
    edge_ref[2:4] = top_ref[1, 0:2]
    for which in range(3):
        tail = end_ref[which, SUBROWS - 2 : SUBROWS]
        edge_ref[4 + 2 * which : 6 + 2 * which] = tail
        tail_ref[2 * which : 2 * which + 2] = tail


def first_products(tail, heads, taps_ref):
    def filtered(which, at):
        sequence = [tail[2 * which : 2 * which + 1], tail[2 * which + 1 : 2 * which + 2],
                    heads[2 * which - 2 : 2 * which - 1], heads[2 * which - 1 : 2 * which]]
        return sum(taps_ref[tap, which : which + 1] * sequence[at + tap] for tap in range(3))

    return [filtered(1, at) * filtered(2, at) for at in range(2)]


def pick(condition, a, b):
    return tuple(jnp.where(condition, x, y) for x, y in zip(a, b))


def put_wire(wire_ref, value):
    for part in range(2):
        total = value[part][0:1] + value[part][1:2]
        difference = value[part][0:1] - value[part][1:2]
        wire_ref[2 * part : 2 * part + 2] = jnp.concatenate([total, difference], axis=0).astype(bf16)


def from_wire(wire_ref):
    value = []
    for part in range(2):
        both = wire_ref[2 * part : 2 * part + 2].astype(f32)
        total, difference = both[0:1], both[1:2]
        value.append(0.5 * jnp.concatenate([total + difference, total - difference], axis=0))
    return tuple(value)


def merge_kernel(total_ref, mate_ref, edge_ref, mate_edge_ref, far_even_ref, far_odd_ref, power_ref, taps_ref,
                 gain_ref, skip_ref, ending_ref, wire_ref, lead_ref, enter_ref, fix_ref):
    cols = slice(None)
    odd = lax.axis_index("seq") % 2 == 1
    far = far_even_ref[...].astype(f32) + far_odd_ref[...].astype(f32)
    mine = edge_ref[...].astype(f32)
    mates = mate_edge_ref[...].astype(f32)
    even_edge, odd_edge = jnp.where(odd, mates, mine), jnp.where(odd, mine, mates)
    power = pair_at(power_ref, SPAN, cols)
    back = pair_at(power_ref, BACK, cols)
    own, mate = pair_at(total_ref, 0, cols), pair_at(mate_ref, 0, cols)
    even_total, odd_total = pick(odd, mate, own), pick(odd, own, mate)
    extras, firsts, endings = [], [], []
    for tail, edge, total in ((far, even_edge, even_total), (even_edge[4:10], odd_edge, odd_total)):
        first, second = first_products(tail, edge[0:4], taps_ref)
        extra = times(back, (second * back[0] + first, second * back[1]))
        extras.append(extra)
        firsts.append((first, second))
        endings.append(plus(total, times(power, extra)))
    joined = plus(times(power, endings[0]), endings[1])
    put_pair(ending_ref, 0, cols, joined)
    put_wire(wire_ref, joined)
    one = (jnp.ones_like(power[0]), jnp.zeros_like(power[0]))
    put_pair(lead_ref, 0, cols, pick(odd, power, one))
    put_pair(enter_ref, 0, cols, pick(odd, plus(endings[0], extras[1]), extras[0]))
    first, second = pick(odd, firsts[1], firsts[0])
    skip = skip_ref[...]
    jump = sum(gain_ref[0, pole : pole + 1] * back[0][pole : pole + 1] - gain_ref[1, pole : pole + 1] * back[1][pole : pole + 1]
               for pole in range(POLES))
    fix_ref[0:1] = skip * first - jump * second
    fix_ref[1:2] = skip * second
    before = jnp.where(odd, even_edge[4:6], far[0:2])
    fix_ref[2:3] = taps_ref[0, 0:1] * before[0:1] + taps_ref[1, 0:1] * before[1:2]
    fix_ref[3:4] = taps_ref[0, 0:1] * before[1:2]


def join_kernel(ending_ref, got_ref, power_ref, lead_ref, enter_ref,
                joined_ref, wire_ref, next_lead_ref, next_enter_ref, *, level):
    upper = (lax.axis_index("seq") >> level) % 2 == 1
    cols = slice(None)
    mine = pair_at(ending_ref, 0, cols)
    other = from_wire(got_ref)
    factor = pair_at(power_ref, SPAN + level, cols)
    early, late = pick(upper, other, mine), pick(upper, mine, other)
    joined = plus(times(factor, early), late)
    put_pair(joined_ref, 0, cols, joined)
    put_wire(wire_ref, joined)
    lead = pair_at(lead_ref, 0, cols)
    enter = pair_at(enter_ref, 0, cols)
    put_pair(next_lead_ref, 0, cols, pick(upper, times(lead, factor), lead))
    put_pair(next_enter_ref, 0, cols, pick(upper, plus(enter, times(lead, other)), enter))


def local_kernel(taps_ref, gain_ref, skip_ref, power_ref, scan_ref, prod_ref, proj_ref, after_ref,
                 query_ref, local_ref, enter_ref, order_ref, q_ref, qs_ref, in_sem, *, base):
    rows, channels = q_ref.shape
    chunk = qs_ref.shape[1]
    count = channels // chunk

    def fetch(i):
        return pltpu.make_async_copy(
            proj_ref.at[0, :, span(base + i * chunk, chunk)], q_ref.at[:, span(i * chunk, chunk)], in_sem.at[i])

    for i in range(count):
        fetch(i).start()
    order_ref[...] = order_matrix(rows, False)

    def body(i, _):
        fetch(i).wait()
        qs_ref[...] = jnp.dot(order_ref[...], q_ref[:, span(i * chunk, chunk)], preferred_element_type=f32)

        def column(inner, outer):
            cols = slice(inner, inner + WIDTH)
            put = span(outer, WIDTH)
            here = span(base + outer, WIDTH)
            queries = short_filter(steps_of(qs_ref, cols), taps_ref, 0, here)
            for j, value in enumerate(queries):
                query_ref[SEGMENTS * j : SEGMENTS * (j + 1), put] = value
            products = []
            for j in range(0, len(queries), 2):
                both = prod_ref[SEGMENTS * j : SEGMENTS * (j + 2), here].astype(f32)
                products += [both[:SEGMENTS], both[SEGMENTS:]]
            before = delayed(products[-1])
            skip = wide(skip_ref[0:1, here])
            sublane = lax.broadcasted_iota(jnp.int32, (SEGMENTS, WIDTH), 0)
            coefs = []
            for pole in range(POLES):
                lam = pole_at(power_ref, LAM, pole, here)
                back = pole_at(power_ref, BACK, pole, here)
                gain = tuple(wide(gain_ref[part, pole : pole + 1, here]) for part in range(2))
                a1, a2 = feedback(lam)
                b1 = gain[0] * lam[0] + gain[1] * lam[1]
                carry = tuple(delayed(scan_ref[2 * part + pole, :, here]) for part in range(2))
                gain_back = times(gain, back)
                y1 = gain[0] * carry[0] - gain[1] * carry[1]
                y2 = gain_back[0] * (carry[0] - before) - gain_back[1] * carry[1]
                coefs.append([a1, a2, gain[0], b1, y1, y2])
                reach = gain
                for level in range(3):
                    factor = pole_at(power_ref, SEGMENT + level, pole, here)
                    bit = (sublane // (1 << level)) % 2 == 1
                    reach = times(reach, (jnp.where(bit, factor[0], 1.0), jnp.where(bit, factor[1], 0.0)))
                for part in range(2):
                    enter_ref[2 * part + pole, :, put] = reach[part]
            previous = before
            for j, value in enumerate(products):
                total = skip * value
                for pole in range(POLES):
                    a1, a2, b0, b1, y1, y2 = coefs[pole]
                    y = a1 * y1 - a2 * y2 + (b0 * value - b1 * previous)
                    coefs[pole][4:] = [y, y1]
                    total = total + y
                previous = value
                local_ref[SEGMENTS * j : SEGMENTS * (j + 1), put] = total

        loop_columns(i, chunk, column)
        return 0

    lax.fori_loop(0, count, body, 0)


def gate_kernel(power_ref, got_ref, lead_ref, enter_ref, fix_ref, *rest, level, parts):
    tables = [rest[3 * i : 3 * i + 3] for i in range(len(parts))]
    out_hbm, order_ref, out_ref, gated_ref, state_ref, out_sem = rest[3 * len(parts) :]
    rows, channels = out_ref.shape
    chunk = gated_ref.shape[1]
    count = channels // chunk
    cols = slice(None)
    upper = (lax.axis_index("seq") >> level) % 2 == 1
    state = pair_at(enter_ref, 0, cols)
    add = times(pair_at(lead_ref, 0, cols), from_wire(got_ref))
    put_pair(state_ref, 0, cols, pick(upper, plus(state, add), state))
    order_ref[...] = order_matrix(rows, True)

    def send(i):
        place = span(i * chunk, chunk)
        return pltpu.make_async_copy(out_ref.at[:, place], out_hbm.at[:, place], out_sem.at[i])

    base = 0
    for part, (query_ref, local_ref, reach_ref) in zip(parts, tables):

        def body(i, _, base=base, query_ref=query_ref, local_ref=local_ref, reach_ref=reach_ref):
            def column(inner, outer):
                cols = slice(inner, inner + WIDTH)
                take = span(outer, WIDTH)
                here = span(base + outer, WIDTH)
                queries = steps_of(query_ref, take)
                local = steps_of(local_ref, take)
                for j in range(2):
                    local[j] = local[j] + jnp.where(first_mask(), wide(fix_ref[j : j + 1, here]), 0.0)
                    queries[j] = queries[j] + jnp.where(first_mask(), wide(fix_ref[2 + j : 3 + j, here]), 0.0)
                coefs = []
                for pole in range(POLES):
                    lam = pole_at(power_ref, LAM, pole, here)
                    back = pole_at(power_ref, BACK, pole, here)
                    state = times(pole_at(state_ref, 0, pole, here), (reach_ref[pole, :, take], reach_ref[2 + pole, :, take]))
                    y2 = state[0] * back[0] - state[1] * back[1]
                    coefs.append([*feedback(lam), state[0], y2])
                gated = []
                for j in range(len(queries)):
                    total = local[j]
                    for pole in range(POLES):
                        a1, a2, y1, y2 = coefs[pole]
                        y = a1 * y1 - a2 * y2
                        coefs[pole][2:] = [y, y1]
                        total = total + y
                    gated.append(queries[j] * total)
                    if j % 2:
                        both = jnp.concatenate(gated[-2:], axis=0)
                        gated_ref[SEGMENTS * (j - 1) : SEGMENTS * (j + 1), cols] = both.astype(bf16)

            loop_columns(i, chunk, column)
            out_ref[:, span(base + i * chunk, chunk)] = jnp.dot(
                order_ref[...], gated_ref[...], preferred_element_type=f32).astype(bf16)
            send(base // chunk + i).start()
            return 0

        lax.fori_loop(0, part // chunk, body, 0)
        base += part
    for i in range(count):
        send(i).wait()


def kernel_call(body, name, outs, scratch, operands, in_hbm, out_hbm=(), **options):
    def spec(far):
        return pl.BlockSpec(memory_space=pltpu.HBM if far else pltpu.VMEM)

    def bound(*refs):
        return body(*refs, **options)

    return pl.pallas_call(
        bound,
        in_specs=[spec(i in in_hbm) for i in range(len(operands))],
        out_specs=[spec(i in out_hbm) for i in range(len(outs))],
        out_shape=[jax.ShapeDtypeStruct(shape, dtype) for shape, dtype in outs],
        scratch_shapes=scratch,
        compiler_params=pltpu.CompilerParams(vmem_limit_bytes=32 << 20),
        name=name,
    )(*operands)


def on_device(projected, short_taps, skip_gain, residues, pole_angles, decay_rates):
    _, rows, channels = projected.shape
    chunk = min(CHUNK, channels)
    devices = lax.axis_size("seq")
    levels = devices.bit_length() - 1
    parts = [channels // sum(PARTS) * share for share in PARTS]
    arguments = [pole_angles, decay_rates, short_taps, residues, skip_gain[None], projected]
    arguments = [pltpu.with_memory_space_constraint(argument, pltpu.HBM) for argument in arguments]
    projected = arguments[-1]
    state = ((4, channels), f32)
    wire = ((4, channels), bf16)
    square = pltpu.VMEM((rows, rows), bf16)
    dma = pltpu.SemaphoreType.DMA

    products, scan, total, edges, tail, powers, taps, gains, skip = kernel_call(
        states_kernel, "states",
        [((rows, channels), bf16), ((4, SEGMENTS, channels), f32), state, ((10, channels), bf16),
         ((6, channels), bf16), ((4 * (SPAN + levels), channels), f32), (short_taps.shape, f32),
         (residues.shape, f32), ((1, channels), f32)],
        [square] + [pltpu.VMEM(pole_angles.shape, f32)] * 2 + [pltpu.VMEM((rows, channels), bf16)] * 2
        + [pltpu.VMEM((2, SUBROWS, channels), bf16), pltpu.VMEM((3, SUBROWS, channels), bf16)]
        + [pltpu.VMEM((rows, chunk), f32)] * 2 + [dma((7,)), dma((2, channels // chunk))],
        arguments, range(6), levels=levels)

    def move(array, pairs):
        return lax.ppermute(array, "seq", [(a, b) for a, b in pairs if b < devices])

    def exchange(array, level):
        return move(array, [(i, i ^ (1 << level)) for i in range(devices)])

    tails_even = move(tail, [(i, i + 1) for i in range(1, devices, 2)])
    tails_odd = move(tail, [(i, i + 2) for i in range(1, devices, 2)])
    mate_edges = exchange(edges, 0)
    mate_total = exchange(total, 0)
    ending, sent, lead, enter, fix = kernel_call(
        merge_kernel, "merge", [state, wire, state, state, state], [],
        [total, mate_total, edges, mate_edges, tails_even, tails_odd, powers, taps, gains, skip], ())

    tables = []
    base = 0
    for level in range(1, levels):
        got = exchange(sent, level)
        while len(tables) < len(parts) and (len(tables) < level or level == levels - 1):
            part = parts[len(tables)]
            plane = ((rows, part), f32)
            tables.append(kernel_call(
                local_kernel, "local", [plane, plane, ((4, SEGMENTS, part), f32)],
                [square, pltpu.VMEM((rows, part), bf16), pltpu.VMEM((rows, chunk), f32), dma((part // chunk,))],
                [taps, gains, skip, powers, scan, products, projected, ending], (6,), base=base))
            base += part
        if level + 1 < levels:
            ending, sent, lead, enter = kernel_call(
                join_kernel, "join", [state, wire, state, state], [], [ending, got, powers, lead, enter], (),
                level=level)

    (out,) = kernel_call(
        gate_kernel, "gate", [((rows, channels), bf16)],
        [square, pltpu.VMEM((rows, channels), bf16), pltpu.VMEM((rows, chunk), bf16),
         pltpu.VMEM((4, channels), f32), dma((channels // chunk,))],
        [powers, got, lead, enter, fix, *[array for table in tables for array in table]], (), (0,),
        level=levels - 1, parts=parts)
    return out


def solution(mesh):
    return jax.shard_map(
        on_device,
        mesh=mesh,
        in_specs=(P(None, ("grp", "seq"), None), P(), P(), P(), P(), P()),
        out_specs=P(("grp", "seq"), None),
        check_vma=False,
    )
```

time: 33.6 us -> 35.4 us (1.054)
  local copies, waits for them, and re-layouts: 5.33 us -> 0 us
  starting transfers between devices: 11 us -> 16.3 us
  Pallas kernels: 10.2 us -> 15 us
  waiting for transfers between devices: 6.42 us -> 3.8 us
    ppermute x5 -> x7, starting transfers between devices: 11 us -> 16.3 us  [move(): return lax.ppermute(array, 'seq', [(a, b) for a, b in pairs if b < devices])]
    pallas_call x7 -> x8, Pallas kernels: 10.2 us -> 15 us  [kernel_call(): pl.pallas_call(bound, in_specs=[spec(i in in_hbm) for i in range(len(oper...]
    unnamed x16 -> x0, local copies, waits for them, and re-layouts: 4.35 us -> none
    ppermute x5 -> x7, waiting for transfers between devices: 6.42 us -> 3.8 us  [move(): return lax.ppermute(array, 'seq', [(a, b) for a, b in pairs if b < devices])]
    slice x1 -> x0, local copies, waits for them, and re-layouts: 0.98 us -> none  [on_device(): projected[:, rows - 2:, :]]
  transfers between devices with their start and end apart: 5 -> 7, of which waited for: 3 -> 2; matrix products, arithmetic and copies ran while one was open for 1% -> 0% of each run, Pallas kernels for 20% -> 16%
where the time goes in v1:
time: 35.4 us; the launch traced here: 35.2 us
  starting transfers between devices  16.3 us (46%)
  Pallas kernels  15 us (42%)
  waiting for transfers between devices  3.8 us (11%)
    ppermute x7, starting transfers between devices, move(): return lax.ppermute(array, 'seq', [(a, b) for a, b in pairs if b < devices])  16.3 us
    pallas_call x8, Pallas kernels, kernel_call(): pl.pallas_call(bound, in_specs=[spec(i in in_hbm) for i in range(len(oper...  15 us
    ppermute x7, waiting for transfers between devices, move(): return lax.ppermute(array, 'seq', [(a, b) for a, b in pairs if b < devices])  3.8 us
  transfers between devices with their start and end apart: 7, of which 2 were waited for; matrix products, arithmetic and copies ran while one was open for 0% of the time, Pallas kernels for 16%

profile of v1, /device:TPU:0, one launch (start us, length us, event | category | flops | bytes accessed | tf_op | source)
XLA Modules:
  0.0 35.2 jit_solution(11533441954748782685)
XLA Ops:
  0.0 5.3 %states.1 = (bf16[128,4096]{1,0:T(8,128)(2,1)S(1)}, f32[4,8,4096]{2,1,0:T(8,128)S(1)}, f32[4,4096]{1,0:T(4,128)S(1)}, bf16[10,4096]{1,0:T(8,128)(2,1)S(1)}, bf16...) custom-call(f32[2,4096]{1,0:T(2,128)} %refs_0_.1, ...), custom_call_target="tpu_custom_call" | custom-call | tf_op jit(solution)/shard_map/states/pallas_call | solution.py:417
  5.3 0.6 %collective-permute-start.1 = (bf16[10,4096]{1,0:T(8,128)(2,1)S(1)}, bf16[10,4096]{1,0:T(8,128)(2,1)S(1)}, u32[]{:S(2)}, u32[]{:S(2)}) collective-permute-start(bf16[10,4096]{1,0:T(8,128)(2,1)S(1)} %get-tuple-element.38.refs_2_), channel_id=1, source_target_pairs={{0,1},{1,0},{2,3},{3,2},{4,5},{5,4},{6,7},{7,6},{8,9},{9,8},{10,11... | collective-permute-start | bytes 245768 | tf_op jit(solution)/shard_map/ppermute | solution.py:453
  5.8 0.1 collective-permute-start
  5.9 0.7 %collective-permute-start.3 = (bf16[6,4096]{1,0:T(8,128)(2,1)S(1)}, bf16[6,4096]{1,0:T(8,128)(2,1)S(1)}, u32[]{:S(2)}, u32[]{:S(2)}) collective-permute-start(bf16[6,4096]{1,0:T(8,128)(2,1)S(1)} %get-tuple-element.39), channel_id=1, source_target_pairs={{1,3},{3,5},{5,7},{7,9},{9,11},{11,13},{13,15},{17,19},{19,21},{21... | collective-permute-start | bytes 147464 | tf_op jit(solution)/shard_map/ppermute | solution.py:453
  6.6 0.7 %collective-permute-start.2 = (bf16[6,4096]{1,0:T(8,128)(2,1)S(1)}, bf16[6,4096]{1,0:T(8,128)(2,1)S(1)}, u32[]{:S(2)}, u32[]{:S(2)}) collective-permute-start(bf16[6,4096]{1,0:T(8,128)(2,1)S(1)} %get-tuple-element.39), channel_id=1, source_target_pairs={{1,2},{3,4},{5,6},{7,8},{9,10},{11,12},{13,14},{17,18},{19,20},{21... | collective-permute-start | bytes 147464 | tf_op jit(solution)/shard_map/ppermute | solution.py:453
  7.2 0.0 collective-permute-done.3.refs_5_
  7.2 0.0 collective-permute-done.2.refs_4_
  7.3 0.0 collective-permute-done.refs_1_
  7.3 0.0 collective-permute-done.1.refs_3_
  7.3 0.6 %merge.1 = (f32[4,4096]{1,0:T(4,128)S(1)}, bf16[4,4096]{1,0:T(4,128)(2,1)S(1)}, f32[4,4096]{1,0:T(4,128)S(1)}, f32[4,4096]{1,0:T(4,128)S(1)}, f32[4,4096]{1,0:T(4,128)S(1)}) custom-call(f32[4,4096]{1,0:T(4,128)S(1)} %get-tuple-element.37.refs_0_, f32[4,4096]{1,0:T(4,128)S(1)} %collective-permute-done.refs_1_, ...), custom_call_target="tpu_custom_call" | custom-call | tf_op jit(solution)/shard_map/merge/pallas_call | solution.py:417
  7.9 8.2 %collective-permute-start.4 = (bf16[4,4096]{1,0:T(4,128)(2,1)S(1)}, bf16[4,4096]{1,0:T(4,128)(2,1)S(1)}, u32[]{:S(2)}, u32[]{:S(2)}) collective-permute-start(bf16[4,4096]{1,0:T(4,128)(2,1)S(1)} %get-tuple-element.44), channel_id=1, source_target_pairs={{0,2},{1,3},{2,0},{3,1},{4,6},{5,7},{6,4},{7,5},{8,10},{9,11},{10,... | collective-permute-start | bytes 98312 | tf_op jit(solution)/shard_map/ppermute | solution.py:453
  16.1 1.9 %collective-permute-done.4.refs_1_ = bf16[4,4096]{1,0:T(4,128)(2,1)S(1)} collective-permute-done((bf16[4,4096]{1,0:T(4,128)(2,1)S(1)}, bf16[4,4096]{1,0:T(4,128)(2,1)S(1)}, u32[]{:S(2)}, u32[]{:S(2)}) %collective-permute-start.4) | collective-permute-done | bytes 32800 | tf_op jit(solution)/shard_map/ppermute | solution.py:453
  18.0 0.3 join.2
  18.3 3.0 %collective-permute-start.5 = (bf16[4,4096]{1,0:T(4,128)(2,1)S(1)}, bf16[4,4096]{1,0:T(4,128)(2,1)S(1)}, u32[]{:S(2)}, u32[]{:S(2)}) collective-permute-start(bf16[4,4096]{1,0:T(4,128)(2,1)S(1)} %get-tuple-element.48), channel_id=1, source_target_pairs={{0,4},{1,5},{2,6},{3,7},{4,0},{5,1},{6,2},{7,3},{8,12},{9,13},{10,... | collective-permute-start | bytes 98312 | tf_op jit(solution)/shard_map/ppermute | solution.py:453
  21.3 1.9 %collective-permute-done.5.refs_1_ = bf16[4,4096]{1,0:T(4,128)(2,1)S(1)} collective-permute-done((bf16[4,4096]{1,0:T(4,128)(2,1)S(1)}, bf16[4,4096]{1,0:T(4,128)(2,1)S(1)}, u32[]{:S(2)}, u32[]{:S(2)}) %collective-permute-start.5) | collective-permute-done | bytes 32800 | tf_op jit(solution)/shard_map/ppermute | solution.py:453
  23.2 0.3 join.3
  23.5 3.1 %collective-permute-start.6 = (bf16[4,4096]{1,0:T(4,128)(2,1)S(1)}, bf16[4,4096]{1,0:T(4,128)(2,1)S(1)}, u32[]{:S(2)}, u32[]{:S(2)}) collective-permute-start(bf16[4,4096]{1,0:T(4,128)(2,1)S(1)} %get-tuple-element.51), channel_id=1, source_target_pairs={{0,8},{1,9},{2,10},{3,11},{4,12},{5,13},{6,14},{7,15},{8,0},{9,1},... | collective-permute-start | bytes 98312 | tf_op jit(solution)/shard_map/ppermute | solution.py:453
  26.6 1.6 %local.3 = (f32[128,1024]{1,0:T(8,128)S(1)}, f32[128,1024]{1,0:T(8,128)S(1)}, f32[4,8,1024]{2,1,0:T(8,128)S(1)}) custom-call(f32[3,3,4096]{2,1,0:T(4,128)S(1)} %get-tuple-element.40.refs_7_.refs_0_, f32[2,2,4096]{2,1,0:T(2,128)S(1)} %get-tuple-element.41.refs_8_.refs_1_, f32[1,4096]{1,0:T(1,128)S(1)} %get-tuple-element.42.refs_9_.refs_2_, ...), custom_call_target="tpu_custom_call" | custom-call | tf_op jit(solution)/shard_map/local/pallas_call | solution.py:417
  28.2 1.6 %local.4 = (f32[128,1024]{1,0:T(8,128)S(1)}, f32[128,1024]{1,0:T(8,128)S(1)}, f32[4,8,1024]{2,1,0:T(8,128)S(1)}) custom-call(f32[3,3,4096]{2,1,0:T(4,128)S(1)} %get-tuple-element.40.refs_7_.refs_0_, f32[2,2,4096]{2,1,0:T(2,128)S(1)} %get-tuple-element.41.refs_8_.refs_1_, f32[1,4096]{1,0:T(1,128)S(1)} %get-tuple-element.42.refs_9_.refs_2_, ...), custom_call_target="tpu_custom_call" | custom-call | tf_op jit(solution)/shard_map/local/pallas_call | solution.py:417
  29.8 2.3 %local.5 = (f32[128,2048]{1,0:T(8,128)S(1)}, f32[128,2048]{1,0:T(8,128)S(1)}, f32[4,8,2048]{2,1,0:T(8,128)S(1)}) custom-call(f32[3,3,4096]{2,1,0:T(4,128)S(1)} %get-tuple-element.40.refs_7_.refs_0_, f32[2,2,4096]{2,1,0:T(2,128)S(1)} %get-tuple-element.41.refs_8_.refs_1_, f32[1,4096]{1,0:T(1,128)S(1)} %get-tuple-element.42.refs_9_.refs_2_, ...), custom_call_target="tpu_custom_call" | custom-call | tf_op jit(solution)/shard_map/local/pallas_call | solution.py:417
  32.2 0.0 collective-permute-done.6.refs_1_
  32.2 3.0 %gate.1 = bf16[128,4096]{1,0:T(8,128)(2,1)} custom-call(f32[36,4096]{1,0:T(8,128)S(1)} %get-tuple-element.36.refs_6_.refs_2_.refs_3_.refs_0_, bf16[4,4096]{1,0:T(4,128)(2,1)S(1)} %collective-permute-done.6.refs_1_, f32[4,4096]{1,0:T(4,128)S(1)} %get-tuple-element.52.refs_2_, f32[4,4096]{1,0:T(4,128)S(1)} %get-tuple-element.53.refs_3_, ...), custom_call_target="tpu_custom_call" | custom-call | tf_op jit(solution)/shard_map/gate/pallas_call | solution.py:417
Async XLA Ops:
  5.3 2.0 %collective-permute-start.1 = (bf16[10,4096]{1,0:T(8,128)(2,1)S(1)}, bf16[10,4096]{1,0:T(8,128)(2,1)S(1)}, u32[]{:S(2)}, u32[]{:S(2)}) collective-permute-start(bf16[10,4096]{1,0:T(8,128)(2,1)S(1)} %get-tuple-element.38.refs_2_), channel_id=1, source_target_pairs={{0,1},{1,0},{2,3},{3,2},{4,5},{5,4},{6,7},{7,6},{8,9},{9,8},{10,11... | collective-permute-start | bytes 245768 | tf_op jit(solution)/shard_map/ppermute | solution.py:453
  5.8 1.4 %collective-permute-start = (f32[4,4096]{1,0:T(4,128)S(1)}, f32[4,4096]{1,0:T(4,128)S(1)}, u32[]{:S(2)}, u32[]{:S(2)}) collective-permute-start(f32[4,4096]{1,0:T(4,128)S(1)} %get-tuple-element.37.refs_0_), channel_id=1, source_target_pairs={{0,1},{1,0},{2,3},{3,2},{4,5},{5,4},{6,7},{7,6},{8,9},{9,8},{10,11... | collective-permute-start | bytes 196616 | tf_op jit(solution)/shard_map/ppermute | solution.py:453
  5.9 1.3 %collective-permute-start.3 = (bf16[6,4096]{1,0:T(8,128)(2,1)S(1)}, bf16[6,4096]{1,0:T(8,128)(2,1)S(1)}, u32[]{:S(2)}, u32[]{:S(2)}) collective-permute-start(bf16[6,4096]{1,0:T(8,128)(2,1)S(1)} %get-tuple-element.39), channel_id=1, source_target_pairs={{1,3},{3,5},{5,7},{7,9},{9,11},{11,13},{13,15},{17,19},{19,21},{21... | collective-permute-start | bytes 147464 | tf_op jit(solution)/shard_map/ppermute | solution.py:453
  6.6 0.7 %collective-permute-start.2 = (bf16[6,4096]{1,0:T(8,128)(2,1)S(1)}, bf16[6,4096]{1,0:T(8,128)(2,1)S(1)}, u32[]{:S(2)}, u32[]{:S(2)}) collective-permute-start(bf16[6,4096]{1,0:T(8,128)(2,1)S(1)} %get-tuple-element.39), channel_id=1, source_target_pairs={{1,2},{3,4},{5,6},{7,8},{9,10},{11,12},{13,14},{17,18},{19,20},{21... | collective-permute-start | bytes 147464 | tf_op jit(solution)/shard_map/ppermute | solution.py:453
  7.9 10.1 %collective-permute-start.4 = (bf16[4,4096]{1,0:T(4,128)(2,1)S(1)}, bf16[4,4096]{1,0:T(4,128)(2,1)S(1)}, u32[]{:S(2)}, u32[]{:S(2)}) collective-permute-start(bf16[4,4096]{1,0:T(4,128)(2,1)S(1)} %get-tuple-element.44), channel_id=1, source_target_pairs={{0,2},{1,3},{2,0},{3,1},{4,6},{5,7},{6,4},{7,5},{8,10},{9,11},{10,... | collective-permute-start | bytes 98312 | tf_op jit(solution)/shard_map/ppermute | solution.py:453
  18.3 4.9 %collective-permute-start.5 = (bf16[4,4096]{1,0:T(4,128)(2,1)S(1)}, bf16[4,4096]{1,0:T(4,128)(2,1)S(1)}, u32[]{:S(2)}, u32[]{:S(2)}) collective-permute-start(bf16[4,4096]{1,0:T(4,128)(2,1)S(1)} %get-tuple-element.48), channel_id=1, source_target_pairs={{0,4},{1,5},{2,6},{3,7},{4,0},{5,1},{6,2},{7,3},{8,12},{9,13},{10,... | collective-permute-start | bytes 98312 | tf_op jit(solution)/shard_map/ppermute | solution.py:453
  23.5 8.7 %collective-permute-start.6 = (bf16[4,4096]{1,0:T(4,128)(2,1)S(1)}, bf16[4,4096]{1,0:T(4,128)(2,1)S(1)}, u32[]{:S(2)}, u32[]{:S(2)}) collective-permute-start(bf16[4,4096]{1,0:T(4,128)(2,1)S(1)} %get-tuple-element.51), channel_id=1, source_target_pairs={{0,8},{1,9},{2,10},{3,11},{4,12},{5,13},{6,14},{7,15},{8,0},{9,1},... | collective-permute-start | bytes 98312 | tf_op jit(solution)/shard_map/ppermute | solution.py:453

commit v2 on v1

--- a/solution.py
+++ b/solution.py
@@ -114,8 +114,8 @@
 
 
 def states_kernel(angle_hbm, decay_hbm, taps_hbm, gain_hbm, skip_hbm, proj_ref,
-                  prod_ref, scan_ref, total_ref, edge_ref, tail_ref, power_ref, taps_ref, gain_ref, skip_ref,
-                  order_ref, angle_ref, decay_ref, k_ref, v_ref, top_ref, end_ref, ks_ref, vs_ref,
+                  prod_ref, scan_ref, keep_total, give_total, keep_edge, give_edge, power_ref, taps_ref, gain_ref, skip_ref,
+                  total_ref, edge_ref, order_ref, angle_ref, decay_ref, k_ref, v_ref, top_ref, end_ref, ks_ref, vs_ref,
                   small_sem, in_sem, *, levels):
     rows, channels = k_ref.shape
     chunk = ks_ref.shape[1]
@@ -187,21 +187,43 @@
     lax.fori_loop(0, count, body, 0)
     for copy in smalls[3:]:
         copy.wait()
-    edge_ref[0:2] = top_ref[0, 0:2]
-    edge_ref[2:4] = top_ref[1, 0:2]
     for which in range(3):
-        tail = end_ref[which, SUBROWS - 2 : SUBROWS]
-        edge_ref[4 + 2 * which : 6 + 2 * which] = tail
-        tail_ref[2 * which : 2 * which + 2] = tail
-
-
-def first_products(tail, heads, taps_ref):
+        edge_ref[2 * which : 2 * which + 2] = end_ref[which, SUBROWS - 2 : SUBROWS]
+    for which in range(2):
+        edge_ref[6 + 2 * which : 8 + 2 * which] = top_ref[which, 0:2]
+    own, other = halves(channels)
+    keep_total[...] = total_ref[:, own]
+    give_total[...] = total_ref[:, other]
+    keep_edge[...] = edge_ref[:, own]
+    give_edge[...] = edge_ref[:, other]
+
+
+def halves(channels):
+    half = channels // 2
+    odd = lax.axis_index("seq") % 2
+    return span(odd * half, half), span((1 - odd) * half, half)
+
+
+def first_products(tail, heads, taps):
     def filtered(which, at):
         sequence = [tail[2 * which : 2 * which + 1], tail[2 * which + 1 : 2 * which + 2],
                     heads[2 * which - 2 : 2 * which - 1], heads[2 * which - 1 : 2 * which]]
-        return sum(taps_ref[tap, which : which + 1] * sequence[at + tap] for tap in range(3))
+        return sum(taps[tap, which : which + 1] * sequence[at + tap] for tap in range(3))
 
     return [filtered(1, at) * filtered(2, at) for at in range(2)]
+
+
+def extra_state(products, back):
+    first, second = products
+    return times(back, (second * back[0] + first, second * back[1]))
+
+
+def fixed_rows(products, tail, taps, skip, gain, back):
+    first, second = products
+    jump = sum(gain[0, pole : pole + 1] * back[0][pole : pole + 1] - gain[1, pole : pole + 1] * back[1][pole : pole + 1]
+               for pole in range(POLES))
+    return [skip * first - jump * second, skip * second,
+            taps[0, 0:1] * tail[0:1] + taps[1, 0:1] * tail[1:2], taps[0, 0:1] * tail[1:2]]
 
 
 def pick(condition, a, b):
@@ -224,57 +246,88 @@
     return tuple(value)
 
 
-def merge_kernel(total_ref, mate_ref, edge_ref, mate_edge_ref, far_even_ref, far_odd_ref, power_ref, taps_ref,
-                 gain_ref, skip_ref, ending_ref, wire_ref, lead_ref, enter_ref, fix_ref):
-    cols = slice(None)
+ALL = slice(None)
+
+
+def merge_kernel(total_ref, mate_ref, edge_ref, mate_edge_ref, power_ref, taps_ref, gain_ref, skip_ref,
+                 joined_ref, wire_ref, lead_ref, enter_ref, base_ref, fix_ref, head_ref, *, channels):
+    device = lax.axis_index("seq")
+    odd = device % 2 == 1
+    half = halves(channels)[0]
+    taps, gain, skip = taps_ref[:, :, half], gain_ref[:, :, half], skip_ref[:, half]
+    power, back = pair_at(power_ref, SPAN, half), pair_at(power_ref, BACK, half)
+    mine, mates = edge_ref[...].astype(f32), mate_edge_ref[...].astype(f32)
+    even_edge, odd_edge = jnp.where(odd, mates, mine), jnp.where(odd, mine, mates)
+    own, mate = pair_at(total_ref, 0, ALL), pair_at(mate_ref, 0, ALL)
+    even_total, odd_total = pick(odd, mate, own), pick(odd, own, mate)
+    products = first_products(even_edge[0:6], odd_edge[6:10], taps)
+    base = plus(even_total, extra_state(products, back))
+    put_pair(base_ref, 0, ALL, base)
+    for i, value in enumerate(fixed_rows(products, even_edge[0:6], taps, skip, gain, back)):
+        fix_ref[i : i + 1] = value
+    start = extra_state(first_products(jnp.zeros_like(even_edge[0:6]), even_edge[6:10], taps), back)
+    enter = tuple(jnp.where(device < 2, part, 0.0) for part in start)
+    put_pair(enter_ref, 0, ALL, enter)
+    joined = plus(odd_total, times(power, plus(base, times(power, enter))))
+    put_pair(joined_ref, 0, ALL, joined)
+    put_pair(lead_ref, 0, ALL, (jnp.ones_like(power[0]), jnp.zeros_like(power[0])))
+    put_wire(wire_ref, joined)
+    wire_ref[4:10] = odd_edge[0:6].astype(bf16)
+    wire_ref[10:14] = even_edge[6:10].astype(bf16)
+    head_ref[...] = even_edge[6:10].astype(bf16)
+
+
+def step_of(level, sent_ref, got_ref, power_ref, taps_ref, lead_ref, enter_ref, tail_before, half):
+    device = lax.axis_index("seq")
+    upper = (device >> level) % 2 == 1
+    leads = jnp.logical_and(upper, (device % (1 << level)) < 2)
+    back = pair_at(power_ref, BACK, half)
+    early_tail = jnp.where(upper, got_ref[4:10].astype(f32), sent_ref[4:10].astype(f32))
+    late_head = sent_ref[10:14].astype(f32)
+    if got_ref.shape[0] > 10:
+        late_head = jnp.where(upper, late_head, got_ref[10:14].astype(f32))
+    extra = extra_state(first_products(early_tail, late_head, taps_ref[:, :, half]), back)
+    other = from_wire(got_ref)
+    lead, enter = pair_at(lead_ref, 0, ALL), pair_at(enter_ref, 0, ALL)
+    enter = pick(upper, plus(enter, times(lead, plus(other, extra))), enter)
+    return upper, other, extra, lead, enter, jnp.where(leads, early_tail, tail_before)
+
+
+def join_kernel(ending_ref, sent_ref, got_ref, power_ref, taps_ref, lead_ref, enter_ref, before_ref,
+                joined_ref, wire_ref, next_lead_ref, next_enter_ref, next_before_ref, *, level, channels):
+    half = halves(channels)[0]
+    upper, other, extra, lead, enter, before = step_of(
+        level, sent_ref, got_ref, power_ref, taps_ref, lead_ref, enter_ref, before_ref[...].astype(f32), half)
+    factor = pair_at(power_ref, SPAN + level, half)
+    mine = pair_at(ending_ref, 0, ALL)
+    early, late = pick(upper, other, mine), pick(upper, mine, other)
+    joined = plus(times(factor, plus(early, extra)), late)
+    put_pair(joined_ref, 0, ALL, joined)
+    put_wire(wire_ref, joined)
+    got, sent = got_ref[...].astype(f32), sent_ref[...].astype(f32)
+    wire_ref[4:10] = jnp.where(upper, sent[4:10], got[4:10]).astype(bf16)
+    wire_ref[10:14] = jnp.where(upper, got[10:14], sent[10:14]).astype(bf16)
+    put_pair(next_lead_ref, 0, ALL, pick(upper, times(lead, factor), lead))
+    put_pair(next_enter_ref, 0, ALL, enter)
+    next_before_ref[...] = before.astype(bf16)
+
+
+def last_kernel(sent_ref, got_ref, power_ref, taps_ref, gain_ref, skip_ref, lead_ref, enter_ref, before_ref,
+                base_ref, fix_ref, head_ref, keep_ref, give_ref, *, level, channels):
+    half = halves(channels)[0]
     odd = lax.axis_index("seq") % 2 == 1
-    far = far_even_ref[...].astype(f32) + far_odd_ref[...].astype(f32)
-    mine = edge_ref[...].astype(f32)
-    mates = mate_edge_ref[...].astype(f32)
-    even_edge, odd_edge = jnp.where(odd, mates, mine), jnp.where(odd, mine, mates)
-    power = pair_at(power_ref, SPAN, cols)
-    back = pair_at(power_ref, BACK, cols)
-    own, mate = pair_at(total_ref, 0, cols), pair_at(mate_ref, 0, cols)
-    even_total, odd_total = pick(odd, mate, own), pick(odd, own, mate)
-    extras, firsts, endings = [], [], []
-    for tail, edge, total in ((far, even_edge, even_total), (even_edge[4:10], odd_edge, odd_total)):
-        first, second = first_products(tail, edge[0:4], taps_ref)
-        extra = times(back, (second * back[0] + first, second * back[1]))
-        extras.append(extra)
-        firsts.append((first, second))
-        endings.append(plus(total, times(power, extra)))
-    joined = plus(times(power, endings[0]), endings[1])
-    put_pair(ending_ref, 0, cols, joined)
-    put_wire(wire_ref, joined)
-    one = (jnp.ones_like(power[0]), jnp.zeros_like(power[0]))
-    put_pair(lead_ref, 0, cols, pick(odd, power, one))
-    put_pair(enter_ref, 0, cols, pick(odd, plus(endings[0], extras[1]), extras[0]))
-    first, second = pick(odd, firsts[1], firsts[0])
-    skip = skip_ref[...]
-    jump = sum(gain_ref[0, pole : pole + 1] * back[0][pole : pole + 1] - gain_ref[1, pole : pole + 1] * back[1][pole : pole + 1]
-               for pole in range(POLES))
-    fix_ref[0:1] = skip * first - jump * second
-    fix_ref[1:2] = skip * second
-    before = jnp.where(odd, even_edge[4:6], far[0:2])
-    fix_ref[2:3] = taps_ref[0, 0:1] * before[0:1] + taps_ref[1, 0:1] * before[1:2]
-    fix_ref[3:4] = taps_ref[0, 0:1] * before[1:2]
-
-
-def join_kernel(ending_ref, got_ref, power_ref, lead_ref, enter_ref,
-                joined_ref, wire_ref, next_lead_ref, next_enter_ref, *, level):
-    upper = (lax.axis_index("seq") >> level) % 2 == 1
-    cols = slice(None)
-    mine = pair_at(ending_ref, 0, cols)
-    other = from_wire(got_ref)
-    factor = pair_at(power_ref, SPAN + level, cols)
-    early, late = pick(upper, other, mine), pick(upper, mine, other)
-    joined = plus(times(factor, early), late)
-    put_pair(joined_ref, 0, cols, joined)
-    put_wire(wire_ref, joined)
-    lead = pair_at(lead_ref, 0, cols)
-    enter = pair_at(enter_ref, 0, cols)
-    put_pair(next_lead_ref, 0, cols, pick(upper, times(lead, factor), lead))
-    put_pair(next_enter_ref, 0, cols, pick(upper, plus(enter, times(lead, other)), enter))
+    _, _, _, _, enter, before = step_of(
+        level, sent_ref, got_ref, power_ref, taps_ref, lead_ref, enter_ref, before_ref[...].astype(f32), half)
+    taps, gain, skip = taps_ref[:, :, half], gain_ref[:, :, half], skip_ref[:, half]
+    power, back = pair_at(power_ref, SPAN, half), pair_at(power_ref, BACK, half)
+    products = first_products(before, head_ref[...].astype(f32), taps)
+    even = [*enter, *fixed_rows(products, before, taps, skip, gain, back)]
+    odds = [*plus(times(power, enter), pair_at(base_ref, 0, ALL)), *(fix_ref[i : i + 1] for i in range(4))]
+    row = 0
+    for a, b in zip(even, odds):
+        keep_ref[row : row + a.shape[0]] = jnp.where(odd, b, a)
+        give_ref[row : row + a.shape[0]] = jnp.where(odd, a, b)
+        row += a.shape[0]
 
 
 def local_kernel(taps_ref, gain_ref, skip_ref, power_ref, scan_ref, prod_ref, proj_ref, after_ref,
@@ -345,17 +398,15 @@
     lax.fori_loop(0, count, body, 0)
 
 
-def gate_kernel(power_ref, got_ref, lead_ref, enter_ref, fix_ref, *rest, level, parts):
+def gate_kernel(power_ref, keep_ref, got_ref, *rest, parts):
     tables = [rest[3 * i : 3 * i + 3] for i in range(len(parts))]
     out_hbm, order_ref, out_ref, gated_ref, state_ref, out_sem = rest[3 * len(parts) :]
     rows, channels = out_ref.shape
     chunk = gated_ref.shape[1]
     count = channels // chunk
-    cols = slice(None)
-    upper = (lax.axis_index("seq") >> level) % 2 == 1
-    state = pair_at(enter_ref, 0, cols)
-    add = times(pair_at(lead_ref, 0, cols), from_wire(got_ref))
-    put_pair(state_ref, 0, cols, pick(upper, plus(state, add), state))
+    own, other = halves(channels)
+    state_ref[:, own] = keep_ref[...]
+    state_ref[:, other] = got_ref[...]
     order_ref[...] = order_matrix(rows, True)
 
     def send(i):
@@ -373,8 +424,8 @@
                 queries = steps_of(query_ref, take)
                 local = steps_of(local_ref, take)
                 for j in range(2):
-                    local[j] = local[j] + jnp.where(first_mask(), wide(fix_ref[j : j + 1, here]), 0.0)
-                    queries[j] = queries[j] + jnp.where(first_mask(), wide(fix_ref[2 + j : 3 + j, here]), 0.0)
+                    local[j] = local[j] + jnp.where(first_mask(), wide(state_ref[4 + j : 5 + j, here]), 0.0)
+                    queries[j] = queries[j] + jnp.where(first_mask(), wide(state_ref[6 + j : 7 + j, here]), 0.0)
                 coefs = []
                 for pole in range(POLES):
                     lam = pole_at(power_ref, LAM, pole, here)
@@ -434,37 +485,33 @@
     arguments = [pole_angles, decay_rates, short_taps, residues, skip_gain[None], projected]
     arguments = [pltpu.with_memory_space_constraint(argument, pltpu.HBM) for argument in arguments]
     projected = arguments[-1]
-    state = ((4, channels), f32)
-    wire = ((4, channels), bf16)
+    half = channels // 2
+    state = ((4, half), f32)
     square = pltpu.VMEM((rows, rows), bf16)
     dma = pltpu.SemaphoreType.DMA
 
-    products, scan, total, edges, tail, powers, taps, gains, skip = kernel_call(
+    products, scan, total, give_total, edge, give_edge, powers, taps, gains, skip = kernel_call(
         states_kernel, "states",
-        [((rows, channels), bf16), ((4, SEGMENTS, channels), f32), state, ((10, channels), bf16),
-         ((6, channels), bf16), ((4 * (SPAN + levels), channels), f32), (short_taps.shape, f32),
-         (residues.shape, f32), ((1, channels), f32)],
-        [square] + [pltpu.VMEM(pole_angles.shape, f32)] * 2 + [pltpu.VMEM((rows, channels), bf16)] * 2
+        [((rows, channels), bf16), ((4, SEGMENTS, channels), f32), state, state, ((10, half), bf16), ((10, half), bf16),
+         ((4 * (SPAN + levels), channels), f32), (short_taps.shape, f32), (residues.shape, f32), ((1, channels), f32)],
+        [pltpu.VMEM((4, channels), f32), pltpu.VMEM((10, channels), bf16), square]
+        + [pltpu.VMEM(pole_angles.shape, f32)] * 2 + [pltpu.VMEM((rows, channels), bf16)] * 2
         + [pltpu.VMEM((2, SUBROWS, channels), bf16), pltpu.VMEM((3, SUBROWS, channels), bf16)]
         + [pltpu.VMEM((rows, chunk), f32)] * 2 + [dma((7,)), dma((2, channels // chunk))],
         arguments, range(6), levels=levels)
 
-    def move(array, pairs):
-        return lax.ppermute(array, "seq", [(a, b) for a, b in pairs if b < devices])
-
     def exchange(array, level):
-        return move(array, [(i, i ^ (1 << level)) for i in range(devices)])
-
-    tails_even = move(tail, [(i, i + 1) for i in range(1, devices, 2)])
-    tails_odd = move(tail, [(i, i + 2) for i in range(1, devices, 2)])
-    mate_edges = exchange(edges, 0)
-    mate_total = exchange(total, 0)
-    ending, sent, lead, enter, fix = kernel_call(
-        merge_kernel, "merge", [state, wire, state, state, state], [],
-        [total, mate_total, edges, mate_edges, tails_even, tails_odd, powers, taps, gains, skip], ())
+        return lax.ppermute(array, "seq", [(i, i ^ (1 << level)) for i in range(devices)])
+
+    mate_edge = exchange(give_edge, 0)
+    mate_total = exchange(give_total, 0)
+    ending, sent, lead, enter, base, fix, head = kernel_call(
+        merge_kernel, "merge", [state, ((14, half), bf16), state, state, state, state, ((4, half), bf16)], [],
+        [total, mate_total, edge, mate_edge, powers, taps, gains, skip], (), channels=channels)
+    before = jnp.zeros((6, half), bf16)
 
     tables = []
-    base = 0
+    start = 0
     for level in range(1, levels):
         got = exchange(sent, level)
         while len(tables) < len(parts) and (len(tables) < level or level == levels - 1):
@@ -473,19 +520,24 @@
             tables.append(kernel_call(
                 local_kernel, "local", [plane, plane, ((4, SEGMENTS, part), f32)],
                 [square, pltpu.VMEM((rows, part), bf16), pltpu.VMEM((rows, chunk), f32), dma((part // chunk,))],
-                [taps, gains, skip, powers, scan, products, projected, ending], (6,), base=base))
-            base += part
+                [taps, gains, skip, powers, scan, products, projected, ending], (6,), base=start))
+            start += part
         if level + 1 < levels:
-            ending, sent, lead, enter = kernel_call(
-                join_kernel, "join", [state, wire, state, state], [], [ending, got, powers, lead, enter], (),
-                level=level)
+            ending, sent, lead, enter, before = kernel_call(
+                join_kernel, "join", [state, ((14, half), bf16), state, state, ((6, half), bf16)], [],
+                [ending, sent, got, powers, taps, lead, enter, before], (), level=level, channels=channels)
+
+    keep, give = kernel_call(
+        last_kernel, "last", [((8, half), f32)] * 2, [],
+        [sent, got, powers, taps, gains, skip, lead, enter, before, base, fix, head], (),
+        level=levels - 1, channels=channels)
+    got = exchange(give, 0)
 
     (out,) = kernel_call(
         gate_kernel, "gate", [((rows, channels), bf16)],
         [square, pltpu.VMEM((rows, channels), bf16), pltpu.VMEM((rows, chunk), bf16),
-         pltpu.VMEM((4, channels), f32), dma((channels // chunk,))],
-        [powers, got, lead, enter, fix, *[array for table in tables for array in table]], (), (0,),
-        level=levels - 1, parts=parts)
+         pltpu.VMEM((8, channels), f32), dma((channels // chunk,))],
+        [powers, keep, got, *[array for table in tables for array in table]], (), (0,), parts=parts)
     return out
 
 

time: 35.4 us -> 32 us (0.904)
  starting transfers between devices: 16.3 us -> 8.17 us
  waiting for transfers between devices: 3.8 us -> 8.56 us
    ppermute x7 -> x6, starting transfers between devices: 16.3 us -> 8.17 us  [exchange(): lax.ppermute(array, 'seq', [(i, i ^ 1 << level) for i in range(devices)])]
    ppermute x7 -> x6, waiting for transfers between devices: 3.8 us -> 8.56 us  [exchange(): lax.ppermute(array, 'seq', [(i, i ^ 1 << level) for i in range(devices)])]
    pallas_call x8 -> x9, Pallas kernels: 15 us -> 15 us  [kernel_call(): pl.pallas_call(bound, in_specs=[spec(i in in_hbm) for i in range(len(oper...]
  transfers between devices with their start and end apart: 7 -> 6, of which waited for: 2 -> 4; matrix products, arithmetic and copies ran while one was open for 0% -> 0% of each run, Pallas kernels for 16% -> 17%
where the time goes in v2:
time: 32 us; the launch traced here: 31.8 us
  Pallas kernels  15 us (47%)
  waiting for transfers between devices  8.56 us (27%)
  starting transfers between devices  8.17 us (26%)
    pallas_call x9, Pallas kernels, kernel_call(): pl.pallas_call(bound, in_specs=[spec(i in in_hbm) for i in range(len(oper...  15 us
    ppermute x6, waiting for transfers between devices, exchange(): lax.ppermute(array, 'seq', [(i, i ^ 1 << level) for i in range(devices)])  8.56 us
    ppermute x6, starting transfers between devices, exchange(): lax.ppermute(array, 'seq', [(i, i ^ 1 << level) for i in range(devices)])  8.17 us
  transfers between devices with their start and end apart: 6, of which 4 were waited for; matrix products, arithmetic and copies ran while one was open for 0% of the time, Pallas kernels for 17%

profile of v2, /device:TPU:0, one launch (start us, length us, event | category | flops | bytes accessed | tf_op | source)
XLA Modules:
  0.0 31.8 jit_solution(8420658827329175973)
XLA Ops:
  0.0 5.3 %states.1 = (bf16[128,4096]{1,0:T(8,128)(2,1)S(1)}, f32[4,8,4096]{2,1,0:T(8,128)S(1)}, f32[4,2048]{1,0:T(4,128)S(1)}, f32[4,2048]{1,0:T(4,128)S(1)}, bf16[10,204...) custom-call(f32[2,4096]{1,0:T(2,128)} %refs_0_.1, ...), custom_call_target="tpu_custom_call" | custom-call | tf_op jit(solution)/shard_map/states/pallas_call | solution.py:468
  5.3 0.6 %collective-permute-start.1 = (bf16[10,2048]{1,0:T(8,128)(2,1)S(1)}, bf16[10,2048]{1,0:T(8,128)(2,1)S(1)}, u32[]{:S(2)}, u32[]{:S(2)}) collective-permute-start(bf16[10,2048]{1,0:T(8,128)(2,1)S(1)} %get-tuple-element.47), channel_id=1, source_target_pairs={{0,1},{1,0},{2,3},{3,2},{4,5},{5,4},{6,7},{7,6},{8,9},{9,8},{10,11... | collective-permute-start | bytes 122888 | tf_op jit(solution)/shard_map/ppermute | solution.py:504
  5.8 0.1 collective-permute-start
  5.9 1.1 %collective-permute-done.refs_1_ = f32[4,2048]{1,0:T(4,128)S(1)} collective-permute-done((f32[4,2048]{1,0:T(4,128)S(1)}, f32[4,2048]{1,0:T(4,128)S(1)}, u32[]{:S(2)}, u32[]{:S(2)}) %collective-permute-start) | collective-permute-done | bytes 32800 | tf_op jit(solution)/shard_map/ppermute | solution.py:504
  7.0 0.0 collective-permute-done.1.refs_3_
  7.0 0.3 %merge.1 = (f32[4,2048]{1,0:T(4,128)S(1)}, bf16[14,2048]{1,0:T(8,128)(2,1)S(1)}, f32[4,2048]{1,0:T(4,128)S(1)}, f32[4,2048]{1,0:T(4,128)S(1)}, f32[4,2048]{1,0:T...) custom-call(f32[4,2048]{1,0:T(4,128)S(1)} %get-tuple-element.44.refs_0_, ...), custom_call_target="tpu_custom_call" | custom-call | tf_op jit(solution)/shard_map/merge/pallas_call | solution.py:468
  7.4 2.7 %collective-permute-start.2 = (bf16[14,2048]{1,0:T(8,128)(2,1)S(1)}, bf16[14,2048]{1,0:T(8,128)(2,1)S(1)}, u32[]{:S(2)}, u32[]{:S(2)}) collective-permute-start(bf16[14,2048]{1,0:T(8,128)(2,1)S(1)} %get-tuple-element.52.refs_1_), channel_id=1, source_target_pairs={{0,2},{1,3},{2,0},{3,1},{4,6},{5,7},{6,4},{7,5},{8,10},{9,11},{10,... | collective-permute-start | bytes 172040 | tf_op jit(solution)/shard_map/ppermute | solution.py:504
  10.1 2.6 %collective-permute-done.2.refs_2_ = bf16[14,2048]{1,0:T(8,128)(2,1)S(1)} collective-permute-done((bf16[14,2048]{1,0:T(8,128)(2,1)S(1)}, bf16[14,2048]{1,0:T(8,128)(2,1)S(1)}, u32[]{:S(2)}, u32[]{:S(2)}) %collective-permute-start.2) | collective-permute-done | bytes 57376 | tf_op jit(solution)/shard_map/ppermute | solution.py:504
  12.7 0.3 join.2
  13.0 1.9 %collective-permute-start.3 = (bf16[14,2048]{1,0:T(8,128)(2,1)S(1)}, bf16[14,2048]{1,0:T(8,128)(2,1)S(1)}, u32[]{:S(2)}, u32[]{:S(2)}) collective-permute-start(bf16[14,2048]{1,0:T(8,128)(2,1)S(1)} %get-tuple-element.56.refs_1_), channel_id=1, source_target_pairs={{0,4},{1,5},{2,6},{3,7},{4,0},{5,1},{6,2},{7,3},{8,12},{9,13},{10,... | collective-permute-start | bytes 172040 | tf_op jit(solution)/shard_map/ppermute | solution.py:504
  14.9 2.5 %collective-permute-done.3.refs_2_ = bf16[14,2048]{1,0:T(8,128)(2,1)S(1)} collective-permute-done((bf16[14,2048]{1,0:T(8,128)(2,1)S(1)}, bf16[14,2048]{1,0:T(8,128)(2,1)S(1)}, u32[]{:S(2)}, u32[]{:S(2)}) %collective-permute-start.3) | collective-permute-done | bytes 57376 | tf_op jit(solution)/shard_map/ppermute | solution.py:504
  17.4 0.3 join.3
  17.7 2.9 %collective-permute-start.4 = (bf16[14,2048]{1,0:T(8,128)(2,1)S(1)}, bf16[14,2048]{1,0:T(8,128)(2,1)S(1)}, u32[]{:S(2)}, u32[]{:S(2)}) collective-permute-start(bf16[14,2048]{1,0:T(8,128)(2,1)S(1)} %get-tuple-element.60.refs_0_), channel_id=1, source_target_pairs={{0,8},{1,9},{2,10},{3,11},{4,12},{5,13},{6,14},{7,15},{8,0},{9,1},... | collective-permute-start | bytes 172040 | tf_op jit(solution)/shard_map/ppermute | solution.py:504
  20.5 2.4 %collective-permute-done.4.refs_1_ = bf16[14,2048]{1,0:T(8,128)(2,1)S(1)} collective-permute-done((bf16[14,2048]{1,0:T(8,128)(2,1)S(1)}, bf16[14,2048]{1,0:T(8,128)(2,1)S(1)}, u32[]{:S(2)}, u32[]{:S(2)}) %collective-permute-start.4) | collective-permute-done | bytes 57376 | tf_op jit(solution)/shard_map/ppermute | solution.py:504
  22.9 0.3 last.1
  23.2 0.1 collective-permute-start.5
  23.3 1.6 %local.3 = (f32[128,1024]{1,0:T(8,128)S(1)}, f32[128,1024]{1,0:T(8,128)S(1)}, f32[4,8,1024]{2,1,0:T(8,128)S(1)}) custom-call(f32[3,3,4096]{2,1,0:T(4,128)S(1)} %get-tuple-element.48.refs_5_.refs_4_.refs_3_.refs_0_, f32[2,2,4096]{2,1,0:T(2,128)S(1)} %get-tuple-element.49.refs_6_.refs_4_.refs_1_, f32[1,4096]{1,0:T(1,128)S(1)} %get-tuple-element.50.refs_7_.refs_5_.refs_2_, ...), custom_call_target="tpu_custom_call" | custom-call | tf_op jit(solution)/shard_map/local/pallas_call | solution.py:468
  24.9 1.6 %local.4 = (f32[128,1024]{1,0:T(8,128)S(1)}, f32[128,1024]{1,0:T(8,128)S(1)}, f32[4,8,1024]{2,1,0:T(8,128)S(1)}) custom-call(f32[3,3,4096]{2,1,0:T(4,128)S(1)} %get-tuple-element.48.refs_5_.refs_4_.refs_3_.refs_0_, f32[2,2,4096]{2,1,0:T(2,128)S(1)} %get-tuple-element.49.refs_6_.refs_4_.refs_1_, f32[1,4096]{1,0:T(1,128)S(1)} %get-tuple-element.50.refs_7_.refs_5_.refs_2_, ...), custom_call_target="tpu_custom_call" | custom-call | tf_op jit(solution)/shard_map/local/pallas_call | solution.py:468
  26.5 2.3 %local.5 = (f32[128,2048]{1,0:T(8,128)S(1)}, f32[128,2048]{1,0:T(8,128)S(1)}, f32[4,8,2048]{2,1,0:T(8,128)S(1)}) custom-call(f32[3,3,4096]{2,1,0:T(4,128)S(1)} %get-tuple-element.48.refs_5_.refs_4_.refs_3_.refs_0_, f32[2,2,4096]{2,1,0:T(2,128)S(1)} %get-tuple-element.49.refs_6_.refs_4_.refs_1_, f32[1,4096]{1,0:T(1,128)S(1)} %get-tuple-element.50.refs_7_.refs_5_.refs_2_, ...), custom_call_target="tpu_custom_call" | custom-call | tf_op jit(solution)/shard_map/local/pallas_call | solution.py:468
  28.8 0.0 collective-permute-done.5.refs_2_
  28.9 3.0 %gate.1 = bf16[128,4096]{1,0:T(8,128)(2,1)} custom-call(f32[36,4096]{1,0:T(8,128)S(1)} %get-tuple-element.43.refs_4_.refs_3_.refs_2_.refs_0_, f32[8,2048]{1,0:T(8,128)S(1)} %get-tuple-element.67.refs_1_, f32[8,2048]{1,0:T(8,128)S(1)} %collective-permute-done.5.refs_2_, f32[128,1024]{1,0:T(8,128)S(1)} %get-tuple-element.71.refs_3_, ...), custom_call_target="tpu_custom_call" | custom-call | tf_op jit(solution)/shard_map/gate/pallas_call | solution.py:468
  (1 shorter events, 0.0 us)
Async XLA Ops:
  5.3 1.8 %collective-permute-start.1 = (bf16[10,2048]{1,0:T(8,128)(2,1)S(1)}, bf16[10,2048]{1,0:T(8,128)(2,1)S(1)}, u32[]{:S(2)}, u32[]{:S(2)}) collective-permute-start(bf16[10,2048]{1,0:T(8,128)(2,1)S(1)} %get-tuple-element.47), channel_id=1, source_target_pairs={{0,1},{1,0},{2,3},{3,2},{4,5},{5,4},{6,7},{7,6},{8,9},{9,8},{10,11... | collective-permute-start | bytes 122888 | tf_op jit(solution)/shard_map/ppermute | solution.py:504
  5.8 1.2 %collective-permute-start = (f32[4,2048]{1,0:T(4,128)S(1)}, f32[4,2048]{1,0:T(4,128)S(1)}, u32[]{:S(2)}, u32[]{:S(2)}) collective-permute-start(f32[4,2048]{1,0:T(4,128)S(1)} %get-tuple-element.45), channel_id=1, source_target_pairs={{0,1},{1,0},{2,3},{3,2},{4,5},{5,4},{6,7},{7,6},{8,9},{9,8},{10,11... | collective-permute-start | bytes 98312 | tf_op jit(solution)/shard_map/ppermute | solution.py:504
  7.4 5.3 %collective-permute-start.2 = (bf16[14,2048]{1,0:T(8,128)(2,1)S(1)}, bf16[14,2048]{1,0:T(8,128)(2,1)S(1)}, u32[]{:S(2)}, u32[]{:S(2)}) collective-permute-start(bf16[14,2048]{1,0:T(8,128)(2,1)S(1)} %get-tuple-element.52.refs_1_), channel_id=1, source_target_pairs={{0,2},{1,3},{2,0},{3,1},{4,6},{5,7},{6,4},{7,5},{8,10},{9,11},{10,... | collective-permute-start | bytes 172040 | tf_op jit(solution)/shard_map/ppermute | solution.py:504
  13.0 4.3 %collective-permute-start.3 = (bf16[14,2048]{1,0:T(8,128)(2,1)S(1)}, bf16[14,2048]{1,0:T(8,128)(2,1)S(1)}, u32[]{:S(2)}, u32[]{:S(2)}) collective-permute-start(bf16[14,2048]{1,0:T(8,128)(2,1)S(1)} %get-tuple-element.56.refs_1_), channel_id=1, source_target_pairs={{0,4},{1,5},{2,6},{3,7},{4,0},{5,1},{6,2},{7,3},{8,12},{9,13},{10,... | collective-permute-start | bytes 172040 | tf_op jit(solution)/shard_map/ppermute | solution.py:504
  17.7 5.2 %collective-permute-start.4 = (bf16[14,2048]{1,0:T(8,128)(2,1)S(1)}, bf16[14,2048]{1,0:T(8,128)(2,1)S(1)}, u32[]{:S(2)}, u32[]{:S(2)}) collective-permute-start(bf16[14,2048]{1,0:T(8,128)(2,1)S(1)} %get-tuple-element.60.refs_0_), channel_id=1, source_target_pairs={{0,8},{1,9},{2,10},{3,11},{4,12},{5,13},{6,14},{7,15},{8,0},{9,1},... | collective-permute-start | bytes 172040 | tf_op jit(solution)/shard_map/ppermute | solution.py:504
  23.2 5.6 %collective-permute-start.5 = (f32[8,2048]{1,0:T(8,128)S(1)}, f32[8,2048]{1,0:T(8,128)S(1)}, u32[]{:S(2)}, u32[]{:S(2)}) collective-permute-start(f32[8,2048]{1,0:T(8,128)S(1)} %get-tuple-element.68), channel_id=1, source_target_pairs={{0,1},{1,0},{2,3},{3,2},{4,5},{5,4},{6,7},{7,6},{8,9},{9,8},{10,11... | collective-permute-start | bytes 196616 | tf_op jit(solution)/shard_map/ppermute | solution.py:504

commit v3 on v2

--- a/solution.py
+++ b/solution.py
@@ -10,7 +10,7 @@
 CHUNK = 512
 POLES = 2
 SUBROWS = 16
-PARTS = (1, 1, 2)
+PARTS = (3, 3, 2)
 f32 = jnp.float32
 bf16 = jnp.bfloat16
 
@@ -115,7 +115,7 @@
 
 def states_kernel(angle_hbm, decay_hbm, taps_hbm, gain_hbm, skip_hbm, proj_ref,
                   prod_ref, scan_ref, keep_total, give_total, keep_edge, give_edge, power_ref, taps_ref, gain_ref, skip_ref,
-                  total_ref, edge_ref, order_ref, angle_ref, decay_ref, k_ref, v_ref, top_ref, end_ref, ks_ref, vs_ref,
+                  q_ref, total_ref, edge_ref, order_ref, angle_ref, decay_ref, k_ref, v_ref, top_ref, end_ref, ks_ref, vs_ref,
                   small_sem, in_sem, *, levels):
     rows, channels = k_ref.shape
     chunk = ks_ref.shape[1]
@@ -126,7 +126,7 @@
         for i, (source, target) in enumerate([
             (angle_hbm, angle_ref), (decay_hbm, decay_ref), (taps_hbm, taps_ref), (gain_hbm, gain_ref),
             (skip_hbm, skip_ref), (proj_ref.at[pl.ds(1, 2), pl.ds(0, SUBROWS)], top_ref),
-            (proj_ref.at[:, pl.ds(last, SUBROWS)], end_ref)])
+            (proj_ref.at[:, pl.ds(last, SUBROWS)], end_ref), (proj_ref.at[0], q_ref)])
     ]
 
     def fetch(i, which, ref):
@@ -293,7 +293,7 @@
     return upper, other, extra, lead, enter, jnp.where(leads, early_tail, tail_before)
 
 
-def join_kernel(ending_ref, sent_ref, got_ref, power_ref, taps_ref, lead_ref, enter_ref, before_ref,
+def join_kernel(ending_ref, sent_ref, got_ref, power_ref, taps_ref, lead_ref, enter_ref, before_ref, after_ref,
                 joined_ref, wire_ref, next_lead_ref, next_enter_ref, next_before_ref, *, level, channels):
     half = halves(channels)[0]
     upper, other, extra, lead, enter, before = step_of(
@@ -313,7 +313,7 @@
 
 
 def last_kernel(sent_ref, got_ref, power_ref, taps_ref, gain_ref, skip_ref, lead_ref, enter_ref, before_ref,
-                base_ref, fix_ref, head_ref, keep_ref, give_ref, *, level, channels):
+                base_ref, fix_ref, head_ref, after_ref, keep_ref, give_ref, *, level, channels):
     half = halves(channels)[0]
     odd = lax.axis_index("seq") % 2 == 1
     _, _, _, _, enter, before = step_of(
@@ -330,23 +330,14 @@
         row += a.shape[0]
 
 
-def local_kernel(taps_ref, gain_ref, skip_ref, power_ref, scan_ref, prod_ref, proj_ref, after_ref,
-                 query_ref, local_ref, enter_ref, order_ref, q_ref, qs_ref, in_sem, *, base):
-    rows, channels = q_ref.shape
+def local_kernel(taps_ref, gain_ref, skip_ref, power_ref, scan_ref, prod_ref, q_ref, after_ref,
+                 query_ref, local_ref, enter_ref, order_ref, qs_ref, *, base):
+    rows, channels = query_ref.shape
     chunk = qs_ref.shape[1]
-    count = channels // chunk
-
-    def fetch(i):
-        return pltpu.make_async_copy(
-            proj_ref.at[0, :, span(base + i * chunk, chunk)], q_ref.at[:, span(i * chunk, chunk)], in_sem.at[i])
-
-    for i in range(count):
-        fetch(i).start()
     order_ref[...] = order_matrix(rows, False)
 
     def body(i, _):
-        fetch(i).wait()
-        qs_ref[...] = jnp.dot(order_ref[...], q_ref[:, span(i * chunk, chunk)], preferred_element_type=f32)
+        qs_ref[...] = jnp.dot(order_ref[...], q_ref[:, span(base + i * chunk, chunk)], preferred_element_type=f32)
 
         def column(inner, outer):
             cols = slice(inner, inner + WIDTH)
@@ -395,7 +386,7 @@
         loop_columns(i, chunk, column)
         return 0
 
-    lax.fori_loop(0, count, body, 0)
+    lax.fori_loop(0, channels // chunk, body, 0)
 
 
 def gate_kernel(power_ref, keep_ref, got_ref, *rest, parts):
@@ -484,20 +475,19 @@
     parts = [channels // sum(PARTS) * share for share in PARTS]
     arguments = [pole_angles, decay_rates, short_taps, residues, skip_gain[None], projected]
     arguments = [pltpu.with_memory_space_constraint(argument, pltpu.HBM) for argument in arguments]
-    projected = arguments[-1]
     half = channels // 2
     state = ((4, half), f32)
     square = pltpu.VMEM((rows, rows), bf16)
     dma = pltpu.SemaphoreType.DMA
 
-    products, scan, total, give_total, edge, give_edge, powers, taps, gains, skip = kernel_call(
+    products, scan, total, give_total, edge, give_edge, powers, taps, gains, skip, query_rows = kernel_call(
         states_kernel, "states",
         [((rows, channels), bf16), ((4, SEGMENTS, channels), f32), state, state, ((10, half), bf16), ((10, half), bf16),
-         ((4 * (SPAN + levels), channels), f32), (short_taps.shape, f32), (residues.shape, f32), ((1, channels), f32)],
+         ((4 * (SPAN + levels), channels), f32), (short_taps.shape, f32), (residues.shape, f32), ((1, channels), f32), ((rows, channels), bf16)],
         [pltpu.VMEM((4, channels), f32), pltpu.VMEM((10, channels), bf16), square]
         + [pltpu.VMEM(pole_angles.shape, f32)] * 2 + [pltpu.VMEM((rows, channels), bf16)] * 2
         + [pltpu.VMEM((2, SUBROWS, channels), bf16), pltpu.VMEM((3, SUBROWS, channels), bf16)]
-        + [pltpu.VMEM((rows, chunk), f32)] * 2 + [dma((7,)), dma((2, channels // chunk))],
+        + [pltpu.VMEM((rows, chunk), f32)] * 2 + [dma((8,)), dma((2, channels // chunk))],
         arguments, range(6), levels=levels)
 
     def exchange(array, level):
@@ -519,17 +509,17 @@
             plane = ((rows, part), f32)
             tables.append(kernel_call(
                 local_kernel, "local", [plane, plane, ((4, SEGMENTS, part), f32)],
-                [square, pltpu.VMEM((rows, part), bf16), pltpu.VMEM((rows, chunk), f32), dma((part // chunk,))],
-                [taps, gains, skip, powers, scan, products, projected, ending], (6,), base=start))
+                [square, pltpu.VMEM((rows, chunk), f32)],
+                [taps, gains, skip, powers, scan, products, query_rows, ending], (), base=start))
             start += part
         if level + 1 < levels:
             ending, sent, lead, enter, before = kernel_call(
                 join_kernel, "join", [state, ((14, half), bf16), state, state, ((6, half), bf16)], [],
-                [ending, sent, got, powers, taps, lead, enter, before], (), level=level, channels=channels)
+                [ending, sent, got, powers, taps, lead, enter, before, tables[-1][2]], (8,), level=level, channels=channels)
 
     keep, give = kernel_call(
         last_kernel, "last", [((8, half), f32)] * 2, [],
-        [sent, got, powers, taps, gains, skip, lead, enter, before, base, fix, head], (),
+        [sent, got, powers, taps, gains, skip, lead, enter, before, base, fix, head, tables[-1][2]], (12,),
         level=levels - 1, channels=channels)
     got = exchange(give, 0)
 

time: 32 us -> 27.6 us (0.86)
  Pallas kernels: 15 us -> 12.2 us
  waiting for transfers between devices: 8.56 us -> 7.04 us
    pallas_call x9, Pallas kernels: 15 us -> 12.2 us  [kernel_call(): pl.pallas_call(bound, in_specs=[spec(i in in_hbm) for i in range(len(oper...]
    ppermute x6, waiting for transfers between devices: 8.56 us -> 7.04 us  [exchange(): lax.ppermute(array, 'seq', [(i, i ^ 1 << level) for i in range(devices)])]
  transfers between devices with their start and end apart: 6 -> 6, of which waited for: 4 -> 5; matrix products, arithmetic and copies ran while one was open for 0% -> 0% of each run, Pallas kernels for 17% -> 10%
where the time goes in v3:
time: 27.6 us; the launch traced here: 27.4 us
  Pallas kernels  12.2 us (44%)
  starting transfers between devices  8.16 us (30%)
  waiting for transfers between devices  7.04 us (26%)
    pallas_call x9, Pallas kernels, kernel_call(): pl.pallas_call(bound, in_specs=[spec(i in in_hbm) for i in range(len(oper...  12.2 us
    ppermute x6, starting transfers between devices, exchange(): lax.ppermute(array, 'seq', [(i, i ^ 1 << level) for i in range(devices)])  8.16 us
    ppermute x6, waiting for transfers between devices, exchange(): lax.ppermute(array, 'seq', [(i, i ^ 1 << level) for i in range(devices)])  7.04 us
  transfers between devices with their start and end apart: 6, of which 5 were waited for; matrix products, arithmetic and copies ran while one was open for 0% of the time, Pallas kernels for 10%

profile of v3, /device:TPU:0, one launch (start us, length us, event | category | flops | bytes accessed | tf_op | source)
XLA Modules:
  0.0 27.4 jit_solution(9206145273089183160)
XLA Ops:
  0.0 5.2 %states.1 = (bf16[128,4096]{1,0:T(8,128)(2,1)S(1)}, f32[4,8,4096]{2,1,0:T(8,128)S(1)}, f32[4,2048]{1,0:T(4,128)S(1)}, f32[4,2048]{1,0:T(4,128)S(1)}, bf16[10,204...) custom-call(f32[2,4096]{1,0:T(2,128)} %refs_0_.1, ...), custom_call_target="tpu_custom_call" | custom-call | tf_op jit(solution)/shard_map/states/pallas_call | solution.py:459
  5.3 0.6 %collective-permute-start.1 = (bf16[10,2048]{1,0:T(8,128)(2,1)S(1)}, bf16[10,2048]{1,0:T(8,128)(2,1)S(1)}, u32[]{:S(2)}, u32[]{:S(2)}) collective-permute-start(bf16[10,2048]{1,0:T(8,128)(2,1)S(1)} %get-tuple-element.48), channel_id=1, source_target_pairs={{0,1},{1,0},{2,3},{3,2},{4,5},{5,4},{6,7},{7,6},{8,9},{9,8},{10,11... | collective-permute-start | bytes 122888 | tf_op jit(solution)/shard_map/ppermute | solution.py:494
  5.8 0.1 collective-permute-start
  5.9 1.1 %collective-permute-done.refs_1_ = f32[4,2048]{1,0:T(4,128)S(1)} collective-permute-done((f32[4,2048]{1,0:T(4,128)S(1)}, f32[4,2048]{1,0:T(4,128)S(1)}, u32[]{:S(2)}, u32[]{:S(2)}) %collective-permute-start) | collective-permute-done | bytes 32800 | tf_op jit(solution)/shard_map/ppermute | solution.py:494
  7.0 0.0 collective-permute-done.1.refs_3_
  7.0 0.3 %merge.1 = (f32[4,2048]{1,0:T(4,128)S(1)}, bf16[14,2048]{1,0:T(8,128)(2,1)S(1)}, f32[4,2048]{1,0:T(4,128)S(1)}, f32[4,2048]{1,0:T(4,128)S(1)}, f32[4,2048]{1,0:T...) custom-call(f32[4,2048]{1,0:T(4,128)S(1)} %get-tuple-element.45.refs_0_, ...), custom_call_target="tpu_custom_call" | custom-call | tf_op jit(solution)/shard_map/merge/pallas_call | solution.py:459
  7.3 2.7 %collective-permute-start.2 = (bf16[14,2048]{1,0:T(8,128)(2,1)S(1)}, bf16[14,2048]{1,0:T(8,128)(2,1)S(1)}, u32[]{:S(2)}, u32[]{:S(2)}) collective-permute-start(bf16[14,2048]{1,0:T(8,128)(2,1)S(1)} %get-tuple-element.53.refs_1_), channel_id=1, source_target_pairs={{0,2},{1,3},{2,0},{3,1},{4,6},{5,7},{6,4},{7,5},{8,10},{9,11},{10,... | collective-permute-start | bytes 172040 | tf_op jit(solution)/shard_map/ppermute | solution.py:494
  10.1 1.0 %local.3 = (f32[128,1536]{1,0:T(8,128)S(1)}, f32[128,1536]{1,0:T(8,128)S(1)}, f32[4,8,1536]{2,1,0:T(8,128)S(1)}) custom-call(f32[3,3,4096]{2,1,0:T(4,128)S(1)} %get-tuple-element.49.refs_5_.refs_0_.refs_4_.refs_3_, f32[2,2,4096]{2,1,0:T(2,128)S(1)} %get-tuple-element.50.refs_6_.refs_1_.refs_4_, f32[1,4096]{1,0:T(1,128)S(1)} %get-tuple-element.51.refs_7_.refs_2_.refs_5_, ...), custom_call_target="tpu_custom_call" | custom-call | tf_op jit(solution)/shard_map/local/pallas_call | solution.py:459
  11.1 1.6 %collective-permute-done.2.refs_2_ = bf16[14,2048]{1,0:T(8,128)(2,1)S(1)} collective-permute-done((bf16[14,2048]{1,0:T(8,128)(2,1)S(1)}, bf16[14,2048]{1,0:T(8,128)(2,1)S(1)}, u32[]{:S(2)}, u32[]{:S(2)}) %collective-permute-start.2) | collective-permute-done | bytes 57376 | tf_op jit(solution)/shard_map/ppermute | solution.py:494
  12.7 0.3 %join.2 = (f32[4,2048]{1,0:T(4,128)S(1)}, bf16[14,2048]{1,0:T(8,128)(2,1)S(1)}, f32[4,2048]{1,0:T(4,128)S(1)}, f32[4,2048]{1,0:T(4,128)S(1)}, bf16[6,2048]{1,0:T(8,128)(2,1)S(1)}) custom-call(f32[4,2048]{1,0:T(4,128)S(1)} %get-tuple-element.52.refs_7_.refs_0_, bf16[14,2048]{1,0:T(8,128)(2,1)S(1)} %get-tuple-element.53.refs_1_, ...), custom_call_target="tpu_custom_call" | custom-call | tf_op jit(solution)/shard_map/join/pallas_call | solution.py:459
  13.0 1.9 %collective-permute-start.3 = (bf16[14,2048]{1,0:T(8,128)(2,1)S(1)}, bf16[14,2048]{1,0:T(8,128)(2,1)S(1)}, u32[]{:S(2)}, u32[]{:S(2)}) collective-permute-start(bf16[14,2048]{1,0:T(8,128)(2,1)S(1)} %get-tuple-element.61.refs_1_), channel_id=1, source_target_pairs={{0,4},{1,5},{2,6},{3,7},{4,0},{5,1},{6,2},{7,3},{8,12},{9,13},{10,... | collective-permute-start | bytes 172040 | tf_op jit(solution)/shard_map/ppermute | solution.py:494
  14.8 1.0 %local.4 = (f32[128,1536]{1,0:T(8,128)S(1)}, f32[128,1536]{1,0:T(8,128)S(1)}, f32[4,8,1536]{2,1,0:T(8,128)S(1)}) custom-call(f32[3,3,4096]{2,1,0:T(4,128)S(1)} %get-tuple-element.49.refs_5_.refs_0_.refs_4_.refs_3_, f32[2,2,4096]{2,1,0:T(2,128)S(1)} %get-tuple-element.50.refs_6_.refs_1_.refs_4_, f32[1,4096]{1,0:T(1,128)S(1)} %get-tuple-element.51.refs_7_.refs_2_.refs_5_, ...), custom_call_target="tpu_custom_call" | custom-call | tf_op jit(solution)/shard_map/local/pallas_call | solution.py:459
  15.9 1.5 %collective-permute-done.3.refs_2_ = bf16[14,2048]{1,0:T(8,128)(2,1)S(1)} collective-permute-done((bf16[14,2048]{1,0:T(8,128)(2,1)S(1)}, bf16[14,2048]{1,0:T(8,128)(2,1)S(1)}, u32[]{:S(2)}, u32[]{:S(2)}) %collective-permute-start.3) | collective-permute-done | bytes 57376 | tf_op jit(solution)/shard_map/ppermute | solution.py:494
  17.3 0.3 %join.3 = (f32[4,2048]{1,0:T(4,128)S(1)}, bf16[14,2048]{1,0:T(8,128)(2,1)S(1)}, f32[4,2048]{1,0:T(4,128)S(1)}, f32[4,2048]{1,0:T(4,128)S(1)}, bf16[6,2048]{1,0:T(8,128)(2,1)S(1)}) custom-call(f32[4,2048]{1,0:T(4,128)S(1)} %get-tuple-element.60.refs_7_.refs_0_, bf16[14,2048]{1,0:T(8,128)(2,1)S(1)} %get-tuple-element.61.refs_1_, ...), custom_call_target="tpu_custom_call" | custom-call | tf_op jit(solution)/shard_map/join/pallas_call | solution.py:459
  17.6 2.9 %collective-permute-start.4 = (bf16[14,2048]{1,0:T(8,128)(2,1)S(1)}, bf16[14,2048]{1,0:T(8,128)(2,1)S(1)}, u32[]{:S(2)}, u32[]{:S(2)}) collective-permute-start(bf16[14,2048]{1,0:T(8,128)(2,1)S(1)} %get-tuple-element.66.refs_0_), channel_id=1, source_target_pairs={{0,8},{1,9},{2,10},{3,11},{4,12},{5,13},{6,14},{7,15},{8,0},{9,1},... | collective-permute-start | bytes 172040 | tf_op jit(solution)/shard_map/ppermute | solution.py:494
  20.5 0.7 %local.5 = (f32[128,1024]{1,0:T(8,128)S(1)}, f32[128,1024]{1,0:T(8,128)S(1)}, f32[4,8,1024]{2,1,0:T(8,128)S(1)}) custom-call(f32[3,3,4096]{2,1,0:T(4,128)S(1)} %get-tuple-element.49.refs_5_.refs_0_.refs_4_.refs_3_, f32[2,2,4096]{2,1,0:T(2,128)S(1)} %get-tuple-element.50.refs_6_.refs_1_.refs_4_, f32[1,4096]{1,0:T(1,128)S(1)} %get-tuple-element.51.refs_7_.refs_2_.refs_5_, ...), custom_call_target="tpu_custom_call" | custom-call | tf_op jit(solution)/shard_map/local/pallas_call | solution.py:459
  21.2 1.7 %collective-permute-done.4.refs_1_ = bf16[14,2048]{1,0:T(8,128)(2,1)S(1)} collective-permute-done((bf16[14,2048]{1,0:T(8,128)(2,1)S(1)}, bf16[14,2048]{1,0:T(8,128)(2,1)S(1)}, u32[]{:S(2)}, u32[]{:S(2)}) %collective-permute-start.4) | collective-permute-done | bytes 57376 | tf_op jit(solution)/shard_map/ppermute | solution.py:494
  22.9 0.3 %last.1 = (f32[8,2048]{1,0:T(8,128)S(1)}, f32[8,2048]{1,0:T(8,128)S(1)}) custom-call(bf16[14,2048]{1,0:T(8,128)(2,1)S(1)} %get-tuple-element.66.refs_0_, bf16[14,2048]{1,0:T(8,128)(2,1)S(1)} %collective-permute-done.4.refs_1_, f32[36,4096]{1,0:T(8,128)S(1)} %get-tuple-element.44.refs_4_.refs_3_.refs_2_.refs_0_, ...), custom_call_target="tpu_custom_call" | custom-call | tf_op jit(solution)/shard_map/last/pallas_call | solution.py:459
  23.2 0.1 collective-permute-start.5
  23.2 1.2 %collective-permute-done.5.refs_2_ = f32[8,2048]{1,0:T(8,128)S(1)} collective-permute-done((f32[8,2048]{1,0:T(8,128)S(1)}, f32[8,2048]{1,0:T(8,128)S(1)}, u32[]{:S(2)}, u32[]{:S(2)}) %collective-permute-start.5) | collective-permute-done | bytes 65568 | tf_op jit(solution)/shard_map/ppermute | solution.py:494
  24.5 3.0 %gate.1 = bf16[128,4096]{1,0:T(8,128)(2,1)} custom-call(f32[36,4096]{1,0:T(8,128)S(1)} %get-tuple-element.44.refs_4_.refs_3_.refs_2_.refs_0_, f32[8,2048]{1,0:T(8,128)S(1)} %get-tuple-element.75.refs_1_, f32[8,2048]{1,0:T(8,128)S(1)} %collective-permute-done.5.refs_2_, f32[128,1536]{1,0:T(8,128)S(1)} %get-tuple-element.77.refs_3_, ...), custom_call_target="tpu_custom_call" | custom-call | tf_op jit(solution)/shard_map/gate/pallas_call | solution.py:459
  (1 shorter events, 0.0 us)
Async XLA Ops:
  5.3 1.8 %collective-permute-start.1 = (bf16[10,2048]{1,0:T(8,128)(2,1)S(1)}, bf16[10,2048]{1,0:T(8,128)(2,1)S(1)}, u32[]{:S(2)}, u32[]{:S(2)}) collective-permute-start(bf16[10,2048]{1,0:T(8,128)(2,1)S(1)} %get-tuple-element.48), channel_id=1, source_target_pairs={{0,1},{1,0},{2,3},{3,2},{4,5},{5,4},{6,7},{7,6},{8,9},{9,8},{10,11... | collective-permute-start | bytes 122888 | tf_op jit(solution)/shard_map/ppermute | solution.py:494
  5.8 1.2 %collective-permute-start = (f32[4,2048]{1,0:T(4,128)S(1)}, f32[4,2048]{1,0:T(4,128)S(1)}, u32[]{:S(2)}, u32[]{:S(2)}) collective-permute-start(f32[4,2048]{1,0:T(4,128)S(1)} %get-tuple-element.46), channel_id=1, source_target_pairs={{0,1},{1,0},{2,3},{3,2},{4,5},{5,4},{6,7},{7,6},{8,9},{9,8},{10,11... | collective-permute-start | bytes 98312 | tf_op jit(solution)/shard_map/ppermute | solution.py:494
  7.3 5.3 %collective-permute-start.2 = (bf16[14,2048]{1,0:T(8,128)(2,1)S(1)}, bf16[14,2048]{1,0:T(8,128)(2,1)S(1)}, u32[]{:S(2)}, u32[]{:S(2)}) collective-permute-start(bf16[14,2048]{1,0:T(8,128)(2,1)S(1)} %get-tuple-element.53.refs_1_), channel_id=1, source_target_pairs={{0,2},{1,3},{2,0},{3,1},{4,6},{5,7},{6,4},{7,5},{8,10},{9,11},{10,... | collective-permute-start | bytes 172040 | tf_op jit(solution)/shard_map/ppermute | solution.py:494
  13.0 4.3 %collective-permute-start.3 = (bf16[14,2048]{1,0:T(8,128)(2,1)S(1)}, bf16[14,2048]{1,0:T(8,128)(2,1)S(1)}, u32[]{:S(2)}, u32[]{:S(2)}) collective-permute-start(bf16[14,2048]{1,0:T(8,128)(2,1)S(1)} %get-tuple-element.61.refs_1_), channel_id=1, source_target_pairs={{0,4},{1,5},{2,6},{3,7},{4,0},{5,1},{6,2},{7,3},{8,12},{9,13},{10,... | collective-permute-start | bytes 172040 | tf_op jit(solution)/shard_map/ppermute | solution.py:494
  17.6 5.2 %collective-permute-start.4 = (bf16[14,2048]{1,0:T(8,128)(2,1)S(1)}, bf16[14,2048]{1,0:T(8,128)(2,1)S(1)}, u32[]{:S(2)}, u32[]{:S(2)}) collective-permute-start(bf16[14,2048]{1,0:T(8,128)(2,1)S(1)} %get-tuple-element.66.refs_0_), channel_id=1, source_target_pairs={{0,8},{1,9},{2,10},{3,11},{4,12},{5,13},{6,14},{7,15},{8,0},{9,1},... | collective-permute-start | bytes 172040 | tf_op jit(solution)/shard_map/ppermute | solution.py:494
  23.2 1.3 %collective-permute-start.5 = (f32[8,2048]{1,0:T(8,128)S(1)}, f32[8,2048]{1,0:T(8,128)S(1)}, u32[]{:S(2)}, u32[]{:S(2)}) collective-permute-start(f32[8,2048]{1,0:T(8,128)S(1)} %get-tuple-element.76), channel_id=1, source_target_pairs={{0,1},{1,0},{2,3},{3,2},{4,5},{5,4},{6,7},{7,6},{8,9},{9,8},{10,11... | collective-permute-start | bytes 196616 | tf_op jit(solution)/shard_map/ppermute | solution.py:494

commit v4 on v3

--- a/solution.py
+++ b/solution.py
@@ -7,10 +7,11 @@
 
 SEGMENTS = 8
 WIDTH = 256
-CHUNK = 512
+CHUNK = 1024
 POLES = 2
 SUBROWS = 16
-PARTS = (3, 3, 2)
+LOCAL_CHUNK = 512
+PARTS = (2, 1, 1)
 f32 = jnp.float32
 bf16 = jnp.bfloat16
 
@@ -38,16 +39,16 @@
 
 
 def pair_at(ref, index, cols):
-    return (ref[4 * index : 4 * index + 2, cols], ref[4 * index + 2 : 4 * index + 4, cols])
+    return (ref[2 * index, :, cols], ref[2 * index + 1, :, cols])
 
 
 def put_pair(ref, index, cols, value):
-    ref[4 * index : 4 * index + 2, cols] = value[0]
-    ref[4 * index + 2 : 4 * index + 4, cols] = value[1]
+    ref[2 * index, :, cols] = value[0]
+    ref[2 * index + 1, :, cols] = value[1]
 
 
 def pole_at(ref, index, pole, cols):
-    return (wide(ref[pl.ds(4 * index + pole, 1), cols]), wide(ref[pl.ds(4 * index + 2 + pole, 1), cols]))
+    return (wide(ref[2 * index, pole : pole + 1, cols]), wide(ref[2 * index + 1, pole : pole + 1, cols]))
 
 
 def half_angle(angle):
@@ -179,7 +180,7 @@
                     state = plus(state, times(factor, moved))
                 for part in range(2):
                     scan_ref[2 * part + pole, :, here] = state[part]
-                    total_ref[2 * part + pole : 2 * part + pole + 1, here] = state[part][SEGMENTS - 1 :]
+                    total_ref[part, pole : pole + 1, here] = state[part][SEGMENTS - 1 :]
 
         loop_columns(i, chunk, column)
         return 0
@@ -188,14 +189,14 @@
     for copy in smalls[3:]:
         copy.wait()
     for which in range(3):
-        edge_ref[2 * which : 2 * which + 2] = end_ref[which, SUBROWS - 2 : SUBROWS]
+        edge_ref[which] = end_ref[which, SUBROWS - 2 : SUBROWS]
     for which in range(2):
-        edge_ref[6 + 2 * which : 8 + 2 * which] = top_ref[which, 0:2]
+        edge_ref[3 + which] = top_ref[which, 0:2]
     own, other = halves(channels)
-    keep_total[...] = total_ref[:, own]
-    give_total[...] = total_ref[:, other]
-    keep_edge[...] = edge_ref[:, own]
-    give_edge[...] = edge_ref[:, other]
+    keep_total[...] = total_ref[:, :, own]
+    give_total[...] = total_ref[:, :, other]
+    keep_edge[...] = edge_ref[:, :, own]
+    give_edge[...] = edge_ref[:, :, other]
 
 
 def halves(channels):
@@ -205,45 +206,48 @@
 
 
 def first_products(tail, heads, taps):
-    def filtered(which, at):
-        sequence = [tail[2 * which : 2 * which + 1], tail[2 * which + 1 : 2 * which + 2],
-                    heads[2 * which - 2 : 2 * which - 1], heads[2 * which - 1 : 2 * which]]
-        return sum(taps[tap, which : which + 1] * sequence[at + tap] for tap in range(3))
-
-    return [filtered(1, at) * filtered(2, at) for at in range(2)]
+    def filtered(which):
+        before, after = tail[which], heads[which - 1]
+        middle = jnp.concatenate([before[1:2], after[0:1]], axis=0)
+        planes = (before, middle, after)
+        return sum(taps[tap, which : which + 1] * planes[tap] for tap in range(3))
+
+    return filtered(1) * filtered(2)
 
 
 def extra_state(products, back):
-    first, second = products
+    first, second = products[0:1], products[1:2]
     return times(back, (second * back[0] + first, second * back[1]))
 
 
 def fixed_rows(products, tail, taps, skip, gain, back):
-    first, second = products
     jump = sum(gain[0, pole : pole + 1] * back[0][pole : pole + 1] - gain[1, pole : pole + 1] * back[1][pole : pole + 1]
                for pole in range(POLES))
-    return [skip * first - jump * second, skip * second,
-            taps[0, 0:1] * tail[0:1] + taps[1, 0:1] * tail[1:2], taps[0, 0:1] * tail[1:2]]
+    none = jnp.zeros_like(jump)
+    local = skip * products - jnp.concatenate([jump * products[1:2], none], axis=0)
+    query = taps[0, 0:1] * tail[0] + jnp.concatenate([taps[1, 0:1] * tail[0][1:2], none], axis=0)
+    return local, query
+
+
+def planes_of(ref, start, stop):
+    return [ref[i].astype(f32) for i in range(start, stop)]
 
 
 def pick(condition, a, b):
     return tuple(jnp.where(condition, x, y) for x, y in zip(a, b))
 
 
+def mixed(value):
+    return jnp.concatenate([value[0:1] + value[1:2], value[0:1] - value[1:2]], axis=0)
+
+
 def put_wire(wire_ref, value):
     for part in range(2):
-        total = value[part][0:1] + value[part][1:2]
-        difference = value[part][0:1] - value[part][1:2]
-        wire_ref[2 * part : 2 * part + 2] = jnp.concatenate([total, difference], axis=0).astype(bf16)
+        wire_ref[part] = mixed(value[part]).astype(bf16)
 
 
 def from_wire(wire_ref):
-    value = []
-    for part in range(2):
-        both = wire_ref[2 * part : 2 * part + 2].astype(f32)
-        total, difference = both[0:1], both[1:2]
-        value.append(0.5 * jnp.concatenate([total + difference, total - difference], axis=0))
-    return tuple(value)
+    return tuple(0.5 * mixed(wire_ref[part].astype(f32)) for part in range(2))
 
 
 ALL = slice(None)
@@ -256,78 +260,85 @@
     half = halves(channels)[0]
     taps, gain, skip = taps_ref[:, :, half], gain_ref[:, :, half], skip_ref[:, half]
     power, back = pair_at(power_ref, SPAN, half), pair_at(power_ref, BACK, half)
-    mine, mates = edge_ref[...].astype(f32), mate_edge_ref[...].astype(f32)
-    even_edge, odd_edge = jnp.where(odd, mates, mine), jnp.where(odd, mine, mates)
+    mine, mates = planes_of(edge_ref, 0, 5), planes_of(mate_edge_ref, 0, 5)
+    even_edge, odd_edge = pick(odd, mates, mine), pick(odd, mine, mates)
     own, mate = pair_at(total_ref, 0, ALL), pair_at(mate_ref, 0, ALL)
     even_total, odd_total = pick(odd, mate, own), pick(odd, own, mate)
-    products = first_products(even_edge[0:6], odd_edge[6:10], taps)
+    products = first_products(even_edge[0:3], odd_edge[3:5], taps)
     base = plus(even_total, extra_state(products, back))
     put_pair(base_ref, 0, ALL, base)
-    for i, value in enumerate(fixed_rows(products, even_edge[0:6], taps, skip, gain, back)):
-        fix_ref[i : i + 1] = value
-    start = extra_state(first_products(jnp.zeros_like(even_edge[0:6]), even_edge[6:10], taps), back)
+    fix_ref[0], fix_ref[1] = fixed_rows(products, even_edge[0:3], taps, skip, gain, back)
+    start = extra_state(first_products([jnp.zeros_like(power[0])] * 3, even_edge[3:5], taps), back)
     enter = tuple(jnp.where(device < 2, part, 0.0) for part in start)
     put_pair(enter_ref, 0, ALL, enter)
     joined = plus(odd_total, times(power, plus(base, times(power, enter))))
     put_pair(joined_ref, 0, ALL, joined)
     put_pair(lead_ref, 0, ALL, (jnp.ones_like(power[0]), jnp.zeros_like(power[0])))
     put_wire(wire_ref, joined)
-    wire_ref[4:10] = odd_edge[0:6].astype(bf16)
-    wire_ref[10:14] = even_edge[6:10].astype(bf16)
-    head_ref[...] = even_edge[6:10].astype(bf16)
-
-
-def step_of(level, sent_ref, got_ref, power_ref, taps_ref, lead_ref, enter_ref, tail_before, half):
+    for i in range(3):
+        wire_ref[2 + i] = odd_edge[i].astype(bf16)
+    for i in range(2):
+        head = even_edge[3 + i].astype(bf16)
+        head_ref[i] = head
+        wire_ref[5 + i] = head
+
+
+def step_of(level, sent_ref, got_ref, own_head, power_ref, taps_ref, lead_ref, enter_ref, tail_before, half):
     device = lax.axis_index("seq")
     upper = (device >> level) % 2 == 1
     leads = jnp.logical_and(upper, (device % (1 << level)) < 2)
     back = pair_at(power_ref, BACK, half)
-    early_tail = jnp.where(upper, got_ref[4:10].astype(f32), sent_ref[4:10].astype(f32))
-    late_head = sent_ref[10:14].astype(f32)
-    if got_ref.shape[0] > 10:
-        late_head = jnp.where(upper, late_head, got_ref[10:14].astype(f32))
+    early_tail = pick(upper, planes_of(got_ref, 2, 5), planes_of(sent_ref, 2, 5))
+    late_head = own_head
+    if got_ref.shape[0] > 5:
+        late_head = pick(upper, own_head, planes_of(got_ref, 5, 7))
     extra = extra_state(first_products(early_tail, late_head, taps_ref[:, :, half]), back)
     other = from_wire(got_ref)
     lead, enter = pair_at(lead_ref, 0, ALL), pair_at(enter_ref, 0, ALL)
     enter = pick(upper, plus(enter, times(lead, plus(other, extra))), enter)
-    return upper, other, extra, lead, enter, jnp.where(leads, early_tail, tail_before)
-
-
-def join_kernel(ending_ref, sent_ref, got_ref, power_ref, taps_ref, lead_ref, enter_ref, before_ref, after_ref,
-                joined_ref, wire_ref, next_lead_ref, next_enter_ref, next_before_ref, *, level, channels):
+    return upper, other, extra, lead, enter, pick(leads, early_tail, tail_before)
+
+
+def join_kernel(ending_ref, sent_ref, got_ref, head_ref, power_ref, taps_ref, lead_ref, enter_ref, before_ref, after_ref,
+                joined_ref, wire_ref, next_head_ref, next_lead_ref, next_enter_ref, next_before_ref, *, level, channels):
     half = halves(channels)[0]
+    own_head = planes_of(head_ref, 0, 2)
     upper, other, extra, lead, enter, before = step_of(
-        level, sent_ref, got_ref, power_ref, taps_ref, lead_ref, enter_ref, before_ref[...].astype(f32), half)
+        level, sent_ref, got_ref, own_head, power_ref, taps_ref, lead_ref, enter_ref, planes_of(before_ref, 0, 3), half)
     factor = pair_at(power_ref, SPAN + level, half)
     mine = pair_at(ending_ref, 0, ALL)
     early, late = pick(upper, other, mine), pick(upper, mine, other)
     joined = plus(times(factor, plus(early, extra)), late)
     put_pair(joined_ref, 0, ALL, joined)
     put_wire(wire_ref, joined)
-    got, sent = got_ref[...].astype(f32), sent_ref[...].astype(f32)
-    wire_ref[4:10] = jnp.where(upper, sent[4:10], got[4:10]).astype(bf16)
-    wire_ref[10:14] = jnp.where(upper, got[10:14], sent[10:14]).astype(bf16)
+    for i, plane in enumerate(pick(upper, planes_of(sent_ref, 2, 5), planes_of(got_ref, 2, 5))):
+        wire_ref[2 + i] = plane.astype(bf16)
+    for i, plane in enumerate(pick(upper, planes_of(got_ref, 5, 7), own_head)):
+        head = plane.astype(bf16)
+        next_head_ref[i] = head
+        if wire_ref.shape[0] > 5:
+            wire_ref[5 + i] = head
     put_pair(next_lead_ref, 0, ALL, pick(upper, times(lead, factor), lead))
     put_pair(next_enter_ref, 0, ALL, enter)
-    next_before_ref[...] = before.astype(bf16)
-
-
-def last_kernel(sent_ref, got_ref, power_ref, taps_ref, gain_ref, skip_ref, lead_ref, enter_ref, before_ref,
-                base_ref, fix_ref, head_ref, after_ref, keep_ref, give_ref, *, level, channels):
+    for i in range(3):
+        next_before_ref[i] = before[i].astype(bf16)
+
+
+def last_kernel(sent_ref, got_ref, head_ref, power_ref, taps_ref, gain_ref, skip_ref, lead_ref, enter_ref, before_ref,
+                base_ref, fix_ref, first_ref, after_ref, keep_ref, give_ref, *, level, channels):
     half = halves(channels)[0]
     odd = lax.axis_index("seq") % 2 == 1
     _, _, _, _, enter, before = step_of(
-        level, sent_ref, got_ref, power_ref, taps_ref, lead_ref, enter_ref, before_ref[...].astype(f32), half)
+        level, sent_ref, got_ref, planes_of(head_ref, 0, 2), power_ref, taps_ref, lead_ref, enter_ref,
+        planes_of(before_ref, 0, 3), half)
     taps, gain, skip = taps_ref[:, :, half], gain_ref[:, :, half], skip_ref[:, half]
     power, back = pair_at(power_ref, SPAN, half), pair_at(power_ref, BACK, half)
-    products = first_products(before, head_ref[...].astype(f32), taps)
+    products = first_products(before, planes_of(first_ref, 0, 2), taps)
     even = [*enter, *fixed_rows(products, before, taps, skip, gain, back)]
-    odds = [*plus(times(power, enter), pair_at(base_ref, 0, ALL)), *(fix_ref[i : i + 1] for i in range(4))]
-    row = 0
-    for a, b in zip(even, odds):
-        keep_ref[row : row + a.shape[0]] = jnp.where(odd, b, a)
-        give_ref[row : row + a.shape[0]] = jnp.where(odd, a, b)
-        row += a.shape[0]
+    odds = [*plus(times(power, enter), pair_at(base_ref, 0, ALL)), fix_ref[0], fix_ref[1]]
+    for i, (a, b) in enumerate(zip(even, odds)):
+        keep_ref[i] = jnp.where(odd, b, a)
+        give_ref[i] = jnp.where(odd, a, b)
 
 
 def local_kernel(taps_ref, gain_ref, skip_ref, power_ref, scan_ref, prod_ref, q_ref, after_ref,
@@ -396,8 +407,8 @@
     chunk = gated_ref.shape[1]
     count = channels // chunk
     own, other = halves(channels)
-    state_ref[:, own] = keep_ref[...]
-    state_ref[:, other] = got_ref[...]
+    state_ref[:, :, own] = keep_ref[...]
+    state_ref[:, :, other] = got_ref[...]
     order_ref[...] = order_matrix(rows, True)
 
     def send(i):
@@ -415,8 +426,8 @@
                 queries = steps_of(query_ref, take)
                 local = steps_of(local_ref, take)
                 for j in range(2):
-                    local[j] = local[j] + jnp.where(first_mask(), wide(state_ref[4 + j : 5 + j, here]), 0.0)
-                    queries[j] = queries[j] + jnp.where(first_mask(), wide(state_ref[6 + j : 7 + j, here]), 0.0)
+                    local[j] = local[j] + jnp.where(first_mask(), wide(state_ref[2, j : j + 1, here]), 0.0)
+                    queries[j] = queries[j] + jnp.where(first_mask(), wide(state_ref[3, j : j + 1, here]), 0.0)
                 coefs = []
                 for pole in range(POLES):
                     lam = pole_at(power_ref, LAM, pole, here)
@@ -476,15 +487,20 @@
     arguments = [pole_angles, decay_rates, short_taps, residues, skip_gain[None], projected]
     arguments = [pltpu.with_memory_space_constraint(argument, pltpu.HBM) for argument in arguments]
     half = channels // 2
-    state = ((4, half), f32)
+    local_chunk = min(LOCAL_CHUNK, channels)
     square = pltpu.VMEM((rows, rows), bf16)
     dma = pltpu.SemaphoreType.DMA
 
+    def pairs(count, dtype=f32, extent=half):
+        return (count, POLES, extent), dtype
+
+    state = pairs(2)
     products, scan, total, give_total, edge, give_edge, powers, taps, gains, skip, query_rows = kernel_call(
         states_kernel, "states",
-        [((rows, channels), bf16), ((4, SEGMENTS, channels), f32), state, state, ((10, half), bf16), ((10, half), bf16),
-         ((4 * (SPAN + levels), channels), f32), (short_taps.shape, f32), (residues.shape, f32), ((1, channels), f32), ((rows, channels), bf16)],
-        [pltpu.VMEM((4, channels), f32), pltpu.VMEM((10, channels), bf16), square]
+        [((rows, channels), bf16), ((4, SEGMENTS, channels), f32), state, state, pairs(5, bf16), pairs(5, bf16),
+         pairs(2 * (SPAN + levels), f32, channels), (short_taps.shape, f32), (residues.shape, f32),
+         ((1, channels), f32), ((rows, channels), bf16)],
+        [pltpu.VMEM(*pairs(2, f32, channels)), pltpu.VMEM(*pairs(5, bf16, channels)), square]
         + [pltpu.VMEM(pole_angles.shape, f32)] * 2 + [pltpu.VMEM((rows, channels), bf16)] * 2
         + [pltpu.VMEM((2, SUBROWS, channels), bf16), pltpu.VMEM((3, SUBROWS, channels), bf16)]
         + [pltpu.VMEM((rows, chunk), f32)] * 2 + [dma((8,)), dma((2, channels // chunk))],
@@ -493,12 +509,16 @@
     def exchange(array, level):
         return lax.ppermute(array, "seq", [(i, i ^ (1 << level)) for i in range(devices)])
 
+    def message(level):
+        return pairs(5 if level == levels - 1 else 7, bf16)
+
     mate_edge = exchange(give_edge, 0)
     mate_total = exchange(give_total, 0)
-    ending, sent, lead, enter, base, fix, head = kernel_call(
-        merge_kernel, "merge", [state, ((14, half), bf16), state, state, state, state, ((4, half), bf16)], [],
+    ending, sent, lead, enter, base, fix, first = kernel_call(
+        merge_kernel, "merge", [state, pairs(7, bf16), state, state, state, state, pairs(2, bf16)], [],
         [total, mate_total, edge, mate_edge, powers, taps, gains, skip], (), channels=channels)
-    before = jnp.zeros((6, half), bf16)
+    head = first
+    before = jnp.zeros(*pairs(3, bf16))
 
     tables = []
     start = 0
@@ -509,24 +529,25 @@
             plane = ((rows, part), f32)
             tables.append(kernel_call(
                 local_kernel, "local", [plane, plane, ((4, SEGMENTS, part), f32)],
-                [square, pltpu.VMEM((rows, chunk), f32)],
+                [square, pltpu.VMEM((rows, local_chunk), f32)],
                 [taps, gains, skip, powers, scan, products, query_rows, ending], (), base=start))
             start += part
+        after = tables[-1][2]
         if level + 1 < levels:
-            ending, sent, lead, enter, before = kernel_call(
-                join_kernel, "join", [state, ((14, half), bf16), state, state, ((6, half), bf16)], [],
-                [ending, sent, got, powers, taps, lead, enter, before, tables[-1][2]], (8,), level=level, channels=channels)
+            ending, sent, head, lead, enter, before = kernel_call(
+                join_kernel, "join", [state, message(level + 1), pairs(2, bf16), state, state, pairs(3, bf16)], [],
+                [ending, sent, got, head, powers, taps, lead, enter, before, after], (9,), level=level, channels=channels)
 
     keep, give = kernel_call(
-        last_kernel, "last", [((8, half), f32)] * 2, [],
-        [sent, got, powers, taps, gains, skip, lead, enter, before, base, fix, head, tables[-1][2]], (12,),
+        last_kernel, "last", [pairs(4)] * 2, [],
+        [sent, got, head, powers, taps, gains, skip, lead, enter, before, base, fix, first, after], (13,),
         level=levels - 1, channels=channels)
     got = exchange(give, 0)
 
     (out,) = kernel_call(
         gate_kernel, "gate", [((rows, channels), bf16)],
         [square, pltpu.VMEM((rows, channels), bf16), pltpu.VMEM((rows, chunk), bf16),
-         pltpu.VMEM((8, channels), f32), dma((channels // chunk,))],
+         pltpu.VMEM(*pairs(4, f32, channels)), dma((channels // chunk,))],
         [powers, keep, got, *[array for table in tables for array in table]], (), (0,), parts=parts)
     return out
 

time: 27.6 us -> 25 us (0.906)
  Pallas kernels: 12.2 us -> 10.1 us
  waiting for transfers between devices: 7.04 us -> 6.48 us
    pallas_call x9, Pallas kernels: 12.2 us -> 10.1 us  [kernel_call(): pl.pallas_call(bound, in_specs=[spec(i in in_hbm) for i in range(len(oper...]
    ppermute x6, waiting for transfers between devices: 7.04 us -> 6.48 us  [exchange(): lax.ppermute(array, 'seq', [(i, i ^ 1 << level) for i in range(devices)])]
  transfers between devices with their start and end apart: 6 -> 6, of which waited for: 5 -> 5; matrix products, arithmetic and copies ran while one was open for 0% -> 0% of each run, Pallas kernels for 10% -> 11%
where the time goes in v4:
time: 25 us; the launch traced here: 24.9 us
  Pallas kernels  10.1 us (40%)
  starting transfers between devices  8.19 us (33%)
  waiting for transfers between devices  6.48 us (26%)
    pallas_call x9, Pallas kernels, kernel_call(): pl.pallas_call(bound, in_specs=[spec(i in in_hbm) for i in range(len(oper...  10.1 us
    ppermute x6, starting transfers between devices, exchange(): lax.ppermute(array, 'seq', [(i, i ^ 1 << level) for i in range(devices)])  8.19 us
    ppermute x6, waiting for transfers between devices, exchange(): lax.ppermute(array, 'seq', [(i, i ^ 1 << level) for i in range(devices)])  6.48 us
  transfers between devices with their start and end apart: 6, of which 5 were waited for; matrix products, arithmetic and copies ran while one was open for 0% of the time, Pallas kernels for 11%

profile of v4, /device:TPU:0, one launch (start us, length us, event | category | flops | bytes accessed | tf_op | source)
XLA Modules:
  0.0 24.9 jit_solution(10685292570614995147)
XLA Ops:
  0.0 4.0 %states.1 = (bf16[128,4096]{1,0:T(8,128)(2,1)S(1)}, f32[4,8,4096]{2,1,0:T(8,128)S(1)}, f32[2,2,2048]{2,1,0:T(2,128)S(1)}, f32[2,2,2048]{2,1,0:T(2,128)S(1)}, bf1...) custom-call(f32[2,4096]{1,0:T(2,128)} %refs_0_.1, ...), custom_call_target="tpu_custom_call" | custom-call | tf_op jit(solution)/shard_map/states/pallas_call | solution.py:470
  4.1 0.6 %collective-permute-start.1 = (bf16[5,2,2048]{2,1,0:T(2,128)(2,1)S(1)}, bf16[5,2,2048]{2,1,0:T(2,128)(2,1)S(1)}, u32[]{:S(2)}, u32[]{:S(2)}) collective-permute-start(bf16[5,2,2048]{2,1,0:T(2,128)(2,1)S(1)} %get-tuple-element.50), channel_id=1, source_target_pairs={{0,1},{1,0},{2,3},{3,2},{4,5},{5,4},{6,7},{7,6},{8,9},{9,8},{10,11... | collective-permute-start | bytes 122888 | tf_op jit(solution)/shard_map/ppermute | solution.py:510
  4.6 0.1 collective-permute-start
  4.7 1.1 %collective-permute-done.refs_1_ = f32[2,2,2048]{2,1,0:T(2,128)S(1)} collective-permute-done((f32[2,2,2048]{2,1,0:T(2,128)S(1)}, f32[2,2,2048]{2,1,0:T(2,128)S(1)}, u32[]{:S(2)}, u32[]{:S(2)}) %collective-permute-start) | collective-permute-done | bytes 32800 | tf_op jit(solution)/shard_map/ppermute | solution.py:510
  5.8 0.0 collective-permute-done.1.refs_3_
  5.8 0.3 %merge.1 = (f32[2,2,2048]{2,1,0:T(2,128)S(1)}, bf16[7,2,2048]{2,1,0:T(2,128)(2,1)S(1)}, f32[2,2,2048]{2,1,0:T(2,128)S(1)}, f32[2,2,2048]{2,1,0:T(2,128)S(1)}, f3...) custom-call(f32[2,2,2048]{2,1,0:T(2,128)S(1)} %get-tuple-element.47.refs_0_, ...), custom_call_target="tpu_custom_call" | custom-call | tf_op jit(solution)/shard_map/merge/pallas_call | solution.py:470
  6.1 2.7 %collective-permute-start.2 = (bf16[7,2,2048]{2,1,0:T(2,128)(2,1)S(1)}, bf16[7,2,2048]{2,1,0:T(2,128)(2,1)S(1)}, u32[]{:S(2)}, u32[]{:S(2)}) collective-permute-start(bf16[7,2,2048]{2,1,0:T(2,128)(2,1)S(1)} %get-tuple-element.55.refs_1_), channel_id=1, source_target_pairs={{0,2},{1,3},{2,0},{3,1},{4,6},{5,7},{6,4},{7,5},{8,10},{9,11},{10,... | collective-permute-start | bytes 172040 | tf_op jit(solution)/shard_map/ppermute | solution.py:510
  8.8 1.4 %local.3 = (f32[128,2048]{1,0:T(8,128)S(1)}, f32[128,2048]{1,0:T(8,128)S(1)}, f32[4,8,2048]{2,1,0:T(8,128)S(1)}) custom-call(f32[3,3,4096]{2,1,0:T(4,128)S(1)} %get-tuple-element.51.refs_5_.refs_0_.refs_4_, f32[2,2,4096]{2,1,0:T(2,128)S(1)} %get-tuple-element.52.refs_6_.refs_1_.refs_5_, f32[1,4096]{1,0:T(1,128)S(1)} %get-tuple-element.53.refs_7_.refs_2_.refs_6_, ...), custom_call_target="tpu_custom_call" | custom-call | tf_op jit(solution)/shard_map/local/pallas_call | solution.py:470
  10.2 1.0 %collective-permute-done.2.refs_2_ = bf16[7,2,2048]{2,1,0:T(2,128)(2,1)S(1)} collective-permute-done((bf16[7,2,2048]{2,1,0:T(2,128)(2,1)S(1)}, bf16[7,2,2048]{2,1,0:T(2,128)(2,1)S(1)}, u32[]{:S(2)}, u32[]{:S(2)}) %collective-permute-start.2) | collective-permute-done | bytes 57376 | tf_op jit(solution)/shard_map/ppermute | solution.py:510
  11.3 0.3 %join.2 = (f32[2,2,2048]{2,1,0:T(2,128)S(1)}, bf16[7,2,2048]{2,1,0:T(2,128)(2,1)S(1)}, bf16[2,2,2048]{2,1,0:T(2,128)(2,1)S(1)}, f32[2,2,2048]{2,1,0:T(2,128)S(1)...) custom-call(f32[2,2,2048]{2,1,0:T(2,128)S(1)} %get-tuple-element.54.refs_7_.refs_0_, ...), custom_call_target="tpu_custom_call" | custom-call | tf_op jit(solution)/shard_map/join/pallas_call | solution.py:470
  11.5 1.9 %collective-permute-start.3 = (bf16[7,2,2048]{2,1,0:T(2,128)(2,1)S(1)}, bf16[7,2,2048]{2,1,0:T(2,128)(2,1)S(1)}, u32[]{:S(2)}, u32[]{:S(2)}) collective-permute-start(bf16[7,2,2048]{2,1,0:T(2,128)(2,1)S(1)} %get-tuple-element.64.refs_1_), channel_id=1, source_target_pairs={{0,4},{1,5},{2,6},{3,7},{4,0},{5,1},{6,2},{7,3},{8,12},{9,13},{10,... | collective-permute-start | bytes 172040 | tf_op jit(solution)/shard_map/ppermute | solution.py:510
  13.4 0.7 %local.4 = (f32[128,1024]{1,0:T(8,128)S(1)}, f32[128,1024]{1,0:T(8,128)S(1)}, f32[4,8,1024]{2,1,0:T(8,128)S(1)}) custom-call(f32[3,3,4096]{2,1,0:T(4,128)S(1)} %get-tuple-element.51.refs_5_.refs_0_.refs_4_, f32[2,2,4096]{2,1,0:T(2,128)S(1)} %get-tuple-element.52.refs_6_.refs_1_.refs_5_, f32[1,4096]{1,0:T(1,128)S(1)} %get-tuple-element.53.refs_7_.refs_2_.refs_6_, ...), custom_call_target="tpu_custom_call" | custom-call | tf_op jit(solution)/shard_map/local/pallas_call | solution.py:470
  14.1 1.7 %collective-permute-done.3.refs_2_ = bf16[7,2,2048]{2,1,0:T(2,128)(2,1)S(1)} collective-permute-done((bf16[7,2,2048]{2,1,0:T(2,128)(2,1)S(1)}, bf16[7,2,2048]{2,1,0:T(2,128)(2,1)S(1)}, u32[]{:S(2)}, u32[]{:S(2)}) %collective-permute-start.3) | collective-permute-done | bytes 57376 | tf_op jit(solution)/shard_map/ppermute | solution.py:510
  15.8 0.3 %join.3 = (f32[2,2,2048]{2,1,0:T(2,128)S(1)}, bf16[5,2,2048]{2,1,0:T(2,128)(2,1)S(1)}, bf16[2,2,2048]{2,1,0:T(2,128)(2,1)S(1)}, f32[2,2,2048]{2,1,0:T(2,128)S(1)...) custom-call(f32[2,2,2048]{2,1,0:T(2,128)S(1)} %get-tuple-element.63.refs_7_.refs_0_, ...), custom_call_target="tpu_custom_call" | custom-call | tf_op jit(solution)/shard_map/join/pallas_call | solution.py:470
  16.0 2.9 %collective-permute-start.4 = (bf16[5,2,2048]{2,1,0:T(2,128)(2,1)S(1)}, bf16[5,2,2048]{2,1,0:T(2,128)(2,1)S(1)}, u32[]{:S(2)}, u32[]{:S(2)}) collective-permute-start(bf16[5,2,2048]{2,1,0:T(2,128)(2,1)S(1)} %get-tuple-element.70.refs_0_), channel_id=1, source_target_pairs={{0,8},{1,9},{2,10},{3,11},{4,12},{5,13},{6,14},{7,15},{8,0},{9,1},... | collective-permute-start | bytes 122888 | tf_op jit(solution)/shard_map/ppermute | solution.py:510
  18.9 0.7 %local.5 = (f32[128,1024]{1,0:T(8,128)S(1)}, f32[128,1024]{1,0:T(8,128)S(1)}, f32[4,8,1024]{2,1,0:T(8,128)S(1)}) custom-call(f32[3,3,4096]{2,1,0:T(4,128)S(1)} %get-tuple-element.51.refs_5_.refs_0_.refs_4_, f32[2,2,4096]{2,1,0:T(2,128)S(1)} %get-tuple-element.52.refs_6_.refs_1_.refs_5_, f32[1,4096]{1,0:T(1,128)S(1)} %get-tuple-element.53.refs_7_.refs_2_.refs_6_, ...), custom_call_target="tpu_custom_call" | custom-call | tf_op jit(solution)/shard_map/local/pallas_call | solution.py:470
  19.6 1.4 %collective-permute-done.4.refs_1_ = bf16[5,2,2048]{2,1,0:T(2,128)(2,1)S(1)} collective-permute-done((bf16[5,2,2048]{2,1,0:T(2,128)(2,1)S(1)}, bf16[5,2,2048]{2,1,0:T(2,128)(2,1)S(1)}, u32[]{:S(2)}, u32[]{:S(2)}) %collective-permute-start.4) | collective-permute-done | bytes 40992 | tf_op jit(solution)/shard_map/ppermute | solution.py:510
  21.0 0.2 last.1
  21.3 0.1 collective-permute-start.5
  21.3 1.2 %collective-permute-done.5.refs_2_ = f32[4,2,2048]{2,1,0:T(2,128)S(1)} collective-permute-done((f32[4,2,2048]{2,1,0:T(2,128)S(1)}, f32[4,2,2048]{2,1,0:T(2,128)S(1)}, u32[]{:S(2)}, u32[]{:S(2)}) %collective-permute-start.5) | collective-permute-done | bytes 65568 | tf_op jit(solution)/shard_map/ppermute | solution.py:510
  22.6 2.3 %gate.1 = bf16[128,4096]{1,0:T(8,128)(2,1)} custom-call(f32[18,2,4096]{2,1,0:T(2,128)S(1)} %get-tuple-element.46.refs_4_.refs_3_.refs_0_, f32[4,2,2048]{2,1,0:T(2,128)S(1)} %get-tuple-element.79.refs_1_, f32[4,2,2048]{2,1,0:T(2,128)S(1)} %collective-permute-done.5.refs_2_, f32[128,2048]{1,0:T(8,128)S(1)} %get-tuple-element.81.refs_3_, ...), custom_call_target="tpu_custom_call" | custom-call | tf_op jit(solution)/shard_map/gate/pallas_call | solution.py:470
  (1 shorter events, 0.0 us)
Async XLA Ops:
  4.1 1.8 %collective-permute-start.1 = (bf16[5,2,2048]{2,1,0:T(2,128)(2,1)S(1)}, bf16[5,2,2048]{2,1,0:T(2,128)(2,1)S(1)}, u32[]{:S(2)}, u32[]{:S(2)}) collective-permute-start(bf16[5,2,2048]{2,1,0:T(2,128)(2,1)S(1)} %get-tuple-element.50), channel_id=1, source_target_pairs={{0,1},{1,0},{2,3},{3,2},{4,5},{5,4},{6,7},{7,6},{8,9},{9,8},{10,11... | collective-permute-start | bytes 122888 | tf_op jit(solution)/shard_map/ppermute | solution.py:510
  4.6 1.2 %collective-permute-start = (f32[2,2,2048]{2,1,0:T(2,128)S(1)}, f32[2,2,2048]{2,1,0:T(2,128)S(1)}, u32[]{:S(2)}, u32[]{:S(2)}) collective-permute-start(f32[2,2,2048]{2,1,0:T(2,128)S(1)} %get-tuple-element.48), channel_id=1, source_target_pairs={{0,1},{1,0},{2,3},{3,2},{4,5},{5,4},{6,7},{7,6},{8,9},{9,8},{10,11... | collective-permute-start | bytes 98312 | tf_op jit(solution)/shard_map/ppermute | solution.py:510
  6.1 5.2 %collective-permute-start.2 = (bf16[7,2,2048]{2,1,0:T(2,128)(2,1)S(1)}, bf16[7,2,2048]{2,1,0:T(2,128)(2,1)S(1)}, u32[]{:S(2)}, u32[]{:S(2)}) collective-permute-start(bf16[7,2,2048]{2,1,0:T(2,128)(2,1)S(1)} %get-tuple-element.55.refs_1_), channel_id=1, source_target_pairs={{0,2},{1,3},{2,0},{3,1},{4,6},{5,7},{6,4},{7,5},{8,10},{9,11},{10,... | collective-permute-start | bytes 172040 | tf_op jit(solution)/shard_map/ppermute | solution.py:510
  11.5 4.2 %collective-permute-start.3 = (bf16[7,2,2048]{2,1,0:T(2,128)(2,1)S(1)}, bf16[7,2,2048]{2,1,0:T(2,128)(2,1)S(1)}, u32[]{:S(2)}, u32[]{:S(2)}) collective-permute-start(bf16[7,2,2048]{2,1,0:T(2,128)(2,1)S(1)} %get-tuple-element.64.refs_1_), channel_id=1, source_target_pairs={{0,4},{1,5},{2,6},{3,7},{4,0},{5,1},{6,2},{7,3},{8,12},{9,13},{10,... | collective-permute-start | bytes 172040 | tf_op jit(solution)/shard_map/ppermute | solution.py:510
  16.0 5.0 %collective-permute-start.4 = (bf16[5,2,2048]{2,1,0:T(2,128)(2,1)S(1)}, bf16[5,2,2048]{2,1,0:T(2,128)(2,1)S(1)}, u32[]{:S(2)}, u32[]{:S(2)}) collective-permute-start(bf16[5,2,2048]{2,1,0:T(2,128)(2,1)S(1)} %get-tuple-element.70.refs_0_), channel_id=1, source_target_pairs={{0,8},{1,9},{2,10},{3,11},{4,12},{5,13},{6,14},{7,15},{8,0},{9,1},... | collective-permute-start | bytes 122888 | tf_op jit(solution)/shard_map/ppermute | solution.py:510
  21.3 1.3 %collective-permute-start.5 = (f32[4,2,2048]{2,1,0:T(2,128)S(1)}, f32[4,2,2048]{2,1,0:T(2,128)S(1)}, u32[]{:S(2)}, u32[]{:S(2)}) collective-permute-start(f32[4,2,2048]{2,1,0:T(2,128)S(1)} %get-tuple-element.80), channel_id=1, source_target_pairs={{0,1},{1,0},{2,3},{3,2},{4,5},{5,4},{6,7},{7,6},{8,9},{9,8},{10,11... | collective-permute-start | bytes 196616 | tf_op jit(solution)/shard_map/ppermute | solution.py:510

commit v5 on v4

--- a/solution.py
+++ b/solution.py
@@ -115,8 +115,8 @@
 
 
 def states_kernel(angle_hbm, decay_hbm, taps_hbm, gain_hbm, skip_hbm, proj_ref,
-                  prod_ref, scan_ref, keep_total, give_total, keep_edge, give_edge, power_ref, taps_ref, gain_ref, skip_ref,
-                  q_ref, total_ref, edge_ref, order_ref, angle_ref, decay_ref, k_ref, v_ref, top_ref, end_ref, ks_ref, vs_ref,
+                  prod_ref, scan_ref, keep_ref, give_ref, power_ref, taps_ref, gain_ref, skip_ref,
+                  q_ref, total_ref, order_ref, angle_ref, decay_ref, k_ref, v_ref, top_ref, end_ref, ks_ref, vs_ref,
                   small_sem, in_sem, *, levels):
     rows, channels = k_ref.shape
     chunk = ks_ref.shape[1]
@@ -189,14 +189,12 @@
     for copy in smalls[3:]:
         copy.wait()
     for which in range(3):
-        edge_ref[which] = end_ref[which, SUBROWS - 2 : SUBROWS]
+        total_ref[2 + which] = end_ref[which, SUBROWS - 2 : SUBROWS].astype(f32)
     for which in range(2):
-        edge_ref[3 + which] = top_ref[which, 0:2]
+        total_ref[5 + which] = top_ref[which, 0:2].astype(f32)
     own, other = halves(channels)
-    keep_total[...] = total_ref[:, :, own]
-    give_total[...] = total_ref[:, :, other]
-    keep_edge[...] = edge_ref[:, :, own]
-    give_edge[...] = edge_ref[:, :, other]
+    keep_ref[...] = total_ref[:, :, own]
+    give_ref[...] = total_ref[:, :, other]
 
 
 def halves(channels):
@@ -253,16 +251,16 @@
 ALL = slice(None)
 
 
-def merge_kernel(total_ref, mate_ref, edge_ref, mate_edge_ref, power_ref, taps_ref, gain_ref, skip_ref,
+def merge_kernel(own_ref, mate_ref, power_ref, taps_ref, gain_ref, skip_ref,
                  joined_ref, wire_ref, lead_ref, enter_ref, base_ref, fix_ref, head_ref, *, channels):
     device = lax.axis_index("seq")
     odd = device % 2 == 1
     half = halves(channels)[0]
     taps, gain, skip = taps_ref[:, :, half], gain_ref[:, :, half], skip_ref[:, half]
     power, back = pair_at(power_ref, SPAN, half), pair_at(power_ref, BACK, half)
-    mine, mates = planes_of(edge_ref, 0, 5), planes_of(mate_edge_ref, 0, 5)
+    mine, mates = planes_of(own_ref, 2, 7), planes_of(mate_ref, 2, 7)
     even_edge, odd_edge = pick(odd, mates, mine), pick(odd, mine, mates)
-    own, mate = pair_at(total_ref, 0, ALL), pair_at(mate_ref, 0, ALL)
+    own, mate = pair_at(own_ref, 0, ALL), pair_at(mate_ref, 0, ALL)
     even_total, odd_total = pick(odd, mate, own), pick(odd, own, mate)
     products = first_products(even_edge[0:3], odd_edge[3:5], taps)
     base = plus(even_total, extra_state(products, back))
@@ -400,39 +398,47 @@
     lax.fori_loop(0, channels // chunk, body, 0)
 
 
-def gate_kernel(power_ref, keep_ref, got_ref, *rest, parts):
-    tables = [rest[3 * i : 3 * i + 3] for i in range(len(parts))]
-    out_hbm, order_ref, out_ref, gated_ref, state_ref, out_sem = rest[3 * len(parts) :]
-    rows, channels = out_ref.shape
+def gate_kernel(power_ref, state_ref, *rest, parts, ready):
+    count = 3 * len(parts)
+    tables, rest = rest[:count], rest[count:]
+    if ready:
+        ready_ref, out_hbm, order_ref, out_ref, gated_ref, out_sem = rest
+    else:
+        out_ref, order_ref, gated_ref = rest
+    half = out_ref.shape[1]
     chunk = gated_ref.shape[1]
-    count = channels // chunk
-    own, other = halves(channels)
-    state_ref[:, :, own] = keep_ref[...]
-    state_ref[:, :, other] = got_ref[...]
-    order_ref[...] = order_matrix(rows, True)
+    own, other = halves(2 * half)
+    odd = lax.axis_index("seq") % 2
+    side = 1 - odd if ready else odd
+    begin = side * half
 
     def send(i):
         place = span(i * chunk, chunk)
-        return pltpu.make_async_copy(out_ref.at[:, place], out_hbm.at[:, place], out_sem.at[i])
-
-    base = 0
-    for part, (query_ref, local_ref, reach_ref) in zip(parts, tables):
-
-        def body(i, _, base=base, query_ref=query_ref, local_ref=local_ref, reach_ref=reach_ref):
+        return pltpu.make_async_copy(
+            out_ref.at[:, place], out_hbm.at[:, span(begin + i * chunk, chunk)], out_sem.at[i])
+
+    if ready:
+        finished = pltpu.make_async_copy(ready_ref, out_hbm.at[:, own], out_sem.at[half // chunk])
+        finished.start()
+    order_ref[...] = order_matrix(gated_ref.shape[0], True)
+
+    def gate_part(base, part, query_ref, local_ref, reach_ref):
+        def body(i, _):
             def column(inner, outer):
                 cols = slice(inner, inner + WIDTH)
                 take = span(outer, WIDTH)
+                there = span(base % half + outer, WIDTH)
                 here = span(base + outer, WIDTH)
                 queries = steps_of(query_ref, take)
                 local = steps_of(local_ref, take)
                 for j in range(2):
-                    local[j] = local[j] + jnp.where(first_mask(), wide(state_ref[2, j : j + 1, here]), 0.0)
-                    queries[j] = queries[j] + jnp.where(first_mask(), wide(state_ref[3, j : j + 1, here]), 0.0)
+                    local[j] = local[j] + jnp.where(first_mask(), wide(state_ref[2, j : j + 1, there]), 0.0)
+                    queries[j] = queries[j] + jnp.where(first_mask(), wide(state_ref[3, j : j + 1, there]), 0.0)
                 coefs = []
                 for pole in range(POLES):
                     lam = pole_at(power_ref, LAM, pole, here)
                     back = pole_at(power_ref, BACK, pole, here)
-                    state = times(pole_at(state_ref, 0, pole, here), (reach_ref[pole, :, take], reach_ref[2 + pole, :, take]))
+                    state = times(pole_at(state_ref, 0, pole, there), (reach_ref[pole, :, take], reach_ref[2 + pole, :, take]))
                     y2 = state[0] * back[0] - state[1] * back[1]
                     coefs.append([*feedback(lam), state[0], y2])
                 gated = []
@@ -449,15 +455,27 @@
                         gated_ref[SEGMENTS * (j - 1) : SEGMENTS * (j + 1), cols] = both.astype(bf16)
 
             loop_columns(i, chunk, column)
-            out_ref[:, span(base + i * chunk, chunk)] = jnp.dot(
+            place = base % half // chunk + i
+            out_ref[:, span(place * chunk, chunk)] = jnp.dot(
                 order_ref[...], gated_ref[...], preferred_element_type=f32).astype(bf16)
-            send(base // chunk + i).start()
+            if ready:
+                send(place).start()
             return 0
 
         lax.fori_loop(0, part // chunk, body, 0)
+
+    base = 0
+    for index, part in enumerate(parts):
+
+        @pl.when(side == base // half)
+        def _(base=base, part=part, refs=tables[3 * index : 3 * index + 3]):
+            gate_part(base, part, *refs)
+
         base += part
-    for i in range(count):
-        send(i).wait()
+    if ready:
+        for i in range(half // chunk):
+            send(i).wait()
+        finished.wait()
 
 
 def kernel_call(body, name, outs, scratch, operands, in_hbm, out_hbm=(), **options):
@@ -495,12 +513,12 @@
         return (count, POLES, extent), dtype
 
     state = pairs(2)
-    products, scan, total, give_total, edge, give_edge, powers, taps, gains, skip, query_rows = kernel_call(
+    products, scan, keep, give, powers, taps, gains, skip, query_rows = kernel_call(
         states_kernel, "states",
-        [((rows, channels), bf16), ((4, SEGMENTS, channels), f32), state, state, pairs(5, bf16), pairs(5, bf16),
+        [((rows, channels), bf16), ((4, SEGMENTS, channels), f32), pairs(7), pairs(7),
          pairs(2 * (SPAN + levels), f32, channels), (short_taps.shape, f32), (residues.shape, f32),
          ((1, channels), f32), ((rows, channels), bf16)],
-        [pltpu.VMEM(*pairs(2, f32, channels)), pltpu.VMEM(*pairs(5, bf16, channels)), square]
+        [pltpu.VMEM(*pairs(7, f32, channels)), square]
         + [pltpu.VMEM(pole_angles.shape, f32)] * 2 + [pltpu.VMEM((rows, channels), bf16)] * 2
         + [pltpu.VMEM((2, SUBROWS, channels), bf16), pltpu.VMEM((3, SUBROWS, channels), bf16)]
         + [pltpu.VMEM((rows, chunk), f32)] * 2 + [dma((8,)), dma((2, channels // chunk))],
@@ -512,11 +530,10 @@
     def message(level):
         return pairs(5 if level == levels - 1 else 7, bf16)
 
-    mate_edge = exchange(give_edge, 0)
-    mate_total = exchange(give_total, 0)
+    got = exchange(give, 0)
     ending, sent, lead, enter, base, fix, first = kernel_call(
         merge_kernel, "merge", [state, pairs(7, bf16), state, state, state, state, pairs(2, bf16)], [],
-        [total, mate_total, edge, mate_edge, powers, taps, gains, skip], (), channels=channels)
+        [keep, got, powers, taps, gains, skip], (), channels=channels)
     head = first
     before = jnp.zeros(*pairs(3, bf16))
 
@@ -543,12 +560,14 @@
         [sent, got, head, powers, taps, gains, skip, lead, enter, before, base, fix, first, after], (13,),
         level=levels - 1, channels=channels)
     got = exchange(give, 0)
-
+    flat = [array for table in tables for array in table]
+    half_plane = ((rows, half), bf16)
+    scratch = [square, pltpu.VMEM(*half_plane), pltpu.VMEM((rows, chunk), bf16), dma((half // chunk + 1,))]
+    (ready,) = kernel_call(
+        gate_kernel, "gate", [half_plane], [square, scratch[2]], [powers, keep, *flat], (), parts=parts, ready=False)
     (out,) = kernel_call(
-        gate_kernel, "gate", [((rows, channels), bf16)],
-        [square, pltpu.VMEM((rows, channels), bf16), pltpu.VMEM((rows, chunk), bf16),
-         pltpu.VMEM(*pairs(4, f32, channels)), dma((channels // chunk,))],
-        [powers, keep, got, *[array for table in tables for array in table]], (), (0,), parts=parts)
+        gate_kernel, "finish", [((rows, channels), bf16)], scratch, [powers, got, *flat, ready], (), (0,),
+        parts=parts, ready=True)
     return out
 
 

time: 25 us -> 24 us (0.960)
  waiting for transfers between devices: 6.48 us -> 4.97 us
  starting transfers between devices: 8.19 us -> 8.68 us
    ppermute x6 -> x5, waiting for transfers between devices: 6.48 us -> 4.97 us  [exchange(): lax.ppermute(array, 'seq', [(i, i ^ 1 << level) for i in range(devices)])]
    ppermute x6 -> x5, starting transfers between devices: 8.19 us -> 8.68 us  [exchange(): lax.ppermute(array, 'seq', [(i, i ^ 1 << level) for i in range(devices)])]
    pallas_call x9 -> x10, Pallas kernels: 10.1 us -> 10.1 us  [kernel_call(): pl.pallas_call(bound, in_specs=[spec(i in in_hbm) for i in range(len(oper...]
  transfers between devices with their start and end apart: 6 -> 5, of which waited for: 5 -> 5; matrix products, arithmetic and copies ran while one was open for 0% -> 0% of each run, Pallas kernels for 11% -> 15%
where the time goes in v5:
time: 24 us; the launch traced here: 23.9 us
  Pallas kernels  10.1 us (42%)
  starting transfers between devices  8.68 us (36%)
  waiting for transfers between devices  4.97 us (21%)
    pallas_call x10, Pallas kernels, kernel_call(): pl.pallas_call(bound, in_specs=[spec(i in in_hbm) for i in range(len(oper...  10.1 us
    ppermute x5, starting transfers between devices, exchange(): lax.ppermute(array, 'seq', [(i, i ^ 1 << level) for i in range(devices)])  8.68 us
    ppermute x5, waiting for transfers between devices, exchange(): lax.ppermute(array, 'seq', [(i, i ^ 1 << level) for i in range(devices)])  4.97 us
  transfers between devices with their start and end apart: 5, of which 5 were waited for; matrix products, arithmetic and copies ran while one was open for 0% of the time, Pallas kernels for 15%

profile of v5, /device:TPU:0, one launch (start us, length us, event | category | flops | bytes accessed | tf_op | source)
XLA Modules:
  0.0 23.9 jit_solution(2699459375114621970)
XLA Ops:
  0.0 4.1 %states.1 = (bf16[128,4096]{1,0:T(8,128)(2,1)S(1)}, f32[4,8,4096]{2,1,0:T(8,128)S(1)}, f32[7,2,2048]{2,1,0:T(2,128)S(1)}, f32[7,2,2048]{2,1,0:T(2,128)S(1)}, f32...) custom-call(f32[2,4096]{1,0:T(2,128)} %refs_0_.1, ...), custom_call_target="tpu_custom_call" | custom-call | tf_op jit(solution)/shard_map/states/pallas_call | solution.py:488
  4.1 0.6 %collective-permute-start = (f32[7,2,2048]{2,1,0:T(2,128)S(1)}, f32[7,2,2048]{2,1,0:T(2,128)S(1)}, u32[]{:S(2)}, u32[]{:S(2)}) collective-permute-start(f32[7,2,2048]{2,1,0:T(2,128)S(1)} %get-tuple-element.46), channel_id=1, source_target_pairs={{0,1},{1,0},{2,3},{3,2},{4,5},{5,4},{6,7},{7,6},{8,9},{9,8},{10,11... | collective-permute-start | bytes 344072 | tf_op jit(solution)/shard_map/ppermute | solution.py:528
  4.6 1.0 %collective-permute-done.refs_1_ = f32[7,2,2048]{2,1,0:T(2,128)S(1)} collective-permute-done((f32[7,2,2048]{2,1,0:T(2,128)S(1)}, f32[7,2,2048]{2,1,0:T(2,128)S(1)}, u32[]{:S(2)}, u32[]{:S(2)}) %collective-permute-start) | collective-permute-done | bytes 114720 | tf_op jit(solution)/shard_map/ppermute | solution.py:528
  5.6 0.2 %merge.1 = (f32[2,2,2048]{2,1,0:T(2,128)S(1)}, bf16[7,2,2048]{2,1,0:T(2,128)(2,1)S(1)}, f32[2,2,2048]{2,1,0:T(2,128)S(1)}, f32[2,2,2048]{2,1,0:T(2,128)S(1)}, f3...) custom-call(f32[7,2,2048]{2,1,0:T(2,128)S(1)} %get-tuple-element.45.refs_0_, ...), custom_call_target="tpu_custom_call" | custom-call | tf_op jit(solution)/shard_map/merge/pallas_call | solution.py:488
  5.8 2.9 %collective-permute-start.1 = (bf16[7,2,2048]{2,1,0:T(2,128)(2,1)S(1)}, bf16[7,2,2048]{2,1,0:T(2,128)(2,1)S(1)}, u32[]{:S(2)}, u32[]{:S(2)}) collective-permute-start(bf16[7,2,2048]{2,1,0:T(2,128)(2,1)S(1)} %get-tuple-element.51.refs_1_), channel_id=1, source_target_pairs={{0,2},{1,3},{2,0},{3,1},{4,6},{5,7},{6,4},{7,5},{8,10},{9,11},{10,... | collective-permute-start | bytes 172040 | tf_op jit(solution)/shard_map/ppermute | solution.py:528
  8.8 1.4 %local.3 = (f32[128,2048]{1,0:T(8,128)S(1)}, f32[128,2048]{1,0:T(8,128)S(1)}, f32[4,8,2048]{2,1,0:T(8,128)S(1)}) custom-call(f32[3,3,4096]{2,1,0:T(4,128)S(1)} %get-tuple-element.47.refs_3_.refs_0_.refs_5_.refs_4_, f32[2,2,4096]{2,1,0:T(2,128)S(1)} %get-tuple-element.48.refs_4_.refs_1_.refs_5_, f32[1,4096]{1,0:T(1,128)S(1)} %get-tuple-element.49.refs_5_.refs_2_.refs_6_, ...), custom_call_target="tpu_custom_call" | custom-call | tf_op jit(solution)/shard_map/local/pallas_call | solution.py:488
  10.2 0.8 %collective-permute-done.1.refs_2_ = bf16[7,2,2048]{2,1,0:T(2,128)(2,1)S(1)} collective-permute-done((bf16[7,2,2048]{2,1,0:T(2,128)(2,1)S(1)}, bf16[7,2,2048]{2,1,0:T(2,128)(2,1)S(1)}, u32[]{:S(2)}, u32[]{:S(2)}) %collective-permute-start.1) | collective-permute-done | bytes 57376 | tf_op jit(solution)/shard_map/ppermute | solution.py:528
  11.0 0.3 %join.2 = (f32[2,2,2048]{2,1,0:T(2,128)S(1)}, bf16[7,2,2048]{2,1,0:T(2,128)(2,1)S(1)}, bf16[2,2,2048]{2,1,0:T(2,128)(2,1)S(1)}, f32[2,2,2048]{2,1,0:T(2,128)S(1)...) custom-call(f32[2,2,2048]{2,1,0:T(2,128)S(1)} %get-tuple-element.50.refs_7_.refs_0_, ...), custom_call_target="tpu_custom_call" | custom-call | tf_op jit(solution)/shard_map/join/pallas_call | solution.py:488
  11.3 2.0 %collective-permute-start.2 = (bf16[7,2,2048]{2,1,0:T(2,128)(2,1)S(1)}, bf16[7,2,2048]{2,1,0:T(2,128)(2,1)S(1)}, u32[]{:S(2)}, u32[]{:S(2)}) collective-permute-start(bf16[7,2,2048]{2,1,0:T(2,128)(2,1)S(1)} %get-tuple-element.60.refs_1_), channel_id=1, source_target_pairs={{0,4},{1,5},{2,6},{3,7},{4,0},{5,1},{6,2},{7,3},{8,12},{9,13},{10,... | collective-permute-start | bytes 172040 | tf_op jit(solution)/shard_map/ppermute | solution.py:528
  13.4 0.7 %local.4 = (f32[128,1024]{1,0:T(8,128)S(1)}, f32[128,1024]{1,0:T(8,128)S(1)}, f32[4,8,1024]{2,1,0:T(8,128)S(1)}) custom-call(f32[3,3,4096]{2,1,0:T(4,128)S(1)} %get-tuple-element.47.refs_3_.refs_0_.refs_5_.refs_4_, f32[2,2,4096]{2,1,0:T(2,128)S(1)} %get-tuple-element.48.refs_4_.refs_1_.refs_5_, f32[1,4096]{1,0:T(1,128)S(1)} %get-tuple-element.49.refs_5_.refs_2_.refs_6_, ...), custom_call_target="tpu_custom_call" | custom-call | tf_op jit(solution)/shard_map/local/pallas_call | solution.py:488
  14.0 1.5 %collective-permute-done.2.refs_2_ = bf16[7,2,2048]{2,1,0:T(2,128)(2,1)S(1)} collective-permute-done((bf16[7,2,2048]{2,1,0:T(2,128)(2,1)S(1)}, bf16[7,2,2048]{2,1,0:T(2,128)(2,1)S(1)}, u32[]{:S(2)}, u32[]{:S(2)}) %collective-permute-start.2) | collective-permute-done | bytes 57376 | tf_op jit(solution)/shard_map/ppermute | solution.py:528
  15.5 0.3 %join.3 = (f32[2,2,2048]{2,1,0:T(2,128)S(1)}, bf16[5,2,2048]{2,1,0:T(2,128)(2,1)S(1)}, bf16[2,2,2048]{2,1,0:T(2,128)(2,1)S(1)}, f32[2,2,2048]{2,1,0:T(2,128)S(1)...) custom-call(f32[2,2,2048]{2,1,0:T(2,128)S(1)} %get-tuple-element.59.refs_7_.refs_0_, ...), custom_call_target="tpu_custom_call" | custom-call | tf_op jit(solution)/shard_map/join/pallas_call | solution.py:488
  15.8 3.1 %collective-permute-start.3 = (bf16[5,2,2048]{2,1,0:T(2,128)(2,1)S(1)}, bf16[5,2,2048]{2,1,0:T(2,128)(2,1)S(1)}, u32[]{:S(2)}, u32[]{:S(2)}) collective-permute-start(bf16[5,2,2048]{2,1,0:T(2,128)(2,1)S(1)} %get-tuple-element.66.refs_0_), channel_id=1, source_target_pairs={{0,8},{1,9},{2,10},{3,11},{4,12},{5,13},{6,14},{7,15},{8,0},{9,1},... | collective-permute-start | bytes 122888 | tf_op jit(solution)/shard_map/ppermute | solution.py:528
  18.9 0.7 %local.5 = (f32[128,1024]{1,0:T(8,128)S(1)}, f32[128,1024]{1,0:T(8,128)S(1)}, f32[4,8,1024]{2,1,0:T(8,128)S(1)}) custom-call(f32[3,3,4096]{2,1,0:T(4,128)S(1)} %get-tuple-element.47.refs_3_.refs_0_.refs_5_.refs_4_, f32[2,2,4096]{2,1,0:T(2,128)S(1)} %get-tuple-element.48.refs_4_.refs_1_.refs_5_, f32[1,4096]{1,0:T(1,128)S(1)} %get-tuple-element.49.refs_5_.refs_2_.refs_6_, ...), custom_call_target="tpu_custom_call" | custom-call | tf_op jit(solution)/shard_map/local/pallas_call | solution.py:488
  19.6 1.3 %collective-permute-done.3.refs_1_ = bf16[5,2,2048]{2,1,0:T(2,128)(2,1)S(1)} collective-permute-done((bf16[5,2,2048]{2,1,0:T(2,128)(2,1)S(1)}, bf16[5,2,2048]{2,1,0:T(2,128)(2,1)S(1)}, u32[]{:S(2)}, u32[]{:S(2)}) %collective-permute-start.3) | collective-permute-done | bytes 40992 | tf_op jit(solution)/shard_map/ppermute | solution.py:528
  20.8 0.2 last.1
  21.1 0.1 collective-permute-start.4
  21.2 0.8 %gate.1.refs_11_ = bf16[128,2048]{1,0:T(8,128)(2,1)S(1)} custom-call(f32[18,2,4096]{2,1,0:T(2,128)S(1)} %get-tuple-element.44.refs_2_.refs_3_.refs_4_.refs_0_, f32[4,2,2048]{2,1,0:T(2,128)S(1)} %get-tuple-element.82.refs_1_, f32[128,2048]{1,0:T(8,128)S(1)} %get-tuple-element.76.refs_2_, f32[128,2048]{1,0:T(8,128)S(1)} %get-tuple-element.77.refs_3_, ...), custom_call_target="tpu_custom_call" | custom-call | tf_op jit(solution)/shard_map/gate/pallas_call | solution.py:488
  22.0 0.4 %collective-permute-done.4.refs_1_ = f32[4,2,2048]{2,1,0:T(2,128)S(1)} collective-permute-done((f32[4,2,2048]{2,1,0:T(2,128)S(1)}, f32[4,2,2048]{2,1,0:T(2,128)S(1)}, u32[]{:S(2)}, u32[]{:S(2)}) %collective-permute-start.4) | collective-permute-done | bytes 65568 | tf_op jit(solution)/shard_map/ppermute | solution.py:528
  22.4 1.5 %finish.1 = bf16[128,4096]{1,0:T(8,128)(2,1)} custom-call(f32[18,2,4096]{2,1,0:T(2,128)S(1)} %get-tuple-element.44.refs_2_.refs_3_.refs_4_.refs_0_, f32[4,2,2048]{2,1,0:T(2,128)S(1)} %collective-permute-done.4.refs_1_, f32[128,2048]{1,0:T(8,128)S(1)} %get-tuple-element.76.refs_2_, f32[128,2048]{1,0:T(8,128)S(1)} %get-tuple-element.77.refs_3_, ...), custom_call_target="tpu_custom_call" | custom-call | tf_op jit(solution)/shard_map/finish/pallas_call | solution.py:488
  (1 shorter events, 0.0 us)
Async XLA Ops:
  4.1 1.5 %collective-permute-start = (f32[7,2,2048]{2,1,0:T(2,128)S(1)}, f32[7,2,2048]{2,1,0:T(2,128)S(1)}, u32[]{:S(2)}, u32[]{:S(2)}) collective-permute-start(f32[7,2,2048]{2,1,0:T(2,128)S(1)} %get-tuple-element.46), channel_id=1, source_target_pairs={{0,1},{1,0},{2,3},{3,2},{4,5},{5,4},{6,7},{7,6},{8,9},{9,8},{10,11... | collective-permute-start | bytes 344072 | tf_op jit(solution)/shard_map/ppermute | solution.py:528
  5.8 5.2 %collective-permute-start.1 = (bf16[7,2,2048]{2,1,0:T(2,128)(2,1)S(1)}, bf16[7,2,2048]{2,1,0:T(2,128)(2,1)S(1)}, u32[]{:S(2)}, u32[]{:S(2)}) collective-permute-start(bf16[7,2,2048]{2,1,0:T(2,128)(2,1)S(1)} %get-tuple-element.51.refs_1_), channel_id=1, source_target_pairs={{0,2},{1,3},{2,0},{3,1},{4,6},{5,7},{6,4},{7,5},{8,10},{9,11},{10,... | collective-permute-start | bytes 172040 | tf_op jit(solution)/shard_map/ppermute | solution.py:528
  11.3 4.2 %collective-permute-start.2 = (bf16[7,2,2048]{2,1,0:T(2,128)(2,1)S(1)}, bf16[7,2,2048]{2,1,0:T(2,128)(2,1)S(1)}, u32[]{:S(2)}, u32[]{:S(2)}) collective-permute-start(bf16[7,2,2048]{2,1,0:T(2,128)(2,1)S(1)} %get-tuple-element.60.refs_1_), channel_id=1, source_target_pairs={{0,4},{1,5},{2,6},{3,7},{4,0},{5,1},{6,2},{7,3},{8,12},{9,13},{10,... | collective-permute-start | bytes 172040 | tf_op jit(solution)/shard_map/ppermute | solution.py:528
  15.8 5.0 %collective-permute-start.3 = (bf16[5,2,2048]{2,1,0:T(2,128)(2,1)S(1)}, bf16[5,2,2048]{2,1,0:T(2,128)(2,1)S(1)}, u32[]{:S(2)}, u32[]{:S(2)}) collective-permute-start(bf16[5,2,2048]{2,1,0:T(2,128)(2,1)S(1)} %get-tuple-element.66.refs_0_), channel_id=1, source_target_pairs={{0,8},{1,9},{2,10},{3,11},{4,12},{5,13},{6,14},{7,15},{8,0},{9,1},... | collective-permute-start | bytes 122888 | tf_op jit(solution)/shard_map/ppermute | solution.py:528
  21.1 1.3 %collective-permute-start.4 = (f32[4,2,2048]{2,1,0:T(2,128)S(1)}, f32[4,2,2048]{2,1,0:T(2,128)S(1)}, u32[]{:S(2)}, u32[]{:S(2)}) collective-permute-start(f32[4,2,2048]{2,1,0:T(2,128)S(1)} %get-tuple-element.75), channel_id=1, source_target_pairs={{0,1},{1,0},{2,3},{3,2},{4,5},{5,4},{6,7},{7,6},{8,9},{9,8},{10,11... | collective-permute-start | bytes 196616 | tf_op jit(solution)/shard_map/ppermute | solution.py:528

commit v6 on v5

--- a/solution.py
+++ b/solution.py
@@ -11,6 +11,7 @@
 POLES = 2
 SUBROWS = 16
 LOCAL_CHUNK = 512
+STATES_CHUNK = 1024
 PARTS = (2, 1, 1)
 f32 = jnp.float32
 bf16 = jnp.bfloat16
@@ -116,29 +117,26 @@
 
 def states_kernel(angle_hbm, decay_hbm, taps_hbm, gain_hbm, skip_hbm, proj_ref,
                   prod_ref, scan_ref, keep_ref, give_ref, power_ref, taps_ref, gain_ref, skip_ref,
-                  q_ref, total_ref, order_ref, angle_ref, decay_ref, k_ref, v_ref, top_ref, end_ref, ks_ref, vs_ref,
+                  q_ref, total_ref, order_ref, angle_ref, decay_ref, kv_ref, ks_ref, vs_ref,
                   small_sem, in_sem, *, levels):
-    rows, channels = k_ref.shape
+    _, rows, channels = kv_ref.shape
     chunk = ks_ref.shape[1]
     count = channels // chunk
-    last = rows - SUBROWS
     smalls = [
         pltpu.make_async_copy(source, target, small_sem.at[i])
         for i, (source, target) in enumerate([
             (angle_hbm, angle_ref), (decay_hbm, decay_ref), (taps_hbm, taps_ref), (gain_hbm, gain_ref),
-            (skip_hbm, skip_ref), (proj_ref.at[pl.ds(1, 2), pl.ds(0, SUBROWS)], top_ref),
-            (proj_ref.at[:, pl.ds(last, SUBROWS)], end_ref), (proj_ref.at[0], q_ref)])
+            (skip_hbm, skip_ref), (proj_ref.at[0], q_ref)])
     ]
 
-    def fetch(i, which, ref):
+    def fetch(i):
         cols = span(i * chunk, chunk)
-        return pltpu.make_async_copy(proj_ref.at[which, :, cols], ref.at[:, cols], in_sem.at[which - 1, i])
+        return pltpu.make_async_copy(proj_ref.at[pl.ds(1, 2), :, cols], kv_ref.at[:, :, cols], in_sem.at[i])
 
     for copy in smalls[:3]:
         copy.start()
     for i in range(count):
-        fetch(i, 1, k_ref).start()
-        fetch(i, 2, v_ref).start()
+        fetch(i).start()
     for copy in smalls[3:]:
         copy.start()
     order_ref[...] = order_matrix(rows, False)
@@ -147,11 +145,10 @@
     fill_powers(power_ref, angle_ref, decay_ref, rows // SEGMENTS, levels)
 
     def body(i, _):
-        fetch(i, 1, k_ref).wait()
-        fetch(i, 2, v_ref).wait()
+        fetch(i).wait()
         at = span(i * chunk, chunk)
-        ks_ref[...] = jnp.dot(order_ref[...], k_ref[:, at], preferred_element_type=f32)
-        vs_ref[...] = jnp.dot(order_ref[...], v_ref[:, at], preferred_element_type=f32)
+        ks_ref[...] = jnp.dot(order_ref[...], kv_ref[0, :, at], preferred_element_type=f32)
+        vs_ref[...] = jnp.dot(order_ref[...], kv_ref[1, :, at], preferred_element_type=f32)
 
         def column(inner, outer):
             cols = slice(inner, inner + WIDTH)
@@ -188,10 +185,11 @@
     lax.fori_loop(0, count, body, 0)
     for copy in smalls[3:]:
         copy.wait()
-    for which in range(3):
-        total_ref[2 + which] = end_ref[which, SUBROWS - 2 : SUBROWS].astype(f32)
+    last = slice(rows - SUBROWS, rows)
+    for which, tail in enumerate((q_ref[last, :], kv_ref[0, last, :], kv_ref[1, last, :])):
+        total_ref[2 + which] = tail[SUBROWS - 2 :].astype(f32)
     for which in range(2):
-        total_ref[5 + which] = top_ref[which, 0:2].astype(f32)
+        total_ref[5 + which] = kv_ref[which, 0:2, :].astype(f32)
     own, other = halves(channels)
     keep_ref[...] = total_ref[:, :, own]
     give_ref[...] = total_ref[:, :, other]
@@ -322,6 +320,48 @@
         next_before_ref[i] = before[i].astype(bf16)
 
 
+def join_blocks(early, late, factor, back, taps):
+    extra = extra_state(first_products(early[2:5], late[5:7], taps), back)
+    begin = plus(early[0:2], extra)
+    return [*plus(times(factor, begin), late[0:2]), *late[2:5], *early[5:7]], begin
+
+
+def quad_kernel(ending_ref, sent_ref, near_ref, far_ref, both_ref, power_ref, taps_ref, lead_ref, enter_ref,
+                before_ref, after_ref, joined_ref, wire_ref, next_head_ref, next_lead_ref, next_enter_ref,
+                next_before_ref, *, level, channels):
+    device = lax.axis_index("seq")
+    half = halves(channels)[0]
+    back, taps = pair_at(power_ref, BACK, half), taps_ref[:, :, half]
+    near, far, both = ([*from_wire(ref), *planes_of(ref, 2, 7)] for ref in (near_ref, far_ref, both_ref))
+    mine = [*pair_at(ending_ref, 0, ALL), *planes_of(sent_ref, 2, 7)]
+    lead, enter, before = pair_at(lead_ref, 0, ALL), pair_at(enter_ref, 0, ALL), planes_of(before_ref, 0, 3)
+    upper = (device >> level) % 2 == 1
+    factor = pair_at(power_ref, SPAN + level, half)
+    other, _ = join_blocks(pick(upper, both, far), pick(upper, far, both), factor, back, taps)
+    for step in range(2):
+        upper = (device >> (level + step)) % 2 == 1
+        leads = jnp.logical_and(upper, (device % (1 << (level + step))) < 2)
+        factor = pair_at(power_ref, SPAN + level + step, half)
+        across = other if step else near
+        early = pick(upper, across, mine)
+        mine, begin = join_blocks(early, pick(upper, mine, across), factor, back, taps)
+        enter = pick(upper, plus(enter, times(lead, begin)), enter)
+        lead = pick(upper, times(lead, factor), lead)
+        before = pick(leads, early[2:5], before)
+    put_pair(joined_ref, 0, ALL, mine[0:2])
+    put_wire(wire_ref, mine[0:2])
+    for i in range(3):
+        wire_ref[2 + i] = mine[2 + i].astype(bf16)
+        next_before_ref[i] = before[i].astype(bf16)
+    for i in range(2):
+        head = mine[5 + i].astype(bf16)
+        next_head_ref[i] = head
+        if wire_ref.shape[0] > 5:
+            wire_ref[5 + i] = head
+    put_pair(next_lead_ref, 0, ALL, lead)
+    put_pair(next_enter_ref, 0, ALL, enter)
+
+
 def last_kernel(sent_ref, got_ref, head_ref, power_ref, taps_ref, gain_ref, skip_ref, lead_ref, enter_ref, before_ref,
                 base_ref, fix_ref, first_ref, after_ref, keep_ref, give_ref, *, level, channels):
     half = halves(channels)[0]
@@ -339,7 +379,7 @@
         give_ref[i] = jnp.where(odd, a, b)
 
 
-def local_kernel(taps_ref, gain_ref, skip_ref, power_ref, scan_ref, prod_ref, q_ref, after_ref,
+def local_kernel(taps_ref, gain_ref, skip_ref, power_ref, scan_ref, prod_ref, q_ref, after_ref, part_ref,
                  query_ref, local_ref, enter_ref, order_ref, qs_ref, *, base):
     rows, channels = query_ref.shape
     chunk = qs_ref.shape[1]
@@ -506,6 +546,7 @@
     arguments = [pltpu.with_memory_space_constraint(argument, pltpu.HBM) for argument in arguments]
     half = channels // 2
     local_chunk = min(LOCAL_CHUNK, channels)
+    wide_chunk = min(STATES_CHUNK, channels)
     square = pltpu.VMEM((rows, rows), bf16)
     dma = pltpu.SemaphoreType.DMA
 
@@ -519,18 +560,17 @@
          pairs(2 * (SPAN + levels), f32, channels), (short_taps.shape, f32), (residues.shape, f32),
          ((1, channels), f32), ((rows, channels), bf16)],
         [pltpu.VMEM(*pairs(7, f32, channels)), square]
-        + [pltpu.VMEM(pole_angles.shape, f32)] * 2 + [pltpu.VMEM((rows, channels), bf16)] * 2
-        + [pltpu.VMEM((2, SUBROWS, channels), bf16), pltpu.VMEM((3, SUBROWS, channels), bf16)]
-        + [pltpu.VMEM((rows, chunk), f32)] * 2 + [dma((8,)), dma((2, channels // chunk))],
+        + [pltpu.VMEM(pole_angles.shape, f32)] * 2 + [pltpu.VMEM((2, rows, channels), bf16)]
+        + [pltpu.VMEM((rows, wide_chunk), f32)] * 2 + [dma((6,)), dma((channels // wide_chunk,))],
         arguments, range(6), levels=levels)
 
-    def exchange(array, level):
-        return lax.ppermute(array, "seq", [(i, i ^ (1 << level)) for i in range(devices)])
+    def exchange(array, mask):
+        return lax.ppermute(array, "seq", [(i, i ^ mask) for i in range(devices)])
 
     def message(level):
         return pairs(5 if level == levels - 1 else 7, bf16)
 
-    got = exchange(give, 0)
+    got = exchange(give, 1)
     ending, sent, lead, enter, base, fix, first = kernel_call(
         merge_kernel, "merge", [state, pairs(7, bf16), state, state, state, state, pairs(2, bf16)], [],
         [keep, got, powers, taps, gains, skip], (), channels=channels)
@@ -538,28 +578,41 @@
     before = jnp.zeros(*pairs(3, bf16))
 
     tables = []
-    start = 0
-    for level in range(1, levels):
-        got = exchange(sent, level)
-        while len(tables) < len(parts) and (len(tables) < level or level == levels - 1):
+
+    def run_local(until):
+        while len(tables) < min(until, len(parts)):
             part = parts[len(tables)]
             plane = ((rows, part), f32)
             tables.append(kernel_call(
                 local_kernel, "local", [plane, plane, ((4, SEGMENTS, part), f32)],
                 [square, pltpu.VMEM((rows, local_chunk), f32)],
-                [taps, gains, skip, powers, scan, products, query_rows, ending], (), base=start))
-            start += part
-        after = tables[-1][2]
-        if level + 1 < levels:
+                [taps, gains, skip, powers, scan, products, query_rows, ending, tables[-1][2] if tables else ending], (7, 8), base=sum(parts[: len(tables)])))
+        return tables[-1][2]
+
+    level = 1
+    if levels > 3:
+        near, far, both = (exchange(sent, mask << level) for mask in (1, 2, 3))
+        after = run_local(2)
+        level = 3
+        ending, sent, head, lead, enter, before = kernel_call(
+            quad_kernel, "quad", [state, message(level), pairs(2, bf16), state, state, pairs(3, bf16)], [],
+            [ending, sent, near, far, both, powers, taps, lead, enter, before, after], (10,),
+            level=1, channels=channels)
+    while level < levels:
+        got = exchange(sent, 1 << level)
+        after = run_local(len(parts) if level == levels - 1 else level)
+        level += 1
+        if level < levels:
             ending, sent, head, lead, enter, before = kernel_call(
-                join_kernel, "join", [state, message(level + 1), pairs(2, bf16), state, state, pairs(3, bf16)], [],
-                [ending, sent, got, head, powers, taps, lead, enter, before, after], (9,), level=level, channels=channels)
+                join_kernel, "join", [state, message(level), pairs(2, bf16), state, state, pairs(3, bf16)], [],
+                [ending, sent, got, head, powers, taps, lead, enter, before, after], (9,), level=level - 1,
+                channels=channels)
 
     keep, give = kernel_call(
         last_kernel, "last", [pairs(4)] * 2, [],
         [sent, got, head, powers, taps, gains, skip, lead, enter, before, base, fix, first, after], (13,),
         level=levels - 1, channels=channels)
-    got = exchange(give, 0)
+    got = exchange(give, 1)
     flat = [array for table in tables for array in table]
     half_plane = ((rows, half), bf16)
     scratch = [square, pltpu.VMEM(*half_plane), pltpu.VMEM((rows, chunk), bf16), dma((half // chunk + 1,))]

time: 24 us -> 22.9 us (0.954)
  starting transfers between devices: 8.68 us -> 7.87 us
    ppermute x5 -> x6, starting transfers between devices: 8.68 us -> 7.87 us  [exchange(): return lax.ppermute(array, 'seq', [(i, i ^ mask) for i in range(devices)])]
    ppermute x5 -> x6, waiting for transfers between devices: 4.97 us -> 4.83 us  [exchange(): return lax.ppermute(array, 'seq', [(i, i ^ mask) for i in range(devices)])]
    pallas_call x10 -> x9, Pallas kernels: 10.1 us -> 10 us  [kernel_call(): pl.pallas_call(bound, in_specs=[spec(i in in_hbm) for i in range(len(oper...]
  transfers between devices with their start and end apart: 5 -> 6, of which waited for: 5 -> 5; matrix products, arithmetic and copies ran while one was open for 0% -> 0% of each run, Pallas kernels for 15% -> 16%
where the time goes in v6:
time: 22.9 us; the launch traced here: 22.8 us
  Pallas kernels  10 us (44%)
  starting transfers between devices  7.87 us (34%)
  waiting for transfers between devices  4.83 us (21%)
    pallas_call x9, Pallas kernels, kernel_call(): pl.pallas_call(bound, in_specs=[spec(i in in_hbm) for i in range(len(oper...  10 us
    ppermute x6, starting transfers between devices, exchange(): return lax.ppermute(array, 'seq', [(i, i ^ mask) for i in range(devices)])  7.87 us
    ppermute x6, waiting for transfers between devices, exchange(): return lax.ppermute(array, 'seq', [(i, i ^ mask) for i in range(devices)])  4.83 us
  transfers between devices with their start and end apart: 6, of which 5 were waited for; matrix products, arithmetic and copies ran while one was open for 0% of the time, Pallas kernels for 16%

profile of v6, /device:TPU:0, one launch (start us, length us, event | category | flops | bytes accessed | tf_op | source)
XLA Modules:
  0.0 22.8 jit_solution(3500445197030419006)
XLA Ops:
  0.0 3.9 %states.1 = (bf16[128,4096]{1,0:T(8,128)(2,1)S(1)}, f32[4,8,4096]{2,1,0:T(8,128)S(1)}, f32[7,2,2048]{2,1,0:T(2,128)S(1)}, f32[7,2,2048]{2,1,0:T(2,128)S(1)}, f32...) custom-call(f32[2,4096]{1,0:T(2,128)} %refs_0_.1, ...), custom_call_target="tpu_custom_call" | custom-call | tf_op jit(solution)/shard_map/states/pallas_call | solution.py:528
  3.9 0.6 %collective-permute-start = (f32[7,2,2048]{2,1,0:T(2,128)S(1)}, f32[7,2,2048]{2,1,0:T(2,128)S(1)}, u32[]{:S(2)}, u32[]{:S(2)}) collective-permute-start(f32[7,2,2048]{2,1,0:T(2,128)S(1)} %get-tuple-element.40), channel_id=1, source_target_pairs={{0,1},{1,0},{2,3},{3,2},{4,5},{5,4},{6,7},{7,6},{8,9},{9,8},{10,11... | collective-permute-start | bytes 344072 | tf_op jit(solution)/shard_map/ppermute | solution.py:568
  4.5 1.0 %collective-permute-done.refs_1_ = f32[7,2,2048]{2,1,0:T(2,128)S(1)} collective-permute-done((f32[7,2,2048]{2,1,0:T(2,128)S(1)}, f32[7,2,2048]{2,1,0:T(2,128)S(1)}, u32[]{:S(2)}, u32[]{:S(2)}) %collective-permute-start) | collective-permute-done | bytes 114720 | tf_op jit(solution)/shard_map/ppermute | solution.py:568
  5.5 0.2 %merge.1 = (f32[2,2,2048]{2,1,0:T(2,128)S(1)}, bf16[7,2,2048]{2,1,0:T(2,128)(2,1)S(1)}, f32[2,2,2048]{2,1,0:T(2,128)S(1)}, f32[2,2,2048]{2,1,0:T(2,128)S(1)}, f3...) custom-call(f32[7,2,2048]{2,1,0:T(2,128)S(1)} %get-tuple-element.39.refs_0_, ...), custom_call_target="tpu_custom_call" | custom-call | tf_op jit(solution)/shard_map/merge/pallas_call | solution.py:528
  5.7 3.9 %collective-permute-start.3 = (bf16[7,2,2048]{2,1,0:T(2,128)(2,1)S(1)}, bf16[7,2,2048]{2,1,0:T(2,128)(2,1)S(1)}, u32[]{:S(2)}, u32[]{:S(2)}) collective-permute-start(bf16[7,2,2048]{2,1,0:T(2,128)(2,1)S(1)} %get-tuple-element.45.refs_1_), channel_id=1, source_target_pairs={{0,6},{1,7},{2,4},{3,5},{4,2},{5,3},{6,0},{7,1},{8,14},{9,15},{10,... | collective-permute-start | bytes 172040 | tf_op jit(solution)/shard_map/ppermute | solution.py:568
  9.7 0.4 %collective-permute-start.2 = (bf16[7,2,2048]{2,1,0:T(2,128)(2,1)S(1)}, bf16[7,2,2048]{2,1,0:T(2,128)(2,1)S(1)}, u32[]{:S(2)}, u32[]{:S(2)}) collective-permute-start(bf16[7,2,2048]{2,1,0:T(2,128)(2,1)S(1)} %get-tuple-element.45.refs_1_), channel_id=1, source_target_pairs={{0,4},{1,5},{2,6},{3,7},{4,0},{5,1},{6,2},{7,3},{8,12},{9,13},{10,... | collective-permute-start | bytes 172040 | tf_op jit(solution)/shard_map/ppermute | solution.py:568
  10.1 0.2 collective-permute-start.1
  10.3 1.4 %local.3 = (f32[128,2048]{1,0:T(8,128)S(1)}, f32[128,2048]{1,0:T(8,128)S(1)}, f32[4,8,2048]{2,1,0:T(8,128)S(1)}) custom-call(f32[3,3,4096]{2,1,0:T(4,128)S(1)} %get-tuple-element.41.refs_3_.refs_0_.refs_6_.refs_4_, f32[2,2,4096]{2,1,0:T(2,128)S(1)} %get-tuple-element.42.refs_4_.refs_1_.refs_5_, f32[1,4096]{1,0:T(1,128)S(1)} %get-tuple-element.43.refs_5_.refs_2_.refs_6_, ...), custom_call_target="tpu_custom_call" | custom-call | tf_op jit(solution)/shard_map/local/pallas_call | solution.py:528
  11.7 0.7 %local.4 = (f32[128,1024]{1,0:T(8,128)S(1)}, f32[128,1024]{1,0:T(8,128)S(1)}, f32[4,8,1024]{2,1,0:T(8,128)S(1)}) custom-call(f32[3,3,4096]{2,1,0:T(4,128)S(1)} %get-tuple-element.41.refs_3_.refs_0_.refs_6_.refs_4_, f32[2,2,4096]{2,1,0:T(2,128)S(1)} %get-tuple-element.42.refs_4_.refs_1_.refs_5_, f32[1,4096]{1,0:T(1,128)S(1)} %get-tuple-element.43.refs_5_.refs_2_.refs_6_, ...), custom_call_target="tpu_custom_call" | custom-call | tf_op jit(solution)/shard_map/local/pallas_call | solution.py:528
  12.4 0.0 collective-permute-done.3.refs_4_
  12.4 1.4 %collective-permute-done.2.refs_3_ = bf16[7,2,2048]{2,1,0:T(2,128)(2,1)S(1)} collective-permute-done((bf16[7,2,2048]{2,1,0:T(2,128)(2,1)S(1)}, bf16[7,2,2048]{2,1,0:T(2,128)(2,1)S(1)}, u32[]{:S(2)}, u32[]{:S(2)}) %collective-permute-start.2) | collective-permute-done | bytes 57376 | tf_op jit(solution)/shard_map/ppermute | solution.py:568
  13.8 0.4 %collective-permute-done.1.refs_2_ = bf16[7,2,2048]{2,1,0:T(2,128)(2,1)S(1)} collective-permute-done((bf16[7,2,2048]{2,1,0:T(2,128)(2,1)S(1)}, bf16[7,2,2048]{2,1,0:T(2,128)(2,1)S(1)}, u32[]{:S(2)}, u32[]{:S(2)}) %collective-permute-start.1) | collective-permute-done | bytes 57376 | tf_op jit(solution)/shard_map/ppermute | solution.py:568
  14.3 0.5 %quad.1 = (f32[2,2,2048]{2,1,0:T(2,128)S(1)}, bf16[5,2,2048]{2,1,0:T(2,128)(2,1)S(1)}, bf16[2,2,2048]{2,1,0:T(2,128)(2,1)S(1)}, f32[2,2,2048]{2,1,0:T(2,128)S(1)...) custom-call(f32[2,2,2048]{2,1,0:T(2,128)S(1)} %get-tuple-element.44.refs_7_.refs_8_.refs_0_, ...), custom_call_target="tpu_custom_call" | custom-call | tf_op jit(solution)/shard_map/quad/pallas_call | solution.py:528
  14.8 2.7 %collective-permute-start.4 = (bf16[5,2,2048]{2,1,0:T(2,128)(2,1)S(1)}, bf16[5,2,2048]{2,1,0:T(2,128)(2,1)S(1)}, u32[]{:S(2)}, u32[]{:S(2)}) collective-permute-start(bf16[5,2,2048]{2,1,0:T(2,128)(2,1)S(1)} %get-tuple-element.53.refs_0_), channel_id=1, source_target_pairs={{0,8},{1,9},{2,10},{3,11},{4,12},{5,13},{6,14},{7,15},{8,0},{9,1},... | collective-permute-start | bytes 122888 | tf_op jit(solution)/shard_map/ppermute | solution.py:568
  17.5 0.7 %local.5 = (f32[128,1024]{1,0:T(8,128)S(1)}, f32[128,1024]{1,0:T(8,128)S(1)}, f32[4,8,1024]{2,1,0:T(8,128)S(1)}) custom-call(f32[3,3,4096]{2,1,0:T(4,128)S(1)} %get-tuple-element.41.refs_3_.refs_0_.refs_6_.refs_4_, f32[2,2,4096]{2,1,0:T(2,128)S(1)} %get-tuple-element.42.refs_4_.refs_1_.refs_5_, f32[1,4096]{1,0:T(1,128)S(1)} %get-tuple-element.43.refs_5_.refs_2_.refs_6_, ...), custom_call_target="tpu_custom_call" | custom-call | tf_op jit(solution)/shard_map/local/pallas_call | solution.py:528
  18.2 1.6 %collective-permute-done.4.refs_1_ = bf16[5,2,2048]{2,1,0:T(2,128)(2,1)S(1)} collective-permute-done((bf16[5,2,2048]{2,1,0:T(2,128)(2,1)S(1)}, bf16[5,2,2048]{2,1,0:T(2,128)(2,1)S(1)}, u32[]{:S(2)}, u32[]{:S(2)}) %collective-permute-start.4) | collective-permute-done | bytes 40992 | tf_op jit(solution)/shard_map/ppermute | solution.py:568
  19.8 0.2 %last.1 = (f32[4,2,2048]{2,1,0:T(2,128)S(1)}, f32[4,2,2048]{2,1,0:T(2,128)S(1)}) custom-call(bf16[5,2,2048]{2,1,0:T(2,128)(2,1)S(1)} %get-tuple-element.53.refs_0_, bf16[5,2,2048]{2,1,0:T(2,128)(2,1)S(1)} %collective-permute-done.4.refs_1_, bf16[2,2,2048]{2,1,0:T(2,128)(2,1)S(1)} %get-tuple-element.54.refs_2_, ...), custom_call_target="tpu_custom_call" | custom-call | tf_op jit(solution)/shard_map/last/pallas_call | solution.py:528
  20.0 0.1 collective-permute-start.5
  20.1 0.8 %gate.1.refs_11_ = bf16[128,2048]{1,0:T(8,128)(2,1)S(1)} custom-call(f32[18,2,4096]{2,1,0:T(2,128)S(1)} %get-tuple-element.38.refs_2_.refs_3_.refs_5_.refs_0_, f32[4,2,2048]{2,1,0:T(2,128)S(1)} %get-tuple-element.70.refs_1_, f32[128,2048]{1,0:T(8,128)S(1)} %get-tuple-element.64.refs_2_, f32[128,2048]{1,0:T(8,128)S(1)} %get-tuple-element.65.refs_3_, ...), custom_call_target="tpu_custom_call" | custom-call | tf_op jit(solution)/shard_map/gate/pallas_call | solution.py:528
  20.9 0.4 %collective-permute-done.5.refs_1_ = f32[4,2,2048]{2,1,0:T(2,128)S(1)} collective-permute-done((f32[4,2,2048]{2,1,0:T(2,128)S(1)}, f32[4,2,2048]{2,1,0:T(2,128)S(1)}, u32[]{:S(2)}, u32[]{:S(2)}) %collective-permute-start.5) | collective-permute-done | bytes 65568 | tf_op jit(solution)/shard_map/ppermute | solution.py:568
  21.3 1.5 %finish.1 = bf16[128,4096]{1,0:T(8,128)(2,1)} custom-call(f32[18,2,4096]{2,1,0:T(2,128)S(1)} %get-tuple-element.38.refs_2_.refs_3_.refs_5_.refs_0_, f32[4,2,2048]{2,1,0:T(2,128)S(1)} %collective-permute-done.5.refs_1_, f32[128,2048]{1,0:T(8,128)S(1)} %get-tuple-element.64.refs_2_, f32[128,2048]{1,0:T(8,128)S(1)} %get-tuple-element.65.refs_3_, ...), custom_call_target="tpu_custom_call" | custom-call | tf_op jit(solution)/shard_map/finish/pallas_call | solution.py:528
  (1 shorter events, 0.0 us)
Async XLA Ops:
  3.9 1.5 %collective-permute-start = (f32[7,2,2048]{2,1,0:T(2,128)S(1)}, f32[7,2,2048]{2,1,0:T(2,128)S(1)}, u32[]{:S(2)}, u32[]{:S(2)}) collective-permute-start(f32[7,2,2048]{2,1,0:T(2,128)S(1)} %get-tuple-element.40), channel_id=1, source_target_pairs={{0,1},{1,0},{2,3},{3,2},{4,5},{5,4},{6,7},{7,6},{8,9},{9,8},{10,11... | collective-permute-start | bytes 344072 | tf_op jit(solution)/shard_map/ppermute | solution.py:568
  5.7 6.7 %collective-permute-start.3 = (bf16[7,2,2048]{2,1,0:T(2,128)(2,1)S(1)}, bf16[7,2,2048]{2,1,0:T(2,128)(2,1)S(1)}, u32[]{:S(2)}, u32[]{:S(2)}) collective-permute-start(bf16[7,2,2048]{2,1,0:T(2,128)(2,1)S(1)} %get-tuple-element.45.refs_1_), channel_id=1, source_target_pairs={{0,6},{1,7},{2,4},{3,5},{4,2},{5,3},{6,0},{7,1},{8,14},{9,15},{10,... | collective-permute-start | bytes 172040 | tf_op jit(solution)/shard_map/ppermute | solution.py:568
  9.7 4.2 %collective-permute-start.2 = (bf16[7,2,2048]{2,1,0:T(2,128)(2,1)S(1)}, bf16[7,2,2048]{2,1,0:T(2,128)(2,1)S(1)}, u32[]{:S(2)}, u32[]{:S(2)}) collective-permute-start(bf16[7,2,2048]{2,1,0:T(2,128)(2,1)S(1)} %get-tuple-element.45.refs_1_), channel_id=1, source_target_pairs={{0,4},{1,5},{2,6},{3,7},{4,0},{5,1},{6,2},{7,3},{8,12},{9,13},{10,... | collective-permute-start | bytes 172040 | tf_op jit(solution)/shard_map/ppermute | solution.py:568
  10.1 4.2 %collective-permute-start.1 = (bf16[7,2,2048]{2,1,0:T(2,128)(2,1)S(1)}, bf16[7,2,2048]{2,1,0:T(2,128)(2,1)S(1)}, u32[]{:S(2)}, u32[]{:S(2)}) collective-permute-start(bf16[7,2,2048]{2,1,0:T(2,128)(2,1)S(1)} %get-tuple-element.45.refs_1_), channel_id=1, source_target_pairs={{0,2},{1,3},{2,0},{3,1},{4,6},{5,7},{6,4},{7,5},{8,10},{9,11},{10,... | collective-permute-start | bytes 172040 | tf_op jit(solution)/shard_map/ppermute | solution.py:568
  14.8 5.0 %collective-permute-start.4 = (bf16[5,2,2048]{2,1,0:T(2,128)(2,1)S(1)}, bf16[5,2,2048]{2,1,0:T(2,128)(2,1)S(1)}, u32[]{:S(2)}, u32[]{:S(2)}) collective-permute-start(bf16[5,2,2048]{2,1,0:T(2,128)(2,1)S(1)} %get-tuple-element.53.refs_0_), channel_id=1, source_target_pairs={{0,8},{1,9},{2,10},{3,11},{4,12},{5,13},{6,14},{7,15},{8,0},{9,1},... | collective-permute-start | bytes 122888 | tf_op jit(solution)/shard_map/ppermute | solution.py:568
  20.0 1.3 %collective-permute-start.5 = (f32[4,2,2048]{2,1,0:T(2,128)S(1)}, f32[4,2,2048]{2,1,0:T(2,128)S(1)}, u32[]{:S(2)}, u32[]{:S(2)}) collective-permute-start(f32[4,2,2048]{2,1,0:T(2,128)S(1)} %get-tuple-element.63), channel_id=1, source_target_pairs={{0,1},{1,0},{2,3},{3,2},{4,5},{5,4},{6,7},{7,6},{8,9},{9,8},{10,11... | collective-permute-start | bytes 196616 | tf_op jit(solution)/shard_map/ppermute | solution.py:568

commit v7 on v6

--- a/solution.py
+++ b/solution.py
@@ -12,7 +12,7 @@
 SUBROWS = 16
 LOCAL_CHUNK = 512
 STATES_CHUNK = 1024
-PARTS = (2, 1, 1)
+PARTS = ((False, 0, 2), (True, 0, 1), (True, 1, 1))
 f32 = jnp.float32
 bf16 = jnp.bfloat16
 
@@ -115,44 +115,26 @@
         body(part * WIDTH, chunk_index * chunk + part * WIDTH)
 
 
-def states_kernel(angle_hbm, decay_hbm, taps_hbm, gain_hbm, skip_hbm, proj_ref,
-                  prod_ref, scan_ref, keep_ref, give_ref, power_ref, taps_ref, gain_ref, skip_ref,
-                  q_ref, total_ref, order_ref, angle_ref, decay_ref, kv_ref, ks_ref, vs_ref,
-                  small_sem, in_sem, *, levels):
-    _, rows, channels = kv_ref.shape
+def side_start(theirs, half):
+    odd = lax.axis_index("seq") % 2
+    return (1 - odd if theirs else odd) * half
+
+
+def half_states(ready, begin, order_ref, power_ref, taps_ref, kv_ref, q_ref, prod_ref, scan_ref, block_ref, ks_ref, vs_ref):
+    _, rows, _ = kv_ref.shape
+    half = prod_ref.shape[1]
     chunk = ks_ref.shape[1]
-    count = channels // chunk
-    smalls = [
-        pltpu.make_async_copy(source, target, small_sem.at[i])
-        for i, (source, target) in enumerate([
-            (angle_hbm, angle_ref), (decay_hbm, decay_ref), (taps_hbm, taps_ref), (gain_hbm, gain_ref),
-            (skip_hbm, skip_ref), (proj_ref.at[0], q_ref)])
-    ]
-
-    def fetch(i):
-        cols = span(i * chunk, chunk)
-        return pltpu.make_async_copy(proj_ref.at[pl.ds(1, 2), :, cols], kv_ref.at[:, :, cols], in_sem.at[i])
-
-    for copy in smalls[:3]:
-        copy.start()
-    for i in range(count):
-        fetch(i).start()
-    for copy in smalls[3:]:
-        copy.start()
-    order_ref[...] = order_matrix(rows, False)
-    for copy in smalls[:3]:
-        copy.wait()
-    fill_powers(power_ref, angle_ref, decay_ref, rows // SEGMENTS, levels)
 
     def body(i, _):
-        fetch(i).wait()
-        at = span(i * chunk, chunk)
+        ready(i)
+        at = span(begin + i * chunk, chunk)
         ks_ref[...] = jnp.dot(order_ref[...], kv_ref[0, :, at], preferred_element_type=f32)
         vs_ref[...] = jnp.dot(order_ref[...], kv_ref[1, :, at], preferred_element_type=f32)
 
         def column(inner, outer):
             cols = slice(inner, inner + WIDTH)
-            here = span(outer, WIDTH)
+            here = span(begin + outer, WIDTH)
+            put = span(outer, WIDTH)
             keys = short_filter(steps_of(ks_ref, cols), taps_ref, 1, here)
             values = short_filter(steps_of(vs_ref, cols), taps_ref, 2, here)
             products = [a * b for a, b in zip(keys, values)]
@@ -160,7 +142,7 @@
                 products[j] = jnp.where(first_mask(), 0.0, products[j])
             for j in range(0, len(products), 2):
                 both = jnp.concatenate(products[j : j + 2], axis=0)
-                prod_ref[SEGMENTS * j : SEGMENTS * (j + 2), here] = both.astype(bf16)
+                prod_ref[SEGMENTS * j : SEGMENTS * (j + 2), put] = both.astype(bf16)
             sublane = lax.broadcasted_iota(jnp.int32, (SEGMENTS, WIDTH), 0)
             for pole in range(POLES):
                 lam = pole_at(power_ref, LAM, pole, here)
@@ -176,23 +158,70 @@
                     moved = tuple(jnp.where(sublane >= by, pltpu.roll(part, by, 0), 0.0) for part in state)
                     state = plus(state, times(factor, moved))
                 for part in range(2):
-                    scan_ref[2 * part + pole, :, here] = state[part]
-                    total_ref[part, pole : pole + 1, here] = state[part][SEGMENTS - 1 :]
+                    scan_ref[2 * part + pole, :, put] = state[part]
+                    block_ref[part, pole : pole + 1, put] = state[part][SEGMENTS - 1 :]
 
         loop_columns(i, chunk, column)
         return 0
 
-    lax.fori_loop(0, count, body, 0)
+    lax.fori_loop(0, half // chunk, body, 0)
+
+
+def put_edges(begin, kv_ref, q_ref, block_ref):
+    _, rows, _ = kv_ref.shape
+    here = span(begin, block_ref.shape[2])
+    last = slice(rows - SUBROWS, rows)
+    for which, tail in enumerate((q_ref[last, here], kv_ref[0, last, here], kv_ref[1, last, here])):
+        block_ref[2 + which] = tail[SUBROWS - 2 :].astype(f32)
+    for which in range(2):
+        block_ref[5 + which] = kv_ref[which, 0:SUBROWS, here][0:2].astype(f32)
+
+
+def first_kernel(angle_hbm, decay_hbm, taps_hbm, gain_hbm, skip_hbm, proj_ref,
+                 prod_ref, scan_ref, give_ref, power_ref, taps_ref, gain_ref, skip_ref, kv_ref, q_ref,
+                 order_ref, angle_ref, decay_ref, ks_ref, vs_ref, small_sem, in_sem, *, levels):
+    _, rows, channels = kv_ref.shape
+    half = channels // 2
+    chunk = ks_ref.shape[1]
+    count = half // chunk
+    begin, rest = side_start(True, half), side_start(False, half)
+    smalls = [
+        pltpu.make_async_copy(source, target, small_sem.at[i])
+        for i, (source, target) in enumerate([
+            (angle_hbm, angle_ref), (decay_hbm, decay_ref), (taps_hbm, taps_ref), (proj_ref.at[0], q_ref),
+            (gain_hbm, gain_ref), (skip_hbm, skip_ref)])
+    ]
+
+    def fetch(start, size, which):
+        cols = span(start, size)
+        return pltpu.make_async_copy(proj_ref.at[pl.ds(1, 2), :, cols], kv_ref.at[:, :, cols], in_sem.at[which])
+
+    for copy in smalls[:3]:
+        copy.start()
+    for i in range(count):
+        fetch(begin + i * chunk, chunk, i).start()
+    for copy in smalls[3:]:
+        copy.start()
+    fetch(rest, half, count).start()
+    order_ref[...] = order_matrix(rows, False)
+    for copy in smalls[:3]:
+        copy.wait()
+    fill_powers(power_ref, angle_ref, decay_ref, rows // SEGMENTS, levels)
+    half_states(lambda i: fetch(begin + i * chunk, chunk, i).wait(), begin, order_ref, power_ref, taps_ref,
+                kv_ref, q_ref, prod_ref, scan_ref, give_ref, ks_ref, vs_ref)
     for copy in smalls[3:]:
         copy.wait()
-    last = slice(rows - SUBROWS, rows)
-    for which, tail in enumerate((q_ref[last, :], kv_ref[0, last, :], kv_ref[1, last, :])):
-        total_ref[2 + which] = tail[SUBROWS - 2 :].astype(f32)
-    for which in range(2):
-        total_ref[5 + which] = kv_ref[which, 0:2, :].astype(f32)
-    own, other = halves(channels)
-    keep_ref[...] = total_ref[:, :, own]
-    give_ref[...] = total_ref[:, :, other]
+    fetch(rest, half, count).wait()
+    put_edges(begin, kv_ref, q_ref, give_ref)
+
+
+def second_kernel(power_ref, taps_ref, kv_ref, q_ref, prod_ref, scan_ref, keep_ref, order_ref, ks_ref, vs_ref):
+    _, rows, channels = kv_ref.shape
+    begin = side_start(False, channels // 2)
+    order_ref[...] = order_matrix(rows, False)
+    half_states(lambda i: None, begin, order_ref, power_ref, taps_ref, kv_ref, q_ref, prod_ref, scan_ref, keep_ref,
+                ks_ref, vs_ref)
+    put_edges(begin, kv_ref, q_ref, keep_ref)
 
 
 def halves(channels):
@@ -380,24 +409,26 @@
 
 
 def local_kernel(taps_ref, gain_ref, skip_ref, power_ref, scan_ref, prod_ref, q_ref, after_ref, part_ref,
-                 query_ref, local_ref, enter_ref, order_ref, qs_ref, *, base):
+                 query_ref, local_ref, enter_ref, order_ref, qs_ref, *, theirs, base):
     rows, channels = query_ref.shape
+    begin = side_start(theirs, prod_ref.shape[1]) + base
     chunk = qs_ref.shape[1]
     order_ref[...] = order_matrix(rows, False)
 
     def body(i, _):
-        qs_ref[...] = jnp.dot(order_ref[...], q_ref[:, span(base + i * chunk, chunk)], preferred_element_type=f32)
+        qs_ref[...] = jnp.dot(order_ref[...], q_ref[:, span(begin + i * chunk, chunk)], preferred_element_type=f32)
 
         def column(inner, outer):
             cols = slice(inner, inner + WIDTH)
             put = span(outer, WIDTH)
-            here = span(base + outer, WIDTH)
+            here = span(begin + outer, WIDTH)
+            take = span(base + outer, WIDTH)
             queries = short_filter(steps_of(qs_ref, cols), taps_ref, 0, here)
             for j, value in enumerate(queries):
                 query_ref[SEGMENTS * j : SEGMENTS * (j + 1), put] = value
             products = []
             for j in range(0, len(queries), 2):
-                both = prod_ref[SEGMENTS * j : SEGMENTS * (j + 2), here].astype(f32)
+                both = prod_ref[SEGMENTS * j : SEGMENTS * (j + 2), take].astype(f32)
                 products += [both[:SEGMENTS], both[SEGMENTS:]]
             before = delayed(products[-1])
             skip = wide(skip_ref[0:1, here])
@@ -409,7 +440,7 @@
                 gain = tuple(wide(gain_ref[part, pole : pole + 1, here]) for part in range(2))
                 a1, a2 = feedback(lam)
                 b1 = gain[0] * lam[0] + gain[1] * lam[1]
-                carry = tuple(delayed(scan_ref[2 * part + pole, :, here]) for part in range(2))
+                carry = tuple(delayed(scan_ref[2 * part + pole, :, take]) for part in range(2))
                 gain_back = times(gain, back)
                 y1 = gain[0] * carry[0] - gain[1] * carry[1]
                 y2 = gain_back[0] * (carry[0] - before) - gain_back[1] * carry[1]
@@ -447,10 +478,8 @@
         out_ref, order_ref, gated_ref = rest
     half = out_ref.shape[1]
     chunk = gated_ref.shape[1]
-    own, other = halves(2 * half)
-    odd = lax.axis_index("seq") % 2
-    side = 1 - odd if ready else odd
-    begin = side * half
+    own = halves(2 * half)[0]
+    begin = side_start(ready, half)
 
     def send(i):
         place = span(i * chunk, chunk)
@@ -467,8 +496,8 @@
             def column(inner, outer):
                 cols = slice(inner, inner + WIDTH)
                 take = span(outer, WIDTH)
-                there = span(base % half + outer, WIDTH)
-                here = span(base + outer, WIDTH)
+                there = span(base + outer, WIDTH)
+                here = span(begin + base + outer, WIDTH)
                 queries = steps_of(query_ref, take)
                 local = steps_of(local_ref, take)
                 for j in range(2):
@@ -495,7 +524,7 @@
                         gated_ref[SEGMENTS * (j - 1) : SEGMENTS * (j + 1), cols] = both.astype(bf16)
 
             loop_columns(i, chunk, column)
-            place = base % half // chunk + i
+            place = base // chunk + i
             out_ref[:, span(place * chunk, chunk)] = jnp.dot(
                 order_ref[...], gated_ref[...], preferred_element_type=f32).astype(bf16)
             if ready:
@@ -506,11 +535,7 @@
 
     base = 0
     for index, part in enumerate(parts):
-
-        @pl.when(side == base // half)
-        def _(base=base, part=part, refs=tables[3 * index : 3 * index + 3]):
-            gate_part(base, part, *refs)
-
+        gate_part(base, part, *tables[3 * index : 3 * index + 3])
         base += part
     if ready:
         for i in range(half // chunk):
@@ -541,7 +566,6 @@
     chunk = min(CHUNK, channels)
     devices = lax.axis_size("seq")
     levels = devices.bit_length() - 1
-    parts = [channels // sum(PARTS) * share for share in PARTS]
     arguments = [pole_angles, decay_rates, short_taps, residues, skip_gain[None], projected]
     arguments = [pltpu.with_memory_space_constraint(argument, pltpu.HBM) for argument in arguments]
     half = channels // 2
@@ -554,14 +578,13 @@
         return (count, POLES, extent), dtype
 
     state = pairs(2)
-    products, scan, keep, give, powers, taps, gains, skip, query_rows = kernel_call(
-        states_kernel, "states",
-        [((rows, channels), bf16), ((4, SEGMENTS, channels), f32), pairs(7), pairs(7),
-         pairs(2 * (SPAN + levels), f32, channels), (short_taps.shape, f32), (residues.shape, f32),
-         ((1, channels), f32), ((rows, channels), bf16)],
-        [pltpu.VMEM(*pairs(7, f32, channels)), square]
-        + [pltpu.VMEM(pole_angles.shape, f32)] * 2 + [pltpu.VMEM((2, rows, channels), bf16)]
-        + [pltpu.VMEM((rows, wide_chunk), f32)] * 2 + [dma((6,)), dma((channels // wide_chunk,))],
+    side_outs = [((rows, half), bf16), ((4, SEGMENTS, half), f32), pairs(7)]
+    working = [pltpu.VMEM((rows, wide_chunk), f32)] * 2
+    *theirs, give, powers, taps, gains, skip, kv_rows, query_rows = kernel_call(
+        first_kernel, "first",
+        [*side_outs, pairs(2 * (SPAN + levels), f32, channels), (short_taps.shape, f32), (residues.shape, f32),
+         ((1, channels), f32), ((2, rows, channels), bf16), ((rows, channels), bf16)],
+        [square] + [pltpu.VMEM(pole_angles.shape, f32)] * 2 + working + [dma((6,)), dma((half // wide_chunk + 1,))],
         arguments, range(6), levels=levels)
 
     def exchange(array, mask):
@@ -571,6 +594,8 @@
         return pairs(5 if level == levels - 1 else 7, bf16)
 
     got = exchange(give, 1)
+    *ours, keep = kernel_call(
+        second_kernel, "second", side_outs, [square] + working, [powers, taps, kv_rows, query_rows], ())
     ending, sent, lead, enter, base, fix, first = kernel_call(
         merge_kernel, "merge", [state, pairs(7, bf16), state, state, state, state, pairs(2, bf16)], [],
         [keep, got, powers, taps, gains, skip], (), channels=channels)
@@ -580,13 +605,16 @@
     tables = []
 
     def run_local(until):
-        while len(tables) < min(until, len(parts)):
-            part = parts[len(tables)]
+        while len(tables) < min(until, len(PARTS)):
+            later, offset, size = PARTS[len(tables)]
+            base, part = half * offset // 2, half * size // 2
             plane = ((rows, part), f32)
+            prod, scan = theirs if later else ours
             tables.append(kernel_call(
                 local_kernel, "local", [plane, plane, ((4, SEGMENTS, part), f32)],
                 [square, pltpu.VMEM((rows, local_chunk), f32)],
-                [taps, gains, skip, powers, scan, products, query_rows, ending, tables[-1][2] if tables else ending], (7, 8), base=sum(parts[: len(tables)])))
+                [taps, gains, skip, powers, scan, prod, query_rows, ending, tables[-1][2] if tables else ending],
+                (7, 8), theirs=later, base=base))
         return tables[-1][2]
 
     level = 1
@@ -600,7 +628,7 @@
             level=1, channels=channels)
     while level < levels:
         got = exchange(sent, 1 << level)
-        after = run_local(len(parts) if level == levels - 1 else level)
+        after = run_local(len(PARTS) if level == levels - 1 else level)
         level += 1
         if level < levels:
             ending, sent, head, lead, enter, before = kernel_call(
@@ -613,13 +641,19 @@
         [sent, got, head, powers, taps, gains, skip, lead, enter, before, base, fix, first, after], (13,),
         level=levels - 1, channels=channels)
     got = exchange(give, 1)
-    flat = [array for table in tables for array in table]
     half_plane = ((rows, half), bf16)
     scratch = [square, pltpu.VMEM(*half_plane), pltpu.VMEM((rows, chunk), bf16), dma((half // chunk + 1,))]
+
+    def side(later):
+        chosen = [(table, half * size // 2) for table, (which, _, size) in zip(tables, PARTS) if which == later]
+        return [array for table, _ in chosen for array in table], [size for _, size in chosen]
+
+    arrays, parts = side(False)
     (ready,) = kernel_call(
-        gate_kernel, "gate", [half_plane], [square, scratch[2]], [powers, keep, *flat], (), parts=parts, ready=False)
+        gate_kernel, "gate", [half_plane], [square, scratch[2]], [powers, keep, *arrays], (), parts=parts, ready=False)
+    arrays, parts = side(True)
     (out,) = kernel_call(
-        gate_kernel, "finish", [((rows, channels), bf16)], scratch, [powers, got, *flat, ready], (), (0,),
+        gate_kernel, "finish", [((rows, channels), bf16)], scratch, [powers, got, *arrays, ready], (), (0,),
         parts=parts, ready=True)
     return out
 

time: 22.9 us -> 22 us (0.961)
  waiting for transfers between devices: 4.83 us -> 3.86 us
  starting transfers between devices: 7.87 us -> 7.52 us
  Pallas kernels: 10 us -> 10.3 us
    ppermute x6, waiting for transfers between devices: 4.83 us -> 3.86 us  [exchange(): return lax.ppermute(array, 'seq', [(i, i ^ mask) for i in range(devices)])]
    ppermute x6, starting transfers between devices: 7.87 us -> 7.52 us  [exchange(): return lax.ppermute(array, 'seq', [(i, i ^ mask) for i in range(devices)])]
    pallas_call x9 -> x10, Pallas kernels: 10 us -> 10.3 us  [kernel_call(): pl.pallas_call(bound, in_specs=[spec(i in in_hbm) for i in range(len(oper...]
  transfers between devices with their start and end apart: 6 -> 6, of which waited for: 5 -> 4; matrix products, arithmetic and copies ran while one was open for 0% -> 0% of each run, Pallas kernels for 16% -> 23%
where the time goes in v7:
time: 22 us; the launch traced here: 21.8 us
  Pallas kernels  10.3 us (47%)
  starting transfers between devices  7.52 us (34%)
  waiting for transfers between devices  3.86 us (18%)
    pallas_call x10, Pallas kernels, kernel_call(): pl.pallas_call(bound, in_specs=[spec(i in in_hbm) for i in range(len(oper...  10.3 us
    ppermute x6, starting transfers between devices, exchange(): return lax.ppermute(array, 'seq', [(i, i ^ mask) for i in range(devices)])  7.52 us
    ppermute x6, waiting for transfers between devices, exchange(): return lax.ppermute(array, 'seq', [(i, i ^ mask) for i in range(devices)])  3.86 us
  transfers between devices with their start and end apart: 6, of which 4 were waited for; matrix products, arithmetic and copies ran while one was open for 0% of the time, Pallas kernels for 23%

profile of v7, /device:TPU:0, one launch (start us, length us, event | category | flops | bytes accessed | tf_op | source)
XLA Modules:
  0.0 21.8 jit_solution(6263057172096863734)
XLA Ops:
  0.0 2.9 %first.1 = (bf16[128,2048]{1,0:T(8,128)(2,1)S(1)}, f32[4,8,2048]{2,1,0:T(8,128)S(1)}, f32[7,2,2048]{2,1,0:T(2,128)S(1)}, f32[18,2,4096]{2,1,0:T(2,128)S(1)}, f32...) custom-call(f32[2,4096]{1,0:T(2,128)} %refs_0_.1, ...), custom_call_target="tpu_custom_call" | custom-call | tf_op jit(solution)/shard_map/first/pallas_call | solution.py:553
  3.0 0.6 %collective-permute-start = (f32[7,2,2048]{2,1,0:T(2,128)S(1)}, f32[7,2,2048]{2,1,0:T(2,128)S(1)}, u32[]{:S(2)}, u32[]{:S(2)}) collective-permute-start(f32[7,2,2048]{2,1,0:T(2,128)S(1)} %get-tuple-element.46), channel_id=1, source_target_pairs={{0,1},{1,0},{2,3},{3,2},{4,5},{5,4},{6,7},{7,6},{8,9},{9,8},{10,11... | collective-permute-start | bytes 344072 | tf_op jit(solution)/shard_map/ppermute | solution.py:591
  3.5 1.3 %second.1 = (bf16[128,2048]{1,0:T(8,128)(2,1)S(1)}, f32[4,8,2048]{2,1,0:T(8,128)S(1)}, f32[7,2,2048]{2,1,0:T(2,128)S(1)}) custom-call(f32[18,2,4096]{2,1,0:T(2,128)S(1)} %get-tuple-element.41.refs_0_.refs_2_.refs_3_.refs_5_, f32[3,3,4096]{2,1,0:T(4,128)S(1)} %get-tuple-element.42.refs_1_.refs_3_.refs_0_.refs_6_.refs_4_, ...), custom_call_target="tpu_custom_call" | custom-call | tf_op jit(solution)/shard_map/second/pallas_call | solution.py:553
  4.9 0.0 collective-permute-done.refs_1_
  4.9 0.3 %merge.1 = (f32[2,2,2048]{2,1,0:T(2,128)S(1)}, bf16[7,2,2048]{2,1,0:T(2,128)(2,1)S(1)}, f32[2,2,2048]{2,1,0:T(2,128)S(1)}, f32[2,2,2048]{2,1,0:T(2,128)S(1)}, f3...) custom-call(f32[7,2,2048]{2,1,0:T(2,128)S(1)} %get-tuple-element.45.refs_0_, ...), custom_call_target="tpu_custom_call" | custom-call | tf_op jit(solution)/shard_map/merge/pallas_call | solution.py:553
  5.1 3.6 %collective-permute-start.3 = (bf16[7,2,2048]{2,1,0:T(2,128)(2,1)S(1)}, bf16[7,2,2048]{2,1,0:T(2,128)(2,1)S(1)}, u32[]{:S(2)}, u32[]{:S(2)}) collective-permute-start(bf16[7,2,2048]{2,1,0:T(2,128)(2,1)S(1)} %get-tuple-element.50.refs_1_), channel_id=1, source_target_pairs={{0,6},{1,7},{2,4},{3,5},{4,2},{5,3},{6,0},{7,1},{8,14},{9,15},{10,... | collective-permute-start | bytes 172040 | tf_op jit(solution)/shard_map/ppermute | solution.py:591
  8.7 0.4 %collective-permute-start.2 = (bf16[7,2,2048]{2,1,0:T(2,128)(2,1)S(1)}, bf16[7,2,2048]{2,1,0:T(2,128)(2,1)S(1)}, u32[]{:S(2)}, u32[]{:S(2)}) collective-permute-start(bf16[7,2,2048]{2,1,0:T(2,128)(2,1)S(1)} %get-tuple-element.50.refs_1_), channel_id=1, source_target_pairs={{0,4},{1,5},{2,6},{3,7},{4,0},{5,1},{6,2},{7,3},{8,12},{9,13},{10,... | collective-permute-start | bytes 172040 | tf_op jit(solution)/shard_map/ppermute | solution.py:591
  9.2 0.2 collective-permute-start.1
  9.4 1.4 %local.3 = (f32[128,2048]{1,0:T(8,128)S(1)}, f32[128,2048]{1,0:T(8,128)S(1)}, f32[4,8,2048]{2,1,0:T(8,128)S(1)}) custom-call(f32[3,3,4096]{2,1,0:T(4,128)S(1)} %get-tuple-element.42.refs_1_.refs_3_.refs_0_.refs_6_.refs_4_, f32[2,2,4096]{2,1,0:T(2,128)S(1)} %get-tuple-element.47.refs_4_.refs_1_.refs_5_, ...), custom_call_target="tpu_custom_call" | custom-call | tf_op jit(solution)/shard_map/local/pallas_call | solution.py:553
  10.8 0.7 %local.4 = (f32[128,1024]{1,0:T(8,128)S(1)}, f32[128,1024]{1,0:T(8,128)S(1)}, f32[4,8,1024]{2,1,0:T(8,128)S(1)}) custom-call(f32[3,3,4096]{2,1,0:T(4,128)S(1)} %get-tuple-element.42.refs_1_.refs_3_.refs_0_.refs_6_.refs_4_, f32[2,2,4096]{2,1,0:T(2,128)S(1)} %get-tuple-element.47.refs_4_.refs_1_.refs_5_, ...), custom_call_target="tpu_custom_call" | custom-call | tf_op jit(solution)/shard_map/local/pallas_call | solution.py:553
  11.5 0.0 collective-permute-done.3.refs_4_
  11.5 1.4 %collective-permute-done.2.refs_3_ = bf16[7,2,2048]{2,1,0:T(2,128)(2,1)S(1)} collective-permute-done((bf16[7,2,2048]{2,1,0:T(2,128)(2,1)S(1)}, bf16[7,2,2048]{2,1,0:T(2,128)(2,1)S(1)}, u32[]{:S(2)}, u32[]{:S(2)}) %collective-permute-start.2) | collective-permute-done | bytes 57376 | tf_op jit(solution)/shard_map/ppermute | solution.py:591
  12.9 0.4 %collective-permute-done.1.refs_2_ = bf16[7,2,2048]{2,1,0:T(2,128)(2,1)S(1)} collective-permute-done((bf16[7,2,2048]{2,1,0:T(2,128)(2,1)S(1)}, bf16[7,2,2048]{2,1,0:T(2,128)(2,1)S(1)}, u32[]{:S(2)}, u32[]{:S(2)}) %collective-permute-start.1) | collective-permute-done | bytes 57376 | tf_op jit(solution)/shard_map/ppermute | solution.py:591
  13.4 0.5 %quad.1 = (f32[2,2,2048]{2,1,0:T(2,128)S(1)}, bf16[5,2,2048]{2,1,0:T(2,128)(2,1)S(1)}, bf16[2,2,2048]{2,1,0:T(2,128)(2,1)S(1)}, f32[2,2,2048]{2,1,0:T(2,128)S(1)...) custom-call(f32[2,2,2048]{2,1,0:T(2,128)S(1)} %get-tuple-element.49.refs_7_.refs_8_.refs_0_, ...), custom_call_target="tpu_custom_call" | custom-call | tf_op jit(solution)/shard_map/quad/pallas_call | solution.py:553
  13.9 2.7 %collective-permute-start.4 = (bf16[5,2,2048]{2,1,0:T(2,128)(2,1)S(1)}, bf16[5,2,2048]{2,1,0:T(2,128)(2,1)S(1)}, u32[]{:S(2)}, u32[]{:S(2)}) collective-permute-start(bf16[5,2,2048]{2,1,0:T(2,128)(2,1)S(1)} %get-tuple-element.59.refs_0_), channel_id=1, source_target_pairs={{0,8},{1,9},{2,10},{3,11},{4,12},{5,13},{6,14},{7,15},{8,0},{9,1},... | collective-permute-start | bytes 122888 | tf_op jit(solution)/shard_map/ppermute | solution.py:591
  16.5 0.7 %local.5 = (f32[128,1024]{1,0:T(8,128)S(1)}, f32[128,1024]{1,0:T(8,128)S(1)}, f32[4,8,1024]{2,1,0:T(8,128)S(1)}) custom-call(f32[3,3,4096]{2,1,0:T(4,128)S(1)} %get-tuple-element.42.refs_1_.refs_3_.refs_0_.refs_6_.refs_4_, f32[2,2,4096]{2,1,0:T(2,128)S(1)} %get-tuple-element.47.refs_4_.refs_1_.refs_5_, ...), custom_call_target="tpu_custom_call" | custom-call | tf_op jit(solution)/shard_map/local/pallas_call | solution.py:553
  17.3 1.6 %collective-permute-done.4.refs_1_ = bf16[5,2,2048]{2,1,0:T(2,128)(2,1)S(1)} collective-permute-done((bf16[5,2,2048]{2,1,0:T(2,128)(2,1)S(1)}, bf16[5,2,2048]{2,1,0:T(2,128)(2,1)S(1)}, u32[]{:S(2)}, u32[]{:S(2)}) %collective-permute-start.4) | collective-permute-done | bytes 40992 | tf_op jit(solution)/shard_map/ppermute | solution.py:591
  18.9 0.2 %last.1 = (f32[4,2,2048]{2,1,0:T(2,128)S(1)}, f32[4,2,2048]{2,1,0:T(2,128)S(1)}) custom-call(bf16[5,2,2048]{2,1,0:T(2,128)(2,1)S(1)} %get-tuple-element.59.refs_0_, bf16[5,2,2048]{2,1,0:T(2,128)(2,1)S(1)} %collective-permute-done.4.refs_1_, bf16[2,2,2048]{2,1,0:T(2,128)(2,1)S(1)} %get-tuple-element.60.refs_2_, ...), custom_call_target="tpu_custom_call" | custom-call | tf_op jit(solution)/shard_map/last/pallas_call | solution.py:553
  19.1 0.1 collective-permute-start.5
  19.2 0.8 %gate.1.refs_8_ = bf16[128,2048]{1,0:T(8,128)(2,1)S(1)} custom-call(f32[18,2,4096]{2,1,0:T(2,128)S(1)} %get-tuple-element.41.refs_0_.refs_2_.refs_3_.refs_5_, f32[4,2,2048]{2,1,0:T(2,128)S(1)} %get-tuple-element.74.refs_1_, f32[128,2048]{1,0:T(8,128)S(1)} %get-tuple-element.75.refs_2_, f32[128,2048]{1,0:T(8,128)S(1)} %get-tuple-element.76.refs_3_, ...), custom_call_target="tpu_custom_call" | custom-call | tf_op jit(solution)/shard_map/gate/pallas_call | solution.py:553
  20.0 0.4 %collective-permute-done.5.refs_1_ = f32[4,2,2048]{2,1,0:T(2,128)S(1)} collective-permute-done((f32[4,2,2048]{2,1,0:T(2,128)S(1)}, f32[4,2,2048]{2,1,0:T(2,128)S(1)}, u32[]{:S(2)}, u32[]{:S(2)}) %collective-permute-start.5) | collective-permute-done | bytes 65568 | tf_op jit(solution)/shard_map/ppermute | solution.py:591
  20.4 1.4 %finish.1 = bf16[128,4096]{1,0:T(8,128)(2,1)} custom-call(f32[18,2,4096]{2,1,0:T(2,128)S(1)} %get-tuple-element.41.refs_0_.refs_2_.refs_3_.refs_5_, f32[4,2,2048]{2,1,0:T(2,128)S(1)} %collective-permute-done.5.refs_1_, f32[128,1024]{1,0:T(8,128)S(1)} %get-tuple-element.70.refs_2_, f32[128,1024]{1,0:T(8,128)S(1)} %get-tuple-element.71.refs_3_, ...), custom_call_target="tpu_custom_call" | custom-call | tf_op jit(solution)/shard_map/finish/pallas_call | solution.py:553
  (1 shorter events, 0.0 us)
Async XLA Ops:
  3.0 1.9 %collective-permute-start = (f32[7,2,2048]{2,1,0:T(2,128)S(1)}, f32[7,2,2048]{2,1,0:T(2,128)S(1)}, u32[]{:S(2)}, u32[]{:S(2)}) collective-permute-start(f32[7,2,2048]{2,1,0:T(2,128)S(1)} %get-tuple-element.46), channel_id=1, source_target_pairs={{0,1},{1,0},{2,3},{3,2},{4,5},{5,4},{6,7},{7,6},{8,9},{9,8},{10,11... | collective-permute-start | bytes 344072 | tf_op jit(solution)/shard_map/ppermute | solution.py:591
  5.1 6.4 %collective-permute-start.3 = (bf16[7,2,2048]{2,1,0:T(2,128)(2,1)S(1)}, bf16[7,2,2048]{2,1,0:T(2,128)(2,1)S(1)}, u32[]{:S(2)}, u32[]{:S(2)}) collective-permute-start(bf16[7,2,2048]{2,1,0:T(2,128)(2,1)S(1)} %get-tuple-element.50.refs_1_), channel_id=1, source_target_pairs={{0,6},{1,7},{2,4},{3,5},{4,2},{5,3},{6,0},{7,1},{8,14},{9,15},{10,... | collective-permute-start | bytes 172040 | tf_op jit(solution)/shard_map/ppermute | solution.py:591
  8.7 4.2 %collective-permute-start.2 = (bf16[7,2,2048]{2,1,0:T(2,128)(2,1)S(1)}, bf16[7,2,2048]{2,1,0:T(2,128)(2,1)S(1)}, u32[]{:S(2)}, u32[]{:S(2)}) collective-permute-start(bf16[7,2,2048]{2,1,0:T(2,128)(2,1)S(1)} %get-tuple-element.50.refs_1_), channel_id=1, source_target_pairs={{0,4},{1,5},{2,6},{3,7},{4,0},{5,1},{6,2},{7,3},{8,12},{9,13},{10,... | collective-permute-start | bytes 172040 | tf_op jit(solution)/shard_map/ppermute | solution.py:591
  9.2 4.2 %collective-permute-start.1 = (bf16[7,2,2048]{2,1,0:T(2,128)(2,1)S(1)}, bf16[7,2,2048]{2,1,0:T(2,128)(2,1)S(1)}, u32[]{:S(2)}, u32[]{:S(2)}) collective-permute-start(bf16[7,2,2048]{2,1,0:T(2,128)(2,1)S(1)} %get-tuple-element.50.refs_1_), channel_id=1, source_target_pairs={{0,2},{1,3},{2,0},{3,1},{4,6},{5,7},{6,4},{7,5},{8,10},{9,11},{10,... | collective-permute-start | bytes 172040 | tf_op jit(solution)/shard_map/ppermute | solution.py:591
  13.9 5.0 %collective-permute-start.4 = (bf16[5,2,2048]{2,1,0:T(2,128)(2,1)S(1)}, bf16[5,2,2048]{2,1,0:T(2,128)(2,1)S(1)}, u32[]{:S(2)}, u32[]{:S(2)}) collective-permute-start(bf16[5,2,2048]{2,1,0:T(2,128)(2,1)S(1)} %get-tuple-element.59.refs_0_), channel_id=1, source_target_pairs={{0,8},{1,9},{2,10},{3,11},{4,12},{5,13},{6,14},{7,15},{8,0},{9,1},... | collective-permute-start | bytes 122888 | tf_op jit(solution)/shard_map/ppermute | solution.py:591
  19.1 1.3 %collective-permute-start.5 = (f32[4,2,2048]{2,1,0:T(2,128)S(1)}, f32[4,2,2048]{2,1,0:T(2,128)S(1)}, u32[]{:S(2)}, u32[]{:S(2)}) collective-permute-start(f32[4,2,2048]{2,1,0:T(2,128)S(1)} %get-tuple-element.69), channel_id=1, source_target_pairs={{0,1},{1,0},{2,3},{3,2},{4,5},{5,4},{6,7},{7,6},{8,9},{9,8},{10,11... | collective-permute-start | bytes 196616 | tf_op jit(solution)/shard_map/ppermute | solution.py:591

commit v8 on v7

--- a/solution.py
+++ b/solution.py
@@ -1,3 +1,6 @@
+import functools
+import itertools
+
 import jax
 import jax.numpy as jnp
 from jax import lax
@@ -107,6 +110,8 @@
 
 
 def span(start, size):
+    if isinstance(start, int):
+        return slice(start, start + size)
     return pl.ds(pl.multiple_of(start, 128), size)
 
 
@@ -123,18 +128,18 @@
 def half_states(ready, begin, order_ref, power_ref, taps_ref, kv_ref, q_ref, prod_ref, scan_ref, block_ref, ks_ref, vs_ref):
     _, rows, _ = kv_ref.shape
     half = prod_ref.shape[1]
-    chunk = ks_ref.shape[1]
+    chunk = min(STATES_CHUNK, half)
 
     def body(i, _):
         ready(i)
         at = span(begin + i * chunk, chunk)
-        ks_ref[...] = jnp.dot(order_ref[...], kv_ref[0, :, at], preferred_element_type=f32)
-        vs_ref[...] = jnp.dot(order_ref[...], kv_ref[1, :, at], preferred_element_type=f32)
+        scratch = slice(i * chunk, (i + 1) * chunk)
+        ks_ref[:, scratch] = jnp.dot(order_ref[...], kv_ref[0, :, at], preferred_element_type=f32)
+        vs_ref[:, scratch] = jnp.dot(order_ref[...], kv_ref[1, :, at], preferred_element_type=f32)
 
         def column(inner, outer):
-            cols = slice(inner, inner + WIDTH)
+            cols = put = slice(outer, outer + WIDTH)
             here = span(begin + outer, WIDTH)
-            put = span(outer, WIDTH)
             keys = short_filter(steps_of(ks_ref, cols), taps_ref, 1, here)
             values = short_filter(steps_of(vs_ref, cols), taps_ref, 2, here)
             products = [a * b for a, b in zip(keys, values)]
@@ -164,7 +169,8 @@
         loop_columns(i, chunk, column)
         return 0
 
-    lax.fori_loop(0, half // chunk, body, 0)
+    for i in range(half // chunk):
+        body(i, 0)
 
 
 def put_edges(begin, kv_ref, q_ref, block_ref):
@@ -182,7 +188,7 @@
                  order_ref, angle_ref, decay_ref, ks_ref, vs_ref, small_sem, in_sem, *, levels):
     _, rows, channels = kv_ref.shape
     half = channels // 2
-    chunk = ks_ref.shape[1]
+    chunk = min(STATES_CHUNK, half)
     count = half // chunk
     begin, rest = side_start(True, half), side_start(False, half)
     smalls = [
@@ -200,14 +206,19 @@
         copy.start()
     for i in range(count):
         fetch(begin + i * chunk, chunk, i).start()
-    for copy in smalls[3:]:
-        copy.start()
-    fetch(rest, half, count).start()
     order_ref[...] = order_matrix(rows, False)
     for copy in smalls[:3]:
         copy.wait()
     fill_powers(power_ref, angle_ref, decay_ref, rows // SEGMENTS, levels)
-    half_states(lambda i: fetch(begin + i * chunk, chunk, i).wait(), begin, order_ref, power_ref, taps_ref,
+
+    def ready(i):
+        fetch(begin + i * chunk, chunk, i).wait()
+        if i == 0:
+            for copy in smalls[3:]:
+                copy.start()
+            fetch(rest, half, count).start()
+
+    half_states(ready, begin, order_ref, power_ref, taps_ref,
                 kv_ref, q_ref, prod_ref, scan_ref, give_ref, ks_ref, vs_ref)
     for copy in smalls[3:]:
         copy.wait()
@@ -258,7 +269,15 @@
     return [ref[i].astype(f32) for i in range(start, stop)]
 
 
+def by_cases(conditions, body):
+    for values in itertools.product((False, True), repeat=len(conditions)):
+        hits = [c if value else jnp.logical_not(c) for c, value in zip(conditions, values)]
+        pl.when(functools.reduce(jnp.logical_and, hits))(functools.partial(body, *values))
+
+
 def pick(condition, a, b):
+    if isinstance(condition, bool):
+        return tuple(a) if condition else tuple(b)
     return tuple(jnp.where(condition, x, y) for x, y in zip(a, b))
 
 
@@ -281,37 +300,38 @@
 def merge_kernel(own_ref, mate_ref, power_ref, taps_ref, gain_ref, skip_ref,
                  joined_ref, wire_ref, lead_ref, enter_ref, base_ref, fix_ref, head_ref, *, channels):
     device = lax.axis_index("seq")
-    odd = device % 2 == 1
-    half = halves(channels)[0]
-    taps, gain, skip = taps_ref[:, :, half], gain_ref[:, :, half], skip_ref[:, half]
-    power, back = pair_at(power_ref, SPAN, half), pair_at(power_ref, BACK, half)
-    mine, mates = planes_of(own_ref, 2, 7), planes_of(mate_ref, 2, 7)
-    even_edge, odd_edge = pick(odd, mates, mine), pick(odd, mine, mates)
-    own, mate = pair_at(own_ref, 0, ALL), pair_at(mate_ref, 0, ALL)
-    even_total, odd_total = pick(odd, mate, own), pick(odd, own, mate)
-    products = first_products(even_edge[0:3], odd_edge[3:5], taps)
-    base = plus(even_total, extra_state(products, back))
-    put_pair(base_ref, 0, ALL, base)
-    fix_ref[0], fix_ref[1] = fixed_rows(products, even_edge[0:3], taps, skip, gain, back)
-    start = extra_state(first_products([jnp.zeros_like(power[0])] * 3, even_edge[3:5], taps), back)
-    enter = tuple(jnp.where(device < 2, part, 0.0) for part in start)
-    put_pair(enter_ref, 0, ALL, enter)
-    joined = plus(odd_total, times(power, plus(base, times(power, enter))))
-    put_pair(joined_ref, 0, ALL, joined)
-    put_pair(lead_ref, 0, ALL, (jnp.ones_like(power[0]), jnp.zeros_like(power[0])))
-    put_wire(wire_ref, joined)
-    for i in range(3):
-        wire_ref[2 + i] = odd_edge[i].astype(bf16)
-    for i in range(2):
-        head = even_edge[3 + i].astype(bf16)
-        head_ref[i] = head
-        wire_ref[5 + i] = head
-
-
-def step_of(level, sent_ref, got_ref, own_head, power_ref, taps_ref, lead_ref, enter_ref, tail_before, half):
-    device = lax.axis_index("seq")
-    upper = (device >> level) % 2 == 1
-    leads = jnp.logical_and(upper, (device % (1 << level)) < 2)
+
+    def body(odd):
+        half = halves(channels)[0]
+        taps, gain, skip = taps_ref[:, :, half], gain_ref[:, :, half], skip_ref[:, half]
+        power, back = pair_at(power_ref, SPAN, half), pair_at(power_ref, BACK, half)
+        mine, mates = planes_of(own_ref, 2, 7), planes_of(mate_ref, 2, 7)
+        even_edge, odd_edge = pick(odd, mates, mine), pick(odd, mine, mates)
+        own, mate = pair_at(own_ref, 0, ALL), pair_at(mate_ref, 0, ALL)
+        even_total, odd_total = pick(odd, mate, own), pick(odd, own, mate)
+        products = first_products(even_edge[0:3], odd_edge[3:5], taps)
+        base = plus(even_total, extra_state(products, back))
+        put_pair(base_ref, 0, ALL, base)
+        fix_ref[0], fix_ref[1] = fixed_rows(products, even_edge[0:3], taps, skip, gain, back)
+        start = extra_state(first_products([jnp.zeros_like(power[0])] * 3, even_edge[3:5], taps), back)
+        enter = tuple(jnp.where(device < 2, part, 0.0) for part in start)
+        put_pair(enter_ref, 0, ALL, enter)
+        joined = plus(odd_total, times(power, plus(base, times(power, enter))))
+        put_pair(joined_ref, 0, ALL, joined)
+        put_pair(lead_ref, 0, ALL, (jnp.ones_like(power[0]), jnp.zeros_like(power[0])))
+        put_wire(wire_ref, joined)
+        for i in range(3):
+            wire_ref[2 + i] = odd_edge[i].astype(bf16)
+        for i in range(2):
+            head = even_edge[3 + i].astype(bf16)
+            head_ref[i] = head
+            wire_ref[5 + i] = head
+
+    by_cases([device % 2 == 1], body)
+
+
+def step_of(level, upper, sent_ref, got_ref, own_head, power_ref, taps_ref, lead_ref, enter_ref, tail_before, half):
+    leads = jnp.logical_and(upper, (lax.axis_index("seq") % (1 << level)) < 2)
     back = pair_at(power_ref, BACK, half)
     early_tail = pick(upper, planes_of(got_ref, 2, 5), planes_of(sent_ref, 2, 5))
     late_head = own_head
@@ -321,15 +341,16 @@
     other = from_wire(got_ref)
     lead, enter = pair_at(lead_ref, 0, ALL), pair_at(enter_ref, 0, ALL)
     enter = pick(upper, plus(enter, times(lead, plus(other, extra))), enter)
-    return upper, other, extra, lead, enter, pick(leads, early_tail, tail_before)
+    return other, extra, lead, enter, pick(leads, early_tail, tail_before)
 
 
 def join_kernel(ending_ref, sent_ref, got_ref, head_ref, power_ref, taps_ref, lead_ref, enter_ref, before_ref, after_ref,
                 joined_ref, wire_ref, next_head_ref, next_lead_ref, next_enter_ref, next_before_ref, *, level, channels):
     half = halves(channels)[0]
     own_head = planes_of(head_ref, 0, 2)
-    upper, other, extra, lead, enter, before = step_of(
-        level, sent_ref, got_ref, own_head, power_ref, taps_ref, lead_ref, enter_ref, planes_of(before_ref, 0, 3), half)
+    upper = (lax.axis_index("seq") >> level) % 2 == 1
+    other, extra, lead, enter, before = step_of(
+        level, upper, sent_ref, got_ref, own_head, power_ref, taps_ref, lead_ref, enter_ref, planes_of(before_ref, 0, 3), half)
     factor = pair_at(power_ref, SPAN + level, half)
     mine = pair_at(ending_ref, 0, ALL)
     early, late = pick(upper, other, mine), pick(upper, mine, other)
@@ -359,53 +380,60 @@
                 before_ref, after_ref, joined_ref, wire_ref, next_head_ref, next_lead_ref, next_enter_ref,
                 next_before_ref, *, level, channels):
     device = lax.axis_index("seq")
-    half = halves(channels)[0]
-    back, taps = pair_at(power_ref, BACK, half), taps_ref[:, :, half]
-    near, far, both = ([*from_wire(ref), *planes_of(ref, 2, 7)] for ref in (near_ref, far_ref, both_ref))
-    mine = [*pair_at(ending_ref, 0, ALL), *planes_of(sent_ref, 2, 7)]
-    lead, enter, before = pair_at(lead_ref, 0, ALL), pair_at(enter_ref, 0, ALL), planes_of(before_ref, 0, 3)
-    upper = (device >> level) % 2 == 1
-    factor = pair_at(power_ref, SPAN + level, half)
-    other, _ = join_blocks(pick(upper, both, far), pick(upper, far, both), factor, back, taps)
-    for step in range(2):
-        upper = (device >> (level + step)) % 2 == 1
-        leads = jnp.logical_and(upper, (device % (1 << (level + step))) < 2)
-        factor = pair_at(power_ref, SPAN + level + step, half)
-        across = other if step else near
-        early = pick(upper, across, mine)
-        mine, begin = join_blocks(early, pick(upper, mine, across), factor, back, taps)
-        enter = pick(upper, plus(enter, times(lead, begin)), enter)
-        lead = pick(upper, times(lead, factor), lead)
-        before = pick(leads, early[2:5], before)
-    put_pair(joined_ref, 0, ALL, mine[0:2])
-    put_wire(wire_ref, mine[0:2])
-    for i in range(3):
-        wire_ref[2 + i] = mine[2 + i].astype(bf16)
-        next_before_ref[i] = before[i].astype(bf16)
-    for i in range(2):
-        head = mine[5 + i].astype(bf16)
-        next_head_ref[i] = head
-        if wire_ref.shape[0] > 5:
-            wire_ref[5 + i] = head
-    put_pair(next_lead_ref, 0, ALL, lead)
-    put_pair(next_enter_ref, 0, ALL, enter)
+
+    def body(*uppers):
+        half = halves(channels)[0]
+        back, taps = pair_at(power_ref, BACK, half), taps_ref[:, :, half]
+        near, far, both = ([*from_wire(ref), *planes_of(ref, 2, 7)] for ref in (near_ref, far_ref, both_ref))
+        mine = [*pair_at(ending_ref, 0, ALL), *planes_of(sent_ref, 2, 7)]
+        lead, enter, before = pair_at(lead_ref, 0, ALL), pair_at(enter_ref, 0, ALL), planes_of(before_ref, 0, 3)
+        upper = uppers[0]
+        factor = pair_at(power_ref, SPAN + level, half)
+        other, _ = join_blocks(pick(upper, both, far), pick(upper, far, both), factor, back, taps)
+        for step in range(2):
+            upper = uppers[step]
+            leads = jnp.logical_and(upper, (device % (1 << (level + step))) < 2)
+            factor = pair_at(power_ref, SPAN + level + step, half)
+            across = other if step else near
+            early = pick(upper, across, mine)
+            mine, begin = join_blocks(early, pick(upper, mine, across), factor, back, taps)
+            enter = pick(upper, plus(enter, times(lead, begin)), enter)
+            lead = pick(upper, times(lead, factor), lead)
+            before = pick(leads, early[2:5], before)
+        put_pair(joined_ref, 0, ALL, mine[0:2])
+        put_wire(wire_ref, mine[0:2])
+        for i in range(3):
+            wire_ref[2 + i] = mine[2 + i].astype(bf16)
+            next_before_ref[i] = before[i].astype(bf16)
+        for i in range(2):
+            head = mine[5 + i].astype(bf16)
+            next_head_ref[i] = head
+            if wire_ref.shape[0] > 5:
+                wire_ref[5 + i] = head
+        put_pair(next_lead_ref, 0, ALL, lead)
+        put_pair(next_enter_ref, 0, ALL, enter)
+
+    by_cases([(device >> (level + step)) % 2 == 1 for step in range(2)], body)
 
 
 def last_kernel(sent_ref, got_ref, head_ref, power_ref, taps_ref, gain_ref, skip_ref, lead_ref, enter_ref, before_ref,
                 base_ref, fix_ref, first_ref, after_ref, keep_ref, give_ref, *, level, channels):
-    half = halves(channels)[0]
-    odd = lax.axis_index("seq") % 2 == 1
-    _, _, _, _, enter, before = step_of(
-        level, sent_ref, got_ref, planes_of(head_ref, 0, 2), power_ref, taps_ref, lead_ref, enter_ref,
-        planes_of(before_ref, 0, 3), half)
-    taps, gain, skip = taps_ref[:, :, half], gain_ref[:, :, half], skip_ref[:, half]
-    power, back = pair_at(power_ref, SPAN, half), pair_at(power_ref, BACK, half)
-    products = first_products(before, planes_of(first_ref, 0, 2), taps)
-    even = [*enter, *fixed_rows(products, before, taps, skip, gain, back)]
-    odds = [*plus(times(power, enter), pair_at(base_ref, 0, ALL)), fix_ref[0], fix_ref[1]]
-    for i, (a, b) in enumerate(zip(even, odds)):
-        keep_ref[i] = jnp.where(odd, b, a)
-        give_ref[i] = jnp.where(odd, a, b)
+    device = lax.axis_index("seq")
+
+    def body(odd, upper):
+        half = halves(channels)[0]
+        _, _, _, enter, before = step_of(
+            level, upper, sent_ref, got_ref, planes_of(head_ref, 0, 2), power_ref, taps_ref, lead_ref, enter_ref,
+            planes_of(before_ref, 0, 3), half)
+        taps, gain, skip = taps_ref[:, :, half], gain_ref[:, :, half], skip_ref[:, half]
+        power, back = pair_at(power_ref, SPAN, half), pair_at(power_ref, BACK, half)
+        products = first_products(before, planes_of(first_ref, 0, 2), taps)
+        even = [*enter, *fixed_rows(products, before, taps, skip, gain, back)]
+        odds = [*plus(times(power, enter), pair_at(base_ref, 0, ALL)), fix_ref[0], fix_ref[1]]
+        for i, (a, b) in enumerate(zip(even, odds)):
+            keep_ref[i], give_ref[i] = (b, a) if odd else (a, b)
+
+    by_cases([device % 2 == 1, (device >> level) % 2 == 1], body)
 
 
 def local_kernel(taps_ref, gain_ref, skip_ref, power_ref, scan_ref, prod_ref, q_ref, after_ref, part_ref,
@@ -477,7 +505,7 @@
     else:
         out_ref, order_ref, gated_ref = rest
     half = out_ref.shape[1]
-    chunk = gated_ref.shape[1]
+    chunk = min(CHUNK, half)
     own = halves(2 * half)[0]
     begin = side_start(ready, half)
 
@@ -494,7 +522,6 @@
     def gate_part(base, part, query_ref, local_ref, reach_ref):
         def body(i, _):
             def column(inner, outer):
-                cols = slice(inner, inner + WIDTH)
                 take = span(outer, WIDTH)
                 there = span(base + outer, WIDTH)
                 here = span(begin + base + outer, WIDTH)
@@ -521,17 +548,18 @@
                     gated.append(queries[j] * total)
                     if j % 2:
                         both = jnp.concatenate(gated[-2:], axis=0)
-                        gated_ref[SEGMENTS * (j - 1) : SEGMENTS * (j + 1), cols] = both.astype(bf16)
+                        gated_ref[SEGMENTS * (j - 1) : SEGMENTS * (j + 1), base + outer : base + outer + WIDTH] = both.astype(bf16)
 
             loop_columns(i, chunk, column)
             place = base // chunk + i
             out_ref[:, span(place * chunk, chunk)] = jnp.dot(
-                order_ref[...], gated_ref[...], preferred_element_type=f32).astype(bf16)
+                order_ref[...], gated_ref[:, span(place * chunk, chunk)], preferred_element_type=f32).astype(bf16)
             if ready:
                 send(place).start()
             return 0
 
-        lax.fori_loop(0, part // chunk, body, 0)
+        for i in range(part // chunk):
+            body(i, 0)
 
     base = 0
     for index, part in enumerate(parts):
@@ -579,7 +607,7 @@
 
     state = pairs(2)
     side_outs = [((rows, half), bf16), ((4, SEGMENTS, half), f32), pairs(7)]
-    working = [pltpu.VMEM((rows, wide_chunk), f32)] * 2
+    working = [pltpu.VMEM((rows, half), f32)] * 2
     *theirs, give, powers, taps, gains, skip, kv_rows, query_rows = kernel_call(
         first_kernel, "first",
         [*side_outs, pairs(2 * (SPAN + levels), f32, channels), (short_taps.shape, f32), (residues.shape, f32),
@@ -642,7 +670,7 @@
         level=levels - 1, channels=channels)
     got = exchange(give, 1)
     half_plane = ((rows, half), bf16)
-    scratch = [square, pltpu.VMEM(*half_plane), pltpu.VMEM((rows, chunk), bf16), dma((half // chunk + 1,))]
+    scratch = [square, pltpu.VMEM(*half_plane), pltpu.VMEM(*half_plane), dma((half // chunk + 1,))]
 
     def side(later):
         chosen = [(table, half * size // 2) for table, (which, _, size) in zip(tables, PARTS) if which == later]

time: 22 us -> 21.6 us (0.982)
  Pallas kernels: 10.3 us -> 9.74 us
    pallas_call x10, Pallas kernels: 10.3 us -> 9.74 us  [kernel_call(): pl.pallas_call(bound, in_specs=[spec(i in in_hbm) for i in range(len(oper...]
  transfers between devices with their start and end apart: 6 -> 6, of which waited for: 4 -> 4; matrix products, arithmetic and copies ran while one was open for 0% -> 0% of each run, Pallas kernels for 23% -> 22%
where the time goes in v8:
time: 21.6 us; the launch traced here: 21.5 us
  Pallas kernels  9.74 us (45%)
  starting transfers between devices  7.59 us (35%)
  waiting for transfers between devices  4.03 us (19%)
    pallas_call x10, Pallas kernels, kernel_call(): pl.pallas_call(bound, in_specs=[spec(i in in_hbm) for i in range(len(oper...  9.74 us
    ppermute x6, starting transfers between devices, exchange(): return lax.ppermute(array, 'seq', [(i, i ^ mask) for i in range(devices)])  7.59 us
    ppermute x6, waiting for transfers between devices, exchange(): return lax.ppermute(array, 'seq', [(i, i ^ mask) for i in range(devices)])  4.03 us
  transfers between devices with their start and end apart: 6, of which 4 were waited for; matrix products, arithmetic and copies ran while one was open for 0% of the time, Pallas kernels for 22%

profile of v8, /device:TPU:0, one launch (start us, length us, event | category | flops | bytes accessed | tf_op | source)
XLA Modules:
  0.0 21.5 jit_solution(1363756849434205489)
XLA Ops:
  0.0 2.9 %first.1 = (bf16[128,2048]{1,0:T(8,128)(2,1)S(1)}, f32[4,8,2048]{2,1,0:T(8,128)S(1)}, f32[7,2,2048]{2,1,0:T(2,128)S(1)}, f32[18,2,4096]{2,1,0:T(2,128)S(1)}, f32...) custom-call(f32[2,4096]{1,0:T(2,128)} %refs_0_.1, ...), custom_call_target="tpu_custom_call" | custom-call | tf_op jit(solution)/shard_map/first/pallas_call | solution.py:581
  2.9 0.6 %collective-permute-start = (f32[7,2,2048]{2,1,0:T(2,128)S(1)}, f32[7,2,2048]{2,1,0:T(2,128)S(1)}, u32[]{:S(2)}, u32[]{:S(2)}) collective-permute-start(f32[7,2,2048]{2,1,0:T(2,128)S(1)} %get-tuple-element.46), channel_id=1, source_target_pairs={{0,1},{1,0},{2,3},{3,2},{4,5},{5,4},{6,7},{7,6},{8,9},{9,8},{10,11... | collective-permute-start | bytes 344072 | tf_op jit(solution)/shard_map/ppermute | solution.py:619
  3.4 1.2 %second.1 = (bf16[128,2048]{1,0:T(8,128)(2,1)S(1)}, f32[4,8,2048]{2,1,0:T(8,128)S(1)}, f32[7,2,2048]{2,1,0:T(2,128)S(1)}) custom-call(f32[18,2,4096]{2,1,0:T(2,128)S(1)} %get-tuple-element.41.refs_0_.refs_2_.refs_3_.refs_5_, f32[3,3,4096]{2,1,0:T(4,128)S(1)} %get-tuple-element.42.refs_1_.refs_3_.refs_0_.refs_6_.refs_4_, ...), custom_call_target="tpu_custom_call" | custom-call | tf_op jit(solution)/shard_map/second/pallas_call | solution.py:581
  4.7 0.0 collective-permute-done.refs_1_
  4.7 0.2 %merge.1 = (f32[2,2,2048]{2,1,0:T(2,128)S(1)}, bf16[7,2,2048]{2,1,0:T(2,128)(2,1)S(1)}, f32[2,2,2048]{2,1,0:T(2,128)S(1)}, f32[2,2,2048]{2,1,0:T(2,128)S(1)}, f3...) custom-call(f32[7,2,2048]{2,1,0:T(2,128)S(1)} %get-tuple-element.45.refs_0_, ...), custom_call_target="tpu_custom_call" | custom-call | tf_op jit(solution)/shard_map/merge/pallas_call | solution.py:581
  4.9 3.7 %collective-permute-start.3 = (bf16[7,2,2048]{2,1,0:T(2,128)(2,1)S(1)}, bf16[7,2,2048]{2,1,0:T(2,128)(2,1)S(1)}, u32[]{:S(2)}, u32[]{:S(2)}) collective-permute-start(bf16[7,2,2048]{2,1,0:T(2,128)(2,1)S(1)} %get-tuple-element.50.refs_1_), channel_id=1, source_target_pairs={{0,6},{1,7},{2,4},{3,5},{4,2},{5,3},{6,0},{7,1},{8,14},{9,15},{10,... | collective-permute-start | bytes 172040 | tf_op jit(solution)/shard_map/ppermute | solution.py:619
  8.6 0.4 %collective-permute-start.2 = (bf16[7,2,2048]{2,1,0:T(2,128)(2,1)S(1)}, bf16[7,2,2048]{2,1,0:T(2,128)(2,1)S(1)}, u32[]{:S(2)}, u32[]{:S(2)}) collective-permute-start(bf16[7,2,2048]{2,1,0:T(2,128)(2,1)S(1)} %get-tuple-element.50.refs_1_), channel_id=1, source_target_pairs={{0,4},{1,5},{2,6},{3,7},{4,0},{5,1},{6,2},{7,3},{8,12},{9,13},{10,... | collective-permute-start | bytes 172040 | tf_op jit(solution)/shard_map/ppermute | solution.py:619
  9.0 0.2 collective-permute-start.1
  9.2 1.4 %local.3 = (f32[128,2048]{1,0:T(8,128)S(1)}, f32[128,2048]{1,0:T(8,128)S(1)}, f32[4,8,2048]{2,1,0:T(8,128)S(1)}) custom-call(f32[3,3,4096]{2,1,0:T(4,128)S(1)} %get-tuple-element.42.refs_1_.refs_3_.refs_0_.refs_6_.refs_4_, f32[2,2,4096]{2,1,0:T(2,128)S(1)} %get-tuple-element.47.refs_4_.refs_1_.refs_5_, ...), custom_call_target="tpu_custom_call" | custom-call | tf_op jit(solution)/shard_map/local/pallas_call | solution.py:581
  10.6 0.7 %local.4 = (f32[128,1024]{1,0:T(8,128)S(1)}, f32[128,1024]{1,0:T(8,128)S(1)}, f32[4,8,1024]{2,1,0:T(8,128)S(1)}) custom-call(f32[3,3,4096]{2,1,0:T(4,128)S(1)} %get-tuple-element.42.refs_1_.refs_3_.refs_0_.refs_6_.refs_4_, f32[2,2,4096]{2,1,0:T(2,128)S(1)} %get-tuple-element.47.refs_4_.refs_1_.refs_5_, ...), custom_call_target="tpu_custom_call" | custom-call | tf_op jit(solution)/shard_map/local/pallas_call | solution.py:581
  11.3 0.0 collective-permute-done.3.refs_4_
  11.3 1.4 %collective-permute-done.2.refs_3_ = bf16[7,2,2048]{2,1,0:T(2,128)(2,1)S(1)} collective-permute-done((bf16[7,2,2048]{2,1,0:T(2,128)(2,1)S(1)}, bf16[7,2,2048]{2,1,0:T(2,128)(2,1)S(1)}, u32[]{:S(2)}, u32[]{:S(2)}) %collective-permute-start.2) | collective-permute-done | bytes 57376 | tf_op jit(solution)/shard_map/ppermute | solution.py:619
  12.7 0.4 %collective-permute-done.1.refs_2_ = bf16[7,2,2048]{2,1,0:T(2,128)(2,1)S(1)} collective-permute-done((bf16[7,2,2048]{2,1,0:T(2,128)(2,1)S(1)}, bf16[7,2,2048]{2,1,0:T(2,128)(2,1)S(1)}, u32[]{:S(2)}, u32[]{:S(2)}) %collective-permute-start.1) | collective-permute-done | bytes 57376 | tf_op jit(solution)/shard_map/ppermute | solution.py:619
  13.2 0.4 %quad.1 = (f32[2,2,2048]{2,1,0:T(2,128)S(1)}, bf16[5,2,2048]{2,1,0:T(2,128)(2,1)S(1)}, bf16[2,2,2048]{2,1,0:T(2,128)(2,1)S(1)}, f32[2,2,2048]{2,1,0:T(2,128)S(1)...) custom-call(f32[2,2,2048]{2,1,0:T(2,128)S(1)} %get-tuple-element.49.refs_7_.refs_8_.refs_0_, ...), custom_call_target="tpu_custom_call" | custom-call | tf_op jit(solution)/shard_map/quad/pallas_call | solution.py:581
  13.7 2.7 %collective-permute-start.4 = (bf16[5,2,2048]{2,1,0:T(2,128)(2,1)S(1)}, bf16[5,2,2048]{2,1,0:T(2,128)(2,1)S(1)}, u32[]{:S(2)}, u32[]{:S(2)}) collective-permute-start(bf16[5,2,2048]{2,1,0:T(2,128)(2,1)S(1)} %get-tuple-element.59.refs_0_), channel_id=1, source_target_pairs={{0,8},{1,9},{2,10},{3,11},{4,12},{5,13},{6,14},{7,15},{8,0},{9,1},... | collective-permute-start | bytes 122888 | tf_op jit(solution)/shard_map/ppermute | solution.py:619
  16.3 0.7 %local.5 = (f32[128,1024]{1,0:T(8,128)S(1)}, f32[128,1024]{1,0:T(8,128)S(1)}, f32[4,8,1024]{2,1,0:T(8,128)S(1)}) custom-call(f32[3,3,4096]{2,1,0:T(4,128)S(1)} %get-tuple-element.42.refs_1_.refs_3_.refs_0_.refs_6_.refs_4_, f32[2,2,4096]{2,1,0:T(2,128)S(1)} %get-tuple-element.47.refs_4_.refs_1_.refs_5_, ...), custom_call_target="tpu_custom_call" | custom-call | tf_op jit(solution)/shard_map/local/pallas_call | solution.py:581
  17.0 1.6 %collective-permute-done.4.refs_1_ = bf16[5,2,2048]{2,1,0:T(2,128)(2,1)S(1)} collective-permute-done((bf16[5,2,2048]{2,1,0:T(2,128)(2,1)S(1)}, bf16[5,2,2048]{2,1,0:T(2,128)(2,1)S(1)}, u32[]{:S(2)}, u32[]{:S(2)}) %collective-permute-start.4) | collective-permute-done | bytes 40992 | tf_op jit(solution)/shard_map/ppermute | solution.py:619
  18.6 0.1 last.1
  18.7 0.1 collective-permute-start.5
  18.8 0.7 %gate.1.refs_8_ = bf16[128,2048]{1,0:T(8,128)(2,1)S(1)} custom-call(f32[18,2,4096]{2,1,0:T(2,128)S(1)} %get-tuple-element.41.refs_0_.refs_2_.refs_3_.refs_5_, f32[4,2,2048]{2,1,0:T(2,128)S(1)} %get-tuple-element.74.refs_1_, f32[128,2048]{1,0:T(8,128)S(1)} %get-tuple-element.75.refs_2_, f32[128,2048]{1,0:T(8,128)S(1)} %get-tuple-element.76.refs_3_, ...), custom_call_target="tpu_custom_call" | custom-call | tf_op jit(solution)/shard_map/gate/pallas_call | solution.py:581
  19.5 0.6 %collective-permute-done.5.refs_1_ = f32[4,2,2048]{2,1,0:T(2,128)S(1)} collective-permute-done((f32[4,2,2048]{2,1,0:T(2,128)S(1)}, f32[4,2,2048]{2,1,0:T(2,128)S(1)}, u32[]{:S(2)}, u32[]{:S(2)}) %collective-permute-start.5) | collective-permute-done | bytes 65568 | tf_op jit(solution)/shard_map/ppermute | solution.py:619
  20.1 1.4 %finish.1 = bf16[128,4096]{1,0:T(8,128)(2,1)} custom-call(f32[18,2,4096]{2,1,0:T(2,128)S(1)} %get-tuple-element.41.refs_0_.refs_2_.refs_3_.refs_5_, f32[4,2,2048]{2,1,0:T(2,128)S(1)} %collective-permute-done.5.refs_1_, f32[128,1024]{1,0:T(8,128)S(1)} %get-tuple-element.70.refs_2_, f32[128,1024]{1,0:T(8,128)S(1)} %get-tuple-element.71.refs_3_, ...), custom_call_target="tpu_custom_call" | custom-call | tf_op jit(solution)/shard_map/finish/pallas_call | solution.py:581
  (1 shorter events, 0.0 us)
Async XLA Ops:
  2.9 1.8 %collective-permute-start = (f32[7,2,2048]{2,1,0:T(2,128)S(1)}, f32[7,2,2048]{2,1,0:T(2,128)S(1)}, u32[]{:S(2)}, u32[]{:S(2)}) collective-permute-start(f32[7,2,2048]{2,1,0:T(2,128)S(1)} %get-tuple-element.46), channel_id=1, source_target_pairs={{0,1},{1,0},{2,3},{3,2},{4,5},{5,4},{6,7},{7,6},{8,9},{9,8},{10,11... | collective-permute-start | bytes 344072 | tf_op jit(solution)/shard_map/ppermute | solution.py:619
  4.9 6.4 %collective-permute-start.3 = (bf16[7,2,2048]{2,1,0:T(2,128)(2,1)S(1)}, bf16[7,2,2048]{2,1,0:T(2,128)(2,1)S(1)}, u32[]{:S(2)}, u32[]{:S(2)}) collective-permute-start(bf16[7,2,2048]{2,1,0:T(2,128)(2,1)S(1)} %get-tuple-element.50.refs_1_), channel_id=1, source_target_pairs={{0,6},{1,7},{2,4},{3,5},{4,2},{5,3},{6,0},{7,1},{8,14},{9,15},{10,... | collective-permute-start | bytes 172040 | tf_op jit(solution)/shard_map/ppermute | solution.py:619
  8.6 4.2 %collective-permute-start.2 = (bf16[7,2,2048]{2,1,0:T(2,128)(2,1)S(1)}, bf16[7,2,2048]{2,1,0:T(2,128)(2,1)S(1)}, u32[]{:S(2)}, u32[]{:S(2)}) collective-permute-start(bf16[7,2,2048]{2,1,0:T(2,128)(2,1)S(1)} %get-tuple-element.50.refs_1_), channel_id=1, source_target_pairs={{0,4},{1,5},{2,6},{3,7},{4,0},{5,1},{6,2},{7,3},{8,12},{9,13},{10,... | collective-permute-start | bytes 172040 | tf_op jit(solution)/shard_map/ppermute | solution.py:619
  9.0 4.2 %collective-permute-start.1 = (bf16[7,2,2048]{2,1,0:T(2,128)(2,1)S(1)}, bf16[7,2,2048]{2,1,0:T(2,128)(2,1)S(1)}, u32[]{:S(2)}, u32[]{:S(2)}) collective-permute-start(bf16[7,2,2048]{2,1,0:T(2,128)(2,1)S(1)} %get-tuple-element.50.refs_1_), channel_id=1, source_target_pairs={{0,2},{1,3},{2,0},{3,1},{4,6},{5,7},{6,4},{7,5},{8,10},{9,11},{10,... | collective-permute-start | bytes 172040 | tf_op jit(solution)/shard_map/ppermute | solution.py:619
  13.7 5.0 %collective-permute-start.4 = (bf16[5,2,2048]{2,1,0:T(2,128)(2,1)S(1)}, bf16[5,2,2048]{2,1,0:T(2,128)(2,1)S(1)}, u32[]{:S(2)}, u32[]{:S(2)}) collective-permute-start(bf16[5,2,2048]{2,1,0:T(2,128)(2,1)S(1)} %get-tuple-element.59.refs_0_), channel_id=1, source_target_pairs={{0,8},{1,9},{2,10},{3,11},{4,12},{5,13},{6,14},{7,15},{8,0},{9,1},... | collective-permute-start | bytes 122888 | tf_op jit(solution)/shard_map/ppermute | solution.py:619
  18.7 1.3 %collective-permute-start.5 = (f32[4,2,2048]{2,1,0:T(2,128)S(1)}, f32[4,2,2048]{2,1,0:T(2,128)S(1)}, u32[]{:S(2)}, u32[]{:S(2)}) collective-permute-start(f32[4,2,2048]{2,1,0:T(2,128)S(1)} %get-tuple-element.69), channel_id=1, source_target_pairs={{0,1},{1,0},{2,3},{3,2},{4,5},{5,4},{6,7},{7,6},{8,9},{9,8},{10,11... | collective-permute-start | bytes 196616 | tf_op jit(solution)/shard_map/ppermute | solution.py:619
